TPU v7x, 128 devices: a whole 4x4x4 slice. The times are simulated.
128 devices in a mesh: feat: 4 (over z), trainer: 32 (over x, y, core).
Axes of the slice: x: 4, y: 4, z: 4, core: 2. Of those that a mesh axis runs over, the one named last changes fastest.
Arguments:
- features: bfloat16 [128, 131072], P('feat', 'trainer'), may hold values from -6 to 6
- first_adjacent: int32 [65536, 15], P('trainer'), may hold values from 0 to 4095
- first_center: int32 [65536], P('trainer'), may hold values from 0 to 4095
- first_count: int32 [65536], P('trainer'), may hold values from 1 to 15
- owner_map: int32 [65536], P('trainer'), may hold values from 0 to 127, as said below
- first_root: bfloat16 [128, 1024], P('feat'), may hold values from -0.5 to 0.5
- first_near: bfloat16 [128, 1024], P('feat'), may hold values from -0.5 to 0.5
- first_bias: float32 [1024], replicated, may hold values from -3 to 3
- second_adjacent: int32 [65536, 10], P(('feat', 'trainer')), may hold values from 0 to 1023, as said below
- second_center: int32 [65536], P(('feat', 'trainer')), may hold values from 0 to 1023, as said below
- second_count: int32 [65536], P(('feat', 'trainer')), may hold values from 1 to 10
- second_root: bfloat16 [1024, 1024], replicated, may hold values from -0.1875 to 0.1875
- second_near: bfloat16 [1024, 1024], replicated, may hold values from -0.1875 to 0.1875
- second_bias: float32 [1024], replicated, may hold values from -3 to 3
- upstream: bfloat16 [65536, 1024], P(('feat', 'trainer')), may hold values from -0.0234375 to 0.0234375
Outputs:
- layer_output: bfloat16 [65536, 1024], P(('feat', 'trainer'))
- rootgrad_two: float32 [1024, 1024], replicated
- neargrad_two: float32 [1024, 1024], replicated
- biasgrad_two: float32 [1024], replicated
- rootgrad_one: float32 [128, 1024], P('feat')
- neargrad_one: float32 [128, 1024], P('feat')
- biasgrad_one: float32 [1024], replicated
Inputs may be any that keep to these rules, and one draw needn't show every extreme that they name: `owner_map`: among the 2048 layer-one nodes of one trainer block at most 32 name any one owner; in every draw some owner is named by exactly 32 nodes of every block, and every owner is named by some node. `second_adjacent`: every entry names a filled row of the owner's table: row s * 32 + c with c smaller than the number of nodes of block s that name this owner. `second_center`: every entry names a filled row of the owner's table, as for second_adjacent.
All inputs are finite; a program needn't handle non-finite values.
Results may differ from a plain program's by a relative error of at most 0.025.
Values may be sent and summed in bfloat16 or wider, within the bound.
No kernel may reach another device: no remote copies, remote signals or barrier semaphores. Data moves between devices by JAX's collectives and lax.ppermute only.
A program may use at most 128 MiB of HBM per device.

v0:
```python
import jax
import jax.numpy as jnp
from jax import lax
from jax.sharding import PartitionSpec as P

CAP = 32


def in_one_piece(arrays, axis, dim, along):
    widths = [a.shape[along] for a in arrays]
    both = jnp.concatenate(arrays, axis=along)
    out = lax.all_gather(both, axis, axis=dim, tiled=True)
    return tuple(jnp.split(out, [sum(widths[:k]) for k in range(1, len(widths))], axis=along))


def in_one(arrays, axis):
    vector, at, finished = (jnp.concatenate([a.reshape(-1) for a in arrays]), 0, [])
    subtotal = lax.psum(vector, axis)
    for a in arrays:
        finished.append(subtotal[at : at + a.size].reshape(a.shape))
        at += a.size
    return tuple(finished)


def cross_rows(left, right):
    return lax.dot_general(
        left, right, (((0,), (0,)), ((), ())), preferred_element_type=jnp.float32
    )


def cross_cols(left, right):
    return lax.dot_general(
        left, right, (((1,), (1,)), ((), ())), preferred_element_type=jnp.float32
    )


def local(
    features,
    first_adjacent,
    first_center,
    first_count,
    owner_map,
    first_root,
    first_near,
    first_bias,
    second_adjacent,
    second_center,
    second_count,
    second_root,
    second_near,
    second_bias,
    upstream,
):
    feat_size = lax.axis_size("feat")
    trainers = lax.axis_size("trainer")
    owners_all = feat_size * trainers
    node_count = owner_map.shape[0]
    hidden_width = first_root.shape[1]
    block_width = features.shape[0]
    input_count = features.shape[1]
    fanout = first_adjacent.shape[1]
    slot_total = owners_all * CAP
    slots = trainers * CAP
    onehot = (owner_map[:, None] == jnp.arange(owners_all, dtype=jnp.int32)[None, :]).astype(
        jnp.int32
    )
    slot_rank = jnp.sum((jnp.cumsum(onehot, axis=0) - onehot) * onehot, axis=1)
    slot_node = (
        jnp.full((slot_total,), node_count, jnp.int32)
        .at[owner_map * CAP + slot_rank]
        .set(jnp.arange(node_count, dtype=jnp.int32))
    )
    filled = slot_node < node_count
    slot_adjacent = jnp.take(first_adjacent, slot_node, axis=0, mode="clip")
    slot_own = jnp.take(first_center, slot_node, axis=0, mode="clip")
    slot_count = jnp.where(filled, jnp.take(first_count, slot_node, axis=0, mode="clip"), 1)
    block_size = 512
    block_total = slot_total // block_size
    input_ids = jnp.arange(input_count, dtype=jnp.int32)[:, None]

    def select_block(pieces):
        adjacent_block, own_block, count_block, filled_block = pieces
        multiples = jnp.zeros((input_count, block_size), jnp.float32)
        for column in range(fanout):
            hits = (input_ids == adjacent_block[None, :, column]) & (
                (column < count_block) & filled_block
            )[None, :]
            multiples = multiples + jnp.where(hits, jnp.float32(1.0), jnp.float32(0.0))
        own_pick = ((input_ids == own_block[None, :]) & filled_block[None, :]).astype(jnp.bfloat16)
        own_cols = jnp.dot(features, own_pick, preferred_element_type=jnp.float32).astype(
            jnp.bfloat16
        )
        near_sum = jnp.dot(
            features, multiples.astype(jnp.bfloat16), preferred_element_type=jnp.float32
        )
        near_cols = (near_sum / count_block.astype(jnp.float32)[None, :]).astype(jnp.bfloat16)
        return (own_cols, near_cols)

    blocks_in = (
        slot_adjacent.reshape(block_total, block_size, fanout),
        slot_own.reshape(block_total, block_size),
        slot_count.reshape(block_total, block_size),
        filled.reshape(block_total, block_size),
    )
    own_blocks, near_blocks = lax.map(select_block, blocks_in)
    slot_center = own_blocks.transpose(1, 0, 2).reshape(block_width, slot_total)
    slot_near = near_blocks.transpose(1, 0, 2).reshape(block_width, slot_total)
    packed = jnp.stack([slot_center, slot_near]).reshape(2, block_width, owners_all, CAP)
    arrived = lax.all_to_all(packed, ("feat", "trainer"), split_axis=2, concat_axis=2, tiled=True)
    arrived = (
        arrived.reshape(2, block_width, feat_size, trainers, CAP)
        .transpose(0, 2, 1, 3, 4)
        .reshape(2, feat_size * block_width, slots)
    )
    owner_center = arrived[0]
    owner_near = arrived[1]
    root_all, near_all = in_one_piece((first_root, first_near), "feat", 0, 1)
    pre_one = jnp.zeros((slots, hidden_width), jnp.float32) + first_bias
    for quarter in range(feat_size):
        low = quarter * block_width
        high = low + block_width
        part = cross_rows(owner_center[low:high], root_all[low:high]) + cross_rows(
            owner_near[low:high], near_all[low:high]
        )
        pre_one = pre_one + part.astype(jnp.bfloat16).astype(jnp.float32)
    hidden_table = jax.nn.softplus(pre_one).astype(jnp.bfloat16)
    slot_ids = jnp.arange(slots, dtype=jnp.int32)
    root_pick = (second_center[:, None] == slot_ids[None, :]).astype(jnp.bfloat16)
    root_rows = jnp.dot(root_pick, hidden_table, preferred_element_type=jnp.float32).astype(
        jnp.bfloat16
    )
    multiples = jnp.zeros((second_center.shape[0], slots), jnp.float32)
    for column in range(second_adjacent.shape[1]):
        hits = (column < second_count)[:, None] & (
            second_adjacent[:, column : column + 1] == slot_ids[None, :]
        )
        multiples = multiples + jnp.where(hits, jnp.float32(1.0), jnp.float32(0.0))
    multiples = multiples.astype(jnp.bfloat16)
    divisor = second_count.astype(jnp.float32)[:, None]
    near_two = (
        jnp.dot(multiples, hidden_table, preferred_element_type=jnp.float32) / divisor
    ).astype(jnp.bfloat16)
    pre_two = jnp.dot(root_rows, second_root, preferred_element_type=jnp.float32)
    pre_two = (
        pre_two + jnp.dot(near_two, second_near, preferred_element_type=jnp.float32) + second_bias
    )
    gate = jax.nn.sigmoid(pre_two)
    layer_output = (pre_two * gate).astype(jnp.bfloat16)
    slope_two = (upstream.astype(jnp.float32) * gate * (1.0 + pre_two * (1.0 - gate))).astype(
        jnp.bfloat16
    )
    rootgrad_two, neargrad_two, biasgrad_two = lax.psum(
        (
            cross_rows(root_rows, slope_two),
            cross_rows(near_two, slope_two),
            jnp.sum(slope_two.astype(jnp.float32), axis=0),
        ),
        ("feat", "trainer"),
    )
    back_root = cross_cols(slope_two, second_root).astype(jnp.bfloat16)
    back_near = (cross_cols(slope_two, second_near) / divisor).astype(jnp.bfloat16)
    table_grad = cross_rows(root_pick, back_root) + cross_rows(multiples, back_near)
    pre_grad = (table_grad * (1.0 - jnp.exp(-hidden_table.astype(jnp.float32)))).astype(
        jnp.bfloat16
    )
    root_full = jnp.dot(owner_center, pre_grad, preferred_element_type=jnp.float32)
    near_full = jnp.dot(owner_near, pre_grad, preferred_element_type=jnp.float32)
    bias_full = jnp.sum(pre_grad.astype(jnp.float32), axis=0)
    root_sum, near_sum, biasgrad_one = in_one(
        (root_full, near_full, bias_full), ("feat", "trainer")
    )
    offset = lax.axis_index("feat") * block_width
    rootgrad_one = lax.dynamic_slice_in_dim(root_sum, offset, block_width, 0)
    neargrad_one = lax.dynamic_slice_in_dim(near_sum, offset, block_width, 0)
    return (
        layer_output,
        rootgrad_two,
        neargrad_two,
        biasgrad_two,
        rootgrad_one,
        neargrad_one,
        biasgrad_one,
    )


def solution(mesh):
    return jax.shard_map(
        local,
        mesh=mesh,
        in_specs=(
            P("feat", "trainer"),
            P("trainer", None),
            P("trainer"),
            P("trainer"),
            P("trainer"),
            P("feat", None),
            P("feat", None),
            P(),
            P(("feat", "trainer"), None),
            P(("feat", "trainer")),
            P(("feat", "trainer")),
            P(),
            P(),
            P(),
            P(("feat", "trainer"), None),
        ),
        out_specs=(
            P(("feat", "trainer"), None),
            P(),
            P(),
            P(),
            P("feat", None),
            P("feat", None),
            P(),
        ),
        check_vma=False,
    )
```

profile of v0, /device:TPU:1, one launch (start us, length us, event | category | flops | bytes accessed | tf_op | source)
XLA Modules:
  0.0 660.4 jit_solution(13970809639460819845)
XLA Ops:
  9.9 8.1 %scatter_custom_fusion = s32[4096]{0:T(1024)S(1)} fusion(s32[2048]{0:T(1024)S(1)} %compare_select_fusion.1, s32[2048]{0:T(1024)S(1)} %iota.50, s32[]{:T(128)} %constant.15.clone.1), kind=kCustom, calls=%fused_computation.160 | custom fusion | bytes 16388 | tf_op jit(solution)/shard_map/scatter | solution.py:71
  18.0 23.0 %gather_fusion.2 = s32[4096]{0:T(1024)S(1)} fusion(s32[2048]{0:T(1024)S(1)} %copy-done.1, s32[4096]{0:T(1024)S(1)} %broadcast_clamp_fusion), kind=kCustom, calls=%fused_computation.2 | custom fusion | bytes 49152 | tf_op jit(solution)/shard_map/jit(_take)/gather | solution.py:76
  41.5 14.2 %gather_fusion.1 = s32[4096,15]{1,0:T(8,128)} fusion(s32[2048,15]{1,0:T(8,128)S(1)} %copy.43, s32[4096]{0:T(1024)S(1)} %broadcast_clamp_fusion), kind=kCustom, calls=%fused_computation.1 | custom fusion | bytes 507904 | tf_op jit(solution)/shard_map/jit(_take)/gather | solution.py:74
  55.7 2.2 copy.44
  57.9 23.0 %gather_fusion = s32[4096]{0:T(1024)S(1)} fusion(s32[2048]{0:T(1024)S(1)} %copy-done.2, s32[4096]{0:T(1024)S(1)} %broadcast_clamp_fusion), kind=kCustom, calls=%fused_computation | custom fusion | bytes 49152 | tf_op jit(solution)/shard_map/jit(_take)/gather | solution.py:75
  81.0 254.4 %while.14 = (s32[]{:T(128)}, bf16[8,32,512]{2,1,0:T(8,128)(2,1)}, bf16[8,32,512]{2,1,0:T(8,128)(2,1)}, s32[8,512]{1,0:T(8,128)S(1)}, pred[8,512]{1,0:T(8,128)(4,...) while((s32[]{:T(128)}, bf16[8,32,512]{2,1,0:T(8,128)(2,1)}, ...), condition=%wide.region_5.6_spmd.clone.clone, body=%wide.region_4.5_spmd.clone.clone.sunk | while | flops 398523904 | bytes 777833 | solution.py:105
  81.5 27.7 %fusion.138 = bf16[8,32,512]{2,1,0:T(8,128)(2,1)} fusion(bf16[8,32,512]{2,1,0:T(8,128)(2,1)} %get-tuple-element.410, s32[]{:T(128)} %get-tuple-element.408, bf16[32,4096]{1,0:T(8,128)(2,1)S(1)} %get-tuple-element.422, s32[512]{0:T(512)S(1)} %bitcast.172, s32[512]{0:T(512)S(1)} %bitcast.173, s32[512]{0:T(512)S(1)} %bitcast.174, ...), kind=kOutput, calls=%fused_computation.63.clone.1 | convolution fusion | flops 260079616 | bytes 335872 | tf_op jit(solution)/shard_map/while/body/eval_jaxpr/dot_general | solution.py:93
  109.2 2.3 fusion.136
  111.7 27.7 %fusion.138 = bf16[8,32,512]{2,1,0:T(8,128)(2,1)} fusion(bf16[8,32,512]{2,1,0:T(8,128)(2,1)} %get-tuple-element.410, s32[]{:T(128)} %get-tuple-element.408, bf16[32,4096]{1,0:T(8,128)(2,1)S(1)} %get-tuple-element.422, s32[512]{0:T(512)S(1)} %bitcast.172, s32[512]{0:T(512)S(1)} %bitcast.173, s32[512]{0:T(512)S(1)} %bitcast.174, ...), kind=kOutput, calls=%fused_computation.63.clone.1 | convolution fusion | flops 260079616 | bytes 335872 | tf_op jit(solution)/shard_map/while/body/eval_jaxpr/dot_general | solution.py:93
  139.4 2.3 fusion.136
  141.9 27.7 %fusion.138 = bf16[8,32,512]{2,1,0:T(8,128)(2,1)} fusion(bf16[8,32,512]{2,1,0:T(8,128)(2,1)} %get-tuple-element.410, s32[]{:T(128)} %get-tuple-element.408, bf16[32,4096]{1,0:T(8,128)(2,1)S(1)} %get-tuple-element.422, s32[512]{0:T(512)S(1)} %bitcast.172, s32[512]{0:T(512)S(1)} %bitcast.173, s32[512]{0:T(512)S(1)} %bitcast.174, ...), kind=kOutput, calls=%fused_computation.63.clone.1 | convolution fusion | flops 260079616 | bytes 335872 | tf_op jit(solution)/shard_map/while/body/eval_jaxpr/dot_general | solution.py:93
  169.6 2.3 fusion.136
  172.1 27.7 %fusion.138 = bf16[8,32,512]{2,1,0:T(8,128)(2,1)} fusion(bf16[8,32,512]{2,1,0:T(8,128)(2,1)} %get-tuple-element.410, s32[]{:T(128)} %get-tuple-element.408, bf16[32,4096]{1,0:T(8,128)(2,1)S(1)} %get-tuple-element.422, s32[512]{0:T(512)S(1)} %bitcast.172, s32[512]{0:T(512)S(1)} %bitcast.173, s32[512]{0:T(512)S(1)} %bitcast.174, ...), kind=kOutput, calls=%fused_computation.63.clone.1 | convolution fusion | flops 260079616 | bytes 335872 | tf_op jit(solution)/shard_map/while/body/eval_jaxpr/dot_general | solution.py:93
  199.8 2.3 fusion.136
  202.3 27.7 %fusion.138 = bf16[8,32,512]{2,1,0:T(8,128)(2,1)} fusion(bf16[8,32,512]{2,1,0:T(8,128)(2,1)} %get-tuple-element.410, s32[]{:T(128)} %get-tuple-element.408, bf16[32,4096]{1,0:T(8,128)(2,1)S(1)} %get-tuple-element.422, s32[512]{0:T(512)S(1)} %bitcast.172, s32[512]{0:T(512)S(1)} %bitcast.173, s32[512]{0:T(512)S(1)} %bitcast.174, ...), kind=kOutput, calls=%fused_computation.63.clone.1 | convolution fusion | flops 260079616 | bytes 335872 | tf_op jit(solution)/shard_map/while/body/eval_jaxpr/dot_general | solution.py:93
  230.0 2.3 fusion.136
  232.4 27.7 %fusion.138 = bf16[8,32,512]{2,1,0:T(8,128)(2,1)} fusion(bf16[8,32,512]{2,1,0:T(8,128)(2,1)} %get-tuple-element.410, s32[]{:T(128)} %get-tuple-element.408, bf16[32,4096]{1,0:T(8,128)(2,1)S(1)} %get-tuple-element.422, s32[512]{0:T(512)S(1)} %bitcast.172, s32[512]{0:T(512)S(1)} %bitcast.173, s32[512]{0:T(512)S(1)} %bitcast.174, ...), kind=kOutput, calls=%fused_computation.63.clone.1 | convolution fusion | flops 260079616 | bytes 335872 | tf_op jit(solution)/shard_map/while/body/eval_jaxpr/dot_general | solution.py:93
  260.1 2.3 fusion.136
  262.6 27.7 %fusion.138 = bf16[8,32,512]{2,1,0:T(8,128)(2,1)} fusion(bf16[8,32,512]{2,1,0:T(8,128)(2,1)} %get-tuple-element.410, s32[]{:T(128)} %get-tuple-element.408, bf16[32,4096]{1,0:T(8,128)(2,1)S(1)} %get-tuple-element.422, s32[512]{0:T(512)S(1)} %bitcast.172, s32[512]{0:T(512)S(1)} %bitcast.173, s32[512]{0:T(512)S(1)} %bitcast.174, ...), kind=kOutput, calls=%fused_computation.63.clone.1 | convolution fusion | flops 260079616 | bytes 335872 | tf_op jit(solution)/shard_map/while/body/eval_jaxpr/dot_general | solution.py:93
  290.3 2.3 fusion.136
  292.8 27.7 %fusion.138 = bf16[8,32,512]{2,1,0:T(8,128)(2,1)} fusion(bf16[8,32,512]{2,1,0:T(8,128)(2,1)} %get-tuple-element.410, s32[]{:T(128)} %get-tuple-element.408, bf16[32,4096]{1,0:T(8,128)(2,1)S(1)} %get-tuple-element.422, s32[512]{0:T(512)S(1)} %bitcast.172, s32[512]{0:T(512)S(1)} %bitcast.173, s32[512]{0:T(512)S(1)} %bitcast.174, ...), kind=kOutput, calls=%fused_computation.63.clone.1 | convolution fusion | flops 260079616 | bytes 335872 | tf_op jit(solution)/shard_map/while/body/eval_jaxpr/dot_general | solution.py:93
  320.5 2.3 fusion.136
  338.2 1.6 stack.8
  339.8 1.7 pad_maximum_fusion
  341.5 2.7 copy.54
  344.1 4.5 reshape.178
  348.6 11.5 %all-to-all-start = ((bf16[128,2,1024]{2,1,0:T(2,128)(2,1)}), bf16[128,2,1024]{2,1,0:T(2,128)(2,1)S(1)}, u32[]{:S(2)}, u32[]{:S(2)}) async-start(bf16[128,2,1024]{2,1,0:T(2,128)(2,1)} %reshape.178), calls=%async_computation | async-start | bytes 1048576 | tf_op jit(solution)/shard_map/all_to_all | solution.py:109
  360.2 15.7 %all_gather.3 = bf16[128,2048]{1,0:T(8,128)(2,1)} all-gather(bf16[32,2048]{1,0:T(8,128)(2,1)S(1)} %pad_maximum_fusion.2), channel_id=1, replica_groups=mesh['feat'=4,'trainer'=32] {'feat'}, dimensions={0}, use_global_device_ids=true | all-gather | bytes 655360 | tf_op jit(solution)/shard_map/all_gather | solution.py:12
  377.7 2.0 reshape.179
  379.7 2.9 copy.53
  382.7 1.3 fusion.91
  384.0 1.5 fusion.90
  385.5 1.2 slice.215
  386.7 1.2 slice.218
  388.0 1.9 slice.221
  389.8 3.5 fusion.81
  393.4 3.6 fusion.78
  398.2 1.9 slice.227
  400.0 3.6 fusion.75
  403.7 1.9 slice.230
  405.5 1.9 slice.209
  407.4 3.6 fusion.84
  411.9 3.1 add_convert_fusion.12
  415.3 1.7 add_convert_fusion.11
  417.6 1.7 add_convert_fusion.10
  419.8 4.4 fusion.53
  424.2 1.7 fusion.66
  426.7 1.3 fusion.94
  428.2 7.0 %divide_convert_fusion.1 = bf16[512,1024]{1,0:T(8,128)(2,1)S(1)} fusion(bf16[1024,1024]{1,0:T(8,128)(2,1)S(1)} %fusion.53, f32[512]{0:T(512)S(1)} %copy-done.27, s32[512]{0:T(512)S(1)} %bitcast.204, s32[512]{0:T(512)S(1)} %bitcast.206, s32[512]{0:T(512)S(1)} %bitcast.190, s32[512]{0:T(512)S(1)} %bitcast.192, s32[512]{0:T(512)S(1)} %bitcast.194, ...), kind=kOutput, calls=%fused_computation.101 | convolution fusion | flops 1095761920 | bytes 3173376 | tf_op jit(solution)/shard_map/dot_general | solution.py:141
  435.3 3.5 convert_reduce_fusion.1
  438.7 6.2 fusion.54
  444.9 5.0 fusion.96
  449.9 3.3 fusion.95
  453.3 11.6 %convert_reduce_fusion = (f32[1024]{0:T(1024)S(1)}, bf16[1024,1024]{1,0:T(8,128)(2,1)}) fusion(bf16[1024,1024]{1,0:T(8,128)(2,1)} %copy-done.44, f32[1024,1024]{1,0:T(8,128)} %fusion.54, bf16[512,1024]{1,0:T(8,128)(2,1)} %get-tuple-element.226, bf16[1024,1024]{1,0:T(8,128)(2,1)S(1)} %copy-done, f32[512]{0:T(512)S(1)} %copy-done.27, s32[512]{0:T(512)S(1)} %bitcast.205, ...), kind=kOutput, calls=%fused_computation.87 | convolution fusion | flops 2177891328 | bytes 11566080 | tf_op jit(solution)/shard_map/dot_general | solution.py:26
  464.8 2.3 squeeze.13
  467.2 2.0 convolution_bitcast_fusion.1
  471.2 2.1 convolution_bitcast_fusion
  474.5 67.6 %psum.30 = f32[1024]{0:T(1024)} all-reduce(f32[1024]{0:T(1024)S(1)} %get-tuple-element.225), channel_id=1, replica_groups=mesh['feat'=4,'trainer'=32] {'feat','trainer'}, use_global_device_ids=true, to_apply=%region_9.10 | all-reduce | flops 1024 | bytes 8192 | tf_op jit(solution)/shard_map/psum | solution.py:152
  542.1 99.2 %all-reduce.3.cloned.1.call-done = (f32[1024,1024]{1,0:T(8,128)}, f32[1024,1024]{1,0:T(8,128)}, f32[263168]{0:T(1024)}) async-done(((f32[1024,1024]{1,0:T(8,128)}, f32[1024,1024]{1,0:T(8,128)}, f32[263168]{0:T(1024)}), (f32[1024,1024]{1,0:T(8,128)}, f32[1024,1024]{1,0:T(8,128)}, f32[263168]{0:T(1024)})) %all-reduce.3.cloned.1.call-update) | async-done | bytes 9441296 | tf_op jit(solution)/shard_map/psum | solution.py:152
  641.3 1.3 fusion.92
  642.6 1.3 slice.322
  644.8 1.6 constant_dynamic-slice_fusion.3
  646.5 4.9 copy.69
  651.4 2.0 copy.70
  (158 shorter events, 17.3 us)
Async XLA Ops:
  7.2 428.1 %copy-start = (bf16[1024,1024]{1,0:T(8,128)(2,1)S(1)}, bf16[1024,1024]{1,0:T(8,128)(2,1)}, u32[]{:S(2)}) copy-start(bf16[1024,1024]{1,0:T(8,128)(2,1)} %param.29) | copy-start | bytes 6291460
  8.5 0.7 copy-start.15
  8.6 9.3 %copy-start.1 = (s32[2048]{0:T(1024)S(1)}, s32[2048]{0:T(1024)}, u32[]{:S(2)}) copy-start(s32[2048]{0:T(1024)} %param.20) | copy-start | bytes 24580
  18.0 23.1 %copy-start.14 = (s32[2048,15]{0,1:T(8,128)S(1)}, s32[2048,15]{0,1:T(8,128)}, u32[]{:S(2)}) copy-start(s32[2048,15]{0,1:T(8,128)} %param.18) | copy-start | bytes 368644
  55.7 2.2 copy-start.2
  57.9 23.1 %copy-start.40 = (bf16[32,4096]{1,0:T(8,128)(2,1)S(1)}, bf16[32,4096]{1,0:T(8,128)(2,1)}, u32[]{:S(2)}) copy-start(bf16[32,4096]{1,0:T(8,128)(2,1)} %param.17) | copy-start | bytes 786436
  344.1 16.0 %copy-start.17 = (bf16[32,1024]{1,0:T(8,128)(2,1)S(1)}, bf16[32,1024]{1,0:T(8,128)(2,1)}, u32[]{:S(2)}) copy-start(bf16[32,1024]{1,0:T(8,128)(2,1)} %param.23) | copy-start | bytes 196612
  344.1 16.0 %copy-start.18 = (bf16[32,1024]{1,0:T(8,128)(2,1)S(1)}, bf16[32,1024]{1,0:T(8,128)(2,1)}, u32[]{:S(2)}) copy-start(bf16[32,1024]{1,0:T(8,128)(2,1)} %param.22) | copy-start | bytes 196612
  344.1 31.8 %copy-start.20 = (s32[512]{0:T(512)S(1)}, s32[512]{0:T(512)}, u32[]{:S(2)}) copy-start(s32[512]{0:T(512)} %param.27) | copy-start | bytes 6148
  344.1 33.0 %copy-start.19 = (s32[512,10]{0,1:T(8,128)S(1)}, s32[512,10]{0,1:T(8,128)}, u32[]{:S(2)}) copy-start(s32[512,10]{0,1:T(8,128)} %param.25) | copy-start | bytes 61444
  348.6 29.1 %all-to-all-start = ((bf16[128,2,1024]{2,1,0:T(2,128)(2,1)}), bf16[128,2,1024]{2,1,0:T(2,128)(2,1)S(1)}, u32[]{:S(2)}, u32[]{:S(2)}) async-start(bf16[128,2,1024]{2,1,0:T(2,128)(2,1)} %reshape.178), calls=%async_computation | async-start | bytes 1048576 | tf_op jit(solution)/shard_map/all_to_all | solution.py:109
  360.1 281.2 %all-reduce.3.cloned.1.call-start = ((), (), s32[]{:S(2)}) async-start(), calls=%async_computation.1 | async-start | bytes 18882560 | tf_op jit(solution)/shard_map/psum | solution.py:152
  389.8 3.5 copy-start.13
  411.9 3.5 copy-start.3
  415.3 2.2 copy-start.4
  415.3 2.2 copy-start.12
  417.6 2.2 copy-start.6
  417.6 2.2 copy-start.16
  417.6 2.2 copy-start.41
  419.8 4.4 copy-start.43
  424.2 3.8 copy-start.44
  424.2 2.4 copy-start.38
  426.6 1.4 copy-start.9
  426.6 1.4 copy-start.21
  426.6 1.4 copy-start.22
  426.6 1.5 copy-start.23
  426.6 1.5 copy-start.24
  426.6 1.5 copy-start.25
  426.6 1.5 copy-start.26
  426.6 1.5 copy-start.27
  426.6 1.5 copy-start.28
  426.6 1.5 copy-start.29
  426.6 1.5 copy-start.30
  426.6 1.5 copy-start.31
  426.7 1.5 copy-start.32
  426.7 1.5 copy-start.33
  426.7 1.5 copy-start.34
  426.7 1.5 copy-start.35
  426.7 1.5 copy-start.36
  426.7 1.5 copy-start.37
  428.2 7.1 %copy-start.39 = (bf16[512,1024]{1,0:T(8,128)(2,1)S(1)}, bf16[512,1024]{1,0:T(8,128)(2,1)}, u32[]{:S(2)}) copy-start(bf16[512,1024]{1,0:T(8,128)(2,1)} %param.31) | copy-start | bytes 3145732
  428.2 7.1 %copy-start.42 = (f32[1024]{0:T(1024)S(1)}, f32[1024]{0:T(1024)}, u32[]{:S(2)}) copy-start(f32[1024]{0:T(1024)} %param.30) | copy-start | bytes 12292
  435.2 3.5 copy-start.11
  444.9 5.0 copy-start.7
  444.9 5.0 copy-start.10
  471.2 2.2 copy-start.8
  646.5 4.9 copy-start.5
Sparse Core Ops, SparseCore 0:
  474.6 166.6 all-reduce.2
where the time goes:
time: 665 us; the launch traced here: 660 us
  matrix products  309 us (46%)
  local copies, waits for them, and re-layouts  123 us (18%)
  waiting for transfers between devices  99.2 us (15%)
  blocking collectives  83.4 us (13%)
  between operations  15 us (2%)
  loops' own time  13.2 us (2%)
  starting transfers between devices  11.5 us (2%)
    dot_general x8, matrix products, select_block(): jnp.dot(features, multiples.astype(jnp.bfloat16), preferred_element_type=...  222 us
    psum x1, waiting for transfers between devices, local(): lax.psum((cross_rows(root_rows, slope_two), cross_rows(near_two, slope_tw...  99.2 us
    psum x1, blocking collectives, local(): lax.psum((cross_rows(root_rows, slope_two), cross_rows(near_two, slope_tw...  67.6 us
    dot_general x12, matrix products, cross_rows(): lax.dot_general(left, right, (((0,), (0,)), ((), ())), preferred_element_...  51.3 us
    gather x1, local copies, waits for them, and re-layouts, local(): slot_own = jnp.take(first_center, slot_node, axis=0, mode='clip')  23 us
    gather x1, local copies, waits for them, and re-layouts, local(): jnp.take(first_count, slot_node, axis=0, mode='clip')  23 us
    unnamed x98, local copies, waits for them, and re-layouts  19.4 us
    dot_general x8, matrix products, select_block(): jnp.dot(features, own_pick, preferred_element_type=jnp.float32)  18.4 us
  transfers between devices with their start and end apart: 2, of which 1 were waited for; matrix products, arithmetic and copies ran while one was open for 0% of the time, Pallas kernels for 0%

commit v1 on v0

v1 whole, which is shorter than its diff:
```python
import jax
import jax.numpy as jnp
from jax import lax
from jax.experimental import pallas as pl
from jax.experimental.pallas import tpu as pltpu
from jax.sharding import Mesh, PartitionSpec as P

CAP = 32
LANES = 128
AXES = ("z", "x", "y", "core")
CHIPS = ("z", "x", "y")
CHUNK = 152
VMEM = pl.BlockSpec(memory_space=pltpu.VMEM)
SMEM = pl.BlockSpec(memory_space=pltpu.SMEM)


def lanes_at(at, size=LANES):
    return pl.ds(pl.multiple_of(at * size, size), size)


def across(left, right):
    return lax.dot_general(
        left, right, (((0,), (0,)), ((), ())), preferred_element_type=jnp.float32
    )


def along(left, right):
    return lax.dot_general(
        left, right, (((1,), (1,)), ((), ())), preferred_element_type=jnp.float32
    )


def matmul(left, right):
    return jnp.dot(left, right, preferred_element_type=jnp.float32)


def aggregate_kernel(feat_ref, adj_ref, count_ref, owner_ref, out_ref, table, rows, places, stage):
    width, inputs = feat_ref.shape
    nodes = owner_ref.shape[1]
    owners = out_ref.shape[0]
    fan = adj_ref.shape[0] - 1
    chunks = inputs // LANES
    groups = nodes // LANES
    parts = width // 8
    for c in range(chunks):
        table[c] = feat_ref[:, c * LANES : (c + 1) * LANES].astype(jnp.float32)

    def one_group(g, carry):
        count = count_ref[:, lanes_at(g)]
        total = [jnp.zeros((8, LANES), jnp.float32) for _ in range(parts)]
        for k in range(fan + 1):
            index = jnp.broadcast_to(adj_ref[k : k + 1, lanes_at(g)], (8, LANES))
            high = lax.shift_right_logical(index, 7)
            low = lax.bitwise_and(index, LANES - 1)
            found = [jnp.zeros((8, LANES), jnp.float32) for _ in range(parts)]
            for c in range(chunks):
                here = high == c
                for v in range(parts):
                    got = jnp.take_along_axis(
                        table[c, v * 8 : (v + 1) * 8, :], low, axis=1, mode="promise_in_bounds"
                    )
                    found[v] = jnp.where(here, got, found[v])
            if k < fan:
                valid = jnp.broadcast_to(k < count, (8, LANES))
                total = [a + jnp.where(valid, b, 0.0) for a, b in zip(total, found)]
            else:
                for v in range(parts):
                    rows[v * 8 : (v + 1) * 8, lanes_at(g)] = found[v]
        divisor = jnp.broadcast_to(count.astype(jnp.float32), (8, LANES))
        for v in range(parts):
            rows[width + v * 8 : width + (v + 1) * 8, lanes_at(g)] = total[v] / divisor
        return carry

    lax.fori_loop(0, groups, one_group, 0)

    span = 256
    before = (
        lax.broadcasted_iota(jnp.int32, (span, span), 0)
        < lax.broadcasted_iota(jnp.int32, (span, span), 1)
    ).astype(jnp.bfloat16)
    owner_ids = lax.broadcasted_iota(jnp.int32, (owners, span), 0)
    ranks = lax.broadcasted_iota(jnp.int32, (CAP, span), 0)
    seen = jnp.zeros((owners, 1), jnp.float32)
    found_at = jnp.zeros((3 * CAP, owners), jnp.float32)
    for b in range(nodes // span):
        hit = owner_ids == owner_ref[:, b * span : (b + 1) * span]
        picked = hit.astype(jnp.bfloat16)
        earlier = matmul(picked, before) + seen
        rank = jnp.sum(jnp.where(hit, earlier, 0.0), axis=0, keepdims=True).astype(jnp.int32)
        seen = seen + jnp.sum(jnp.where(hit, 1.0, 0.0), axis=1, keepdims=True)
        node = lax.broadcasted_iota(jnp.int32, (CAP, span), 1) + b * span
        mine = ranks == rank
        weights = jnp.concatenate(
            [
                jnp.where(mine, lax.shift_right_logical(node, 7), 0).astype(jnp.float32),
                jnp.where(mine, lax.bitwise_and(node, LANES - 1), 0).astype(jnp.float32),
                jnp.where(mine, 1.0, 0.0),
            ],
            axis=0,
        ).astype(jnp.bfloat16)
        found_at = found_at + along(weights, picked)
    places[...] = found_at.astype(jnp.int32)

    half = 2 * width
    for pair in range(CAP // 2):
        for j in range(2):
            r = pair * 2 + j
            high = jnp.broadcast_to(places[r : r + 1, :], (8, owners))
            low = jnp.broadcast_to(places[CAP + r : CAP + r + 1, :], (8, owners))
            filled = jnp.broadcast_to(places[2 * CAP + r : 2 * CAP + r + 1, :], (8, owners)) > 0
            for v in range(half // 8):
                found = jnp.zeros((8, owners), jnp.float32)
                for g in range(groups):
                    got = jnp.take_along_axis(
                        rows[v * 8 : (v + 1) * 8, g * LANES : (g + 1) * LANES],
                        low,
                        axis=1,
                        mode="promise_in_bounds",
                    )
                    found = jnp.where(high == g, got, found)
                stage[j * half + v * 8 : j * half + (v + 1) * 8, :] = jnp.where(filled, found, 0.0)
        out_ref[:, pair * LANES : (pair + 1) * LANES] = stage[...].T.astype(out_ref.dtype)


def aggregate(features, adjacent, count, owner, owners):
    width, inputs = features.shape
    nodes = owner.shape[1]
    return pl.pallas_call(
        aggregate_kernel,
        out_shape=jax.ShapeDtypeStruct((owners, CAP * 2 * width), jnp.bfloat16),
        in_specs=[VMEM] * 4,
        out_specs=VMEM,
        scratch_shapes=[
            pltpu.VMEM((inputs // LANES, width, LANES), jnp.float32),
            pltpu.VMEM((2 * width, nodes), jnp.float32),
            pltpu.VMEM((3 * CAP, owners), jnp.int32),
            pltpu.VMEM((4 * width, owners), jnp.float32),
        ],
        name="aggregate",
        cost_estimate=pl.CostEstimate(flops=40_000_000, bytes_accessed=3_000_000, transcendentals=0),
    )(features, adjacent, count, owner)


def picks_kernel(adj_ref, center_ref, count_ref, out_ref, flip_ref):
    nodes, fan = adj_ref.shape
    slots = out_ref.shape[1]

    def table_row(slot):
        return lax.bitwise_and(slot, CAP - 1) * (slots // CAP) + lax.shift_right_logical(slot, 5)

    def one_tile(t, carry):
        at = pl.ds(pl.multiple_of(t * 16, 16), 16)
        number = lax.broadcasted_iota(jnp.int32, (16, fan), 1)
        adjacent = jnp.where(number < count_ref[at, :], table_row(adj_ref[at, :]), -1)
        center = jnp.broadcast_to(table_row(center_ref[at, :]), (16, LANES))
        spread = [jnp.broadcast_to(adjacent[:, k : k + 1], (16, LANES)) for k in range(fan)]
        for c in range(slots // LANES):
            ids = lax.broadcasted_iota(jnp.int32, (16, LANES), 1) + c * LANES
            total = jnp.zeros((16, LANES), jnp.float32)
            for k in range(fan):
                total = total + jnp.where(spread[k] == ids, 1.0, 0.0)
            out_ref[at, c * LANES : (c + 1) * LANES] = jnp.where(center == ids, 1.0, 0.0).astype(
                out_ref.dtype
            )
            low = pl.ds(pl.multiple_of(nodes + t * 16, 16), 16)
            out_ref[low, c * LANES : (c + 1) * LANES] = total.astype(out_ref.dtype)
        return carry

    lax.fori_loop(0, nodes // 16, one_tile, 0)

    def one_flip(t, carry):
        flip_ref[:, lanes_at(t)] = out_ref[lanes_at(t), :].T
        return carry

    lax.fori_loop(0, 2 * nodes // LANES, one_flip, 0)


def picks(adjacent, center, count, slots):
    nodes = adjacent.shape[0]
    return pl.pallas_call(
        picks_kernel,
        out_shape=(
            jax.ShapeDtypeStruct((2 * nodes, slots), jnp.bfloat16),
            jax.ShapeDtypeStruct((slots, 2 * nodes), jnp.bfloat16),
        ),
        in_specs=[VMEM] * 3,
        out_specs=(VMEM, VMEM),
        name="picks",
        cost_estimate=pl.CostEstimate(flops=20_000_000, bytes_accessed=5_000_000, transcendentals=0),
    )(adjacent, center, count)


def owner_kernel(
    core_ref, arrived_ref, first_ref, bias_one_ref, picks_ref, flip_ref, count_ref, root_ref,
    near_ref, bias_two_ref, upstream_ref, out_ref, kept_ref, sent_ref, inputs, inputs_flip,
    hidden, rows, slope, back, bias_grads,
):
    core = core_ref[0]
    slots, depth = inputs.shape
    hidden_width = hidden.shape[1]
    nodes = slope.shape[0]
    quarter = depth // 4
    sources = slots // CAP
    tile = 256
    for r in range(CAP):
        pieces = [
            arrived_ref[f * sources : (f + 1) * sources, r * quarter : (r + 1) * quarter]
            for f in range(4)
        ]
        inputs[r * sources : (r + 1) * sources, :] = jnp.concatenate(pieces, axis=1)
    for t in range(slots // tile):
        inputs_flip[:, t * tile : (t + 1) * tile] = inputs[t * tile : (t + 1) * tile, :].T

    def first_layer(t, carry):
        cols = lanes_at(t, tile)
        pre = matmul(inputs[...], first_ref[:, cols]) + bias_one_ref[:, cols]
        value = jnp.maximum(pre, 0.0) + jnp.log1p(jnp.exp(-jnp.abs(pre)))
        hidden[:, cols] = value.astype(jnp.bfloat16)
        return carry

    lax.fori_loop(0, hidden_width // tile, first_layer, 0)
    inverse = 1.0 / count_ref[...].astype(jnp.float32)

    def select(t, carry):
        cols = lanes_at(t, tile)
        rows[:nodes, cols] = matmul(picks_ref[:nodes, :], hidden[:, cols]).astype(jnp.bfloat16)
        total = matmul(picks_ref[nodes:, :], hidden[:, cols])
        rows[nodes:, cols] = (total * inverse).astype(jnp.bfloat16)
        return carry

    lax.fori_loop(0, hidden_width // tile, select, 0)

    def second_layer(t, carry):
        cols = lanes_at(t, tile)
        pre = matmul(rows[:nodes, :], root_ref[:, cols]) + matmul(rows[nodes:, :], near_ref[:, cols])
        pre = pre + bias_two_ref[:, cols]
        gate = jax.nn.sigmoid(pre)
        out_ref[:, cols] = (pre * gate).astype(jnp.bfloat16)
        grad = upstream_ref[:, cols].astype(jnp.float32) * gate * (1.0 + pre * (1.0 - gate))
        grad = grad.astype(jnp.bfloat16)
        slope[:, cols] = grad
        bias_grads[0:1, cols] = jnp.sum(grad.astype(jnp.float32), axis=0, keepdims=True)
        return carry

    lax.fori_loop(0, hidden_width // tile, second_layer, 0)

    for place, to_ref in enumerate((kept_ref, sent_ref)):
        which = core ^ place

        def weight_grads(t, carry, to_ref=to_ref, which=which):
            left = rows[pl.ds(pl.multiple_of(which * nodes, nodes), nodes), lanes_at(t, tile)]
            product = across(left, slope[...]).astype(jnp.bfloat16)
            for c in range(tile // 16):
                for lane in range(hidden_width // LANES):
                    to_ref[t * (tile // 16) + c, lane * 16 : (lane + 1) * 16, :] = product[
                        c * 16 : (c + 1) * 16, lane * LANES : (lane + 1) * LANES
                    ]
            return carry

        lax.fori_loop(0, hidden_width // tile, weight_grads, 0)

    def backward(t, carry):
        cols = lanes_at(t, tile)
        back[:nodes, cols] = along(slope[...], root_ref[cols, :]).astype(jnp.bfloat16)
        near = along(slope[...], near_ref[cols, :])
        back[nodes:, cols] = (near * inverse).astype(jnp.bfloat16)
        return carry

    lax.fori_loop(0, hidden_width // tile, backward, 0)

    def first_grads(t, carry):
        cols = lanes_at(t, tile)
        table_grad = matmul(flip_ref[...], back[:, cols])
        grad = table_grad * (1.0 - jnp.exp(-hidden[:, cols].astype(jnp.float32)))
        grad = grad.astype(jnp.bfloat16)
        bias_grads[1:2, cols] = jnp.sum(grad.astype(jnp.float32), axis=0, keepdims=True)
        for place, to_ref in enumerate((kept_ref, sent_ref)):
            which = core ^ place
            left = inputs_flip[pl.ds(pl.multiple_of(which * LANES, LANES), LANES), :]
            product = matmul(left, grad).astype(jnp.bfloat16)
            for c in range(8):
                for lane in range(tile // LANES):
                    chunk = c * 8 + t * (tile // LANES) + lane
                    to_ref[chunk, LANES : LANES + 16, :] = product[
                        c * 16 : (c + 1) * 16, lane * LANES : (lane + 1) * LANES
                    ]
        return carry

    lax.fori_loop(0, hidden_width // tile, first_grads, 0)
    for place, to_ref in enumerate((kept_ref, sent_ref)):
        which = core ^ place
        to_ref[:, LANES + 16 :, :] = jnp.zeros((to_ref.shape[0], 8, LANES), jnp.bfloat16)
        for lane in range(8):
            cols = slice(lane * LANES, (lane + 1) * LANES)
            row = jnp.where(which == 0, bias_grads[0:1, cols], bias_grads[1:2, cols])
            to_ref[lane, LANES + 16 :, :] = jnp.broadcast_to(row, (8, LANES)).astype(jnp.bfloat16)


def owner_step(
    core, arrived, first, bias_one, picked, flipped, count, root, near, bias_two, upstream
):
    nodes, hidden_width = upstream.shape
    slots = picked.shape[1]
    depth = first.shape[0]
    bf16, f32 = jnp.bfloat16, jnp.float32
    share = jax.ShapeDtypeStruct((64, CHUNK, LANES), bf16)
    return pl.pallas_call(
        owner_kernel,
        out_shape=(jax.ShapeDtypeStruct((nodes, hidden_width), bf16), share, share),
        in_specs=[SMEM] + [VMEM] * 10,
        out_specs=(VMEM, VMEM, VMEM),
        scratch_shapes=[
            pltpu.VMEM((slots, depth), bf16),
            pltpu.VMEM((depth, slots), bf16),
            pltpu.VMEM((slots, hidden_width), bf16),
            pltpu.VMEM((2 * nodes, hidden_width), bf16),
            pltpu.VMEM((nodes, hidden_width), bf16),
            pltpu.VMEM((2 * nodes, hidden_width), bf16),
            pltpu.VMEM((8, hidden_width), f32),
        ],
        name="owner_step",
        cost_estimate=pl.CostEstimate(
            flops=12_000_000_000, bytes_accessed=18_000_000, transcendentals=3_000_000
        ),
    )(core, arrived, first, bias_one, picked, flipped, count, root, near, bias_two, upstream)


def spread_kernel(core_ref, z_ref, kept_ref, other_ref, root_ref, near_ref, first_root_ref, first_near_ref, bias_two_ref, bias_one_ref):
    even = core_ref[0] == 0
    z = z_ref[0]

    def one_chunk(c, carry):
        at = pl.ds(pl.multiple_of(c * 16, 16), 16)
        for lane in range(8):
            kept = kept_ref[c, lane * 16 : (lane + 1) * 16, :].astype(jnp.float32)
            other = other_ref[c, lane * 16 : (lane + 1) * 16, :].astype(jnp.float32)
            cols = slice(lane * LANES, (lane + 1) * LANES)
            root_ref[at, cols] = jnp.where(even, kept, other)
            near_ref[at, cols] = jnp.where(even, other, kept)
        return carry

    lax.fori_loop(0, 64, one_chunk, 0)
    here = lax.shift_right_logical(z, 1) == core_ref[0]
    base = lax.bitwise_and(z, 1) * 4
    for j, to_ref in enumerate((first_root_ref, first_near_ref)):
        for i in range(2):
            for lane in range(8):
                chunk = (base + 2 * j + i) * 8 + lane
                kept = kept_ref[chunk, LANES : LANES + 16, :].astype(jnp.float32)
                other = other_ref[chunk, LANES : LANES + 16, :].astype(jnp.float32)
                to_ref[i * 16 : (i + 1) * 16, lane * LANES : (lane + 1) * LANES] = jnp.where(
                    here, kept, other
                )
    for lane in range(8):
        kept = kept_ref[lane, LANES + 16 :, :].astype(jnp.float32)[0:1, :]
        other = other_ref[lane, LANES + 16 :, :].astype(jnp.float32)[0:1, :]
        cols = slice(lane * LANES, (lane + 1) * LANES)
        bias_two_ref[:, cols] = jnp.where(even, kept, other)
        bias_one_ref[:, cols] = jnp.where(even, other, kept)


def spread(core, z, kept, other, hidden_width):
    f32 = jnp.float32
    square = jax.ShapeDtypeStruct((hidden_width, hidden_width), f32)
    slab = jax.ShapeDtypeStruct((32, hidden_width), f32)
    line = jax.ShapeDtypeStruct((1, hidden_width), f32)
    return pl.pallas_call(
        spread_kernel,
        out_shape=(square, square, slab, slab, line, line),
        in_specs=[SMEM, SMEM, VMEM, VMEM],
        out_specs=(VMEM,) * 6,
        name="spread",
    )(core, z, kept, other)


def weights_of_all(own, z):
    first = lax.ppermute(own, "z", [(0, 1), (1, 0), (2, 3), (3, 2)])
    odd = lax.bitwise_and(z, 1) == 1
    pair = jnp.concatenate([jnp.where(odd, first, own), jnp.where(odd, own, first)], axis=0)
    second = lax.ppermute(pair, "z", [(0, 3), (3, 0), (1, 2), (2, 1)])
    late = z >= 2
    return jnp.concatenate([jnp.where(late, second, pair), jnp.where(late, pair, second)], axis=0)


def exchange(value, axes):
    return lax.all_to_all(value, axes, split_axis=0, concat_axis=0, tiled=True)


def local(
    features,
    first_adjacent,
    first_center,
    first_count,
    owner_map,
    first_root,
    first_near,
    first_bias,
    second_adjacent,
    second_center,
    second_count,
    second_root,
    second_near,
    second_bias,
    upstream,
):
    owners = 128
    hidden_width = first_root.shape[1]
    z = lax.axis_index("z")
    core = lax.axis_index("core")[None]
    first_all = weights_of_all(jnp.concatenate([first_root, first_near], axis=0), z)
    columns = jnp.concatenate([first_adjacent, first_center[:, None]], axis=1).T
    packed = aggregate(features, columns, first_count[None], owner_map[None], owners)
    arrived = exchange(packed, AXES)
    count = second_count[:, None]
    picked, flipped = picks(second_adjacent, second_center[:, None], count, owners * 8)
    layer_output, kept, sent = owner_step(
        core, arrived, first_all, first_bias[None], picked, flipped, count, second_root,
        second_near, second_bias[None], upstream,
    )
    received = lax.ppermute(sent, "core", [(0, 1), (1, 0)])
    both = (kept.astype(jnp.float32) + received.astype(jnp.float32)).astype(jnp.bfloat16)
    terms = exchange(both, CHIPS)
    total = jnp.sum(terms.astype(jnp.float32), axis=0).astype(jnp.bfloat16)
    mine = exchange(jnp.broadcast_to(total[None], terms.shape), CHIPS)
    other = lax.ppermute(mine, "core", [(0, 1), (1, 0)])
    root_two, near_two, root_one, near_one, bias_two, bias_one = spread(
        core, z[None], mine, other, hidden_width
    )
    return (layer_output, root_two, near_two, bias_two[0], root_one, near_one, bias_one[0])


def solution(mesh):
    chips = Mesh(mesh.devices.reshape(4, 4, 4, 2), AXES)
    trainer = ("x", "y", "core")
    return jax.shard_map(
        local,
        mesh=chips,
        in_specs=(
            P("z", trainer),
            P(trainer, None),
            P(trainer),
            P(trainer),
            P(trainer),
            P("z", None),
            P("z", None),
            P(),
            P(AXES, None),
            P(AXES),
            P(AXES),
            P(),
            P(),
            P(),
            P(AXES, None),
        ),
        out_specs=(
            P(AXES, None),
            P(),
            P(),
            P(),
            P("z", None),
            P("z", None),
            P(),
        ),
        check_vma=False,
    )
```

time: 665 us -> 216 us (0.32)
  matrix products: 309 us -> 0 us
  local copies, waits for them, and re-layouts: 123 us -> 9.32 us
  waiting for transfers between devices: 99.2 us -> 12.1 us
  Pallas kernels: 0 us -> 87.1 us
  between operations: 15 us -> 0.73 us
  loops' own time: 13.2 us -> 0 us
  starting transfers between devices: 11.5 us -> 18.3 us
    dot_general x34 -> x0, matrix products: 309 us -> none  [the longest x8 222 us: select_block(): jnp.dot(features, multiples.astype(jnp.bfloat16), preferred_element_type=...]
    psum x1 -> x0, waiting for transfers between devices: 99.2 us -> none  [local(): lax.psum((cross_rows(root_rows, slope_two), cross_rows(near_two, slope_tw...]
    pallas_call x0 -> x4, Pallas kernels: none -> 87.1 us  [the longest x1 41.9 us: aggregate(): pl.pallas_call(aggregate_kernel, out_shape=jax.ShapeDtypeStruct((owners,...]
    all_to_all x0 -> x2, blocking collectives: none -> 81 us  [exchange(): return lax.all_to_all(value, axes, split_axis=0, concat_axis=0, tiled=True)]
    psum x1 -> x0, blocking collectives: 67.6 us -> none  [local(): lax.psum((cross_rows(root_rows, slope_two), cross_rows(near_two, slope_tw...]
    gather x3 -> x0, local copies, waits for them, and re-layouts: 60.3 us -> none  [the longest x1 23 us: local(): slot_own = jnp.take(first_center, slot_node, axis=0, mode='clip')]
    slice x23 -> x0, local copies, waits for them, and re-layouts: 19.2 us -> none  [the longest x4 6.83 us: local(): owner_center[low:high]]
    all_gather x1 -> x0, blocking collectives: 15.7 us -> none  [in_one_piece(): out = lax.all_gather(both, axis, axis=dim, tiled=True)]
  transfers between devices with their start and end apart: 2 -> 5, of which waited for: 1 -> 3; matrix products, arithmetic and copies ran while one was open for 0% -> 4% of each run, Pallas kernels for 0% -> 24%
where the time goes in v1:
time: 216 us
  Pallas kernels  87.1 us (40%)
  blocking collectives  81 us (38%)
  starting transfers between devices  18.3 us (8%)
  waiting for transfers between devices  12.1 us (6%)
  local copies, waits for them, and re-layouts  9.32 us (4%)
  other arithmetic  7.3 us (3%)
    all_to_all x2, blocking collectives, exchange(): return lax.all_to_all(value, axes, split_axis=0, concat_axis=0, tiled=True)  81 us
    pallas_call x1, Pallas kernels, aggregate(): pl.pallas_call(aggregate_kernel, out_shape=jax.ShapeDtypeStruct((owners,...  41.9 us
    pallas_call x1, Pallas kernels, owner_step(): pl.pallas_call(owner_kernel, out_shape=(jax.ShapeDtypeStruct((nodes, hidd...  27.6 us
    pallas_call x1, Pallas kernels, picks(): pl.pallas_call(picks_kernel, out_shape=(jax.ShapeDtypeStruct((2 * nodes,...  11 us
    all_to_all x1, starting transfers between devices, exchange(): return lax.all_to_all(value, axes, split_axis=0, concat_axis=0, tiled=True)  8.33 us
    pallas_call x1, Pallas kernels, spread(): pl.pallas_call(spread_kernel, out_shape=(square, square, slab, slab, line...  6.66 us
    unnamed x15, local copies, waits for them, and re-layouts  5.91 us
    ppermute x1, waiting for transfers between devices, local(): received = lax.ppermute(sent, 'core', [(0, 1), (1, 0)])  4.56 us
  transfers between devices with their start and end apart: 5, of which 3 were waited for; matrix products, arithmetic and copies ran while one was open for 4% of the time, Pallas kernels for 24%

profile of v1, /device:TPU:1, one launch (start us, length us, event | category | flops | bytes accessed | tf_op | source)
XLA Modules:
  0.0 215.9 jit_solution(10036958962982209604)
XLA Ops:
  0.6 0.8 constant_dynamic-update-slice_fusion.1
  1.5 0.8 constant_dynamic-update-slice_fusion
  2.3 2.5 %collective-permute-start = (bf16[64,1024]{1,0:T(8,128)(2,1)S(1)}, bf16[64,1024]{1,0:T(8,128)(2,1)S(1)}, u32[]{:S(2)}, u32[]{:S(2)}) collective-permute-start(bf16[64,1024]{1,0:T(8,128)(2,1)S(1)} %constant_dynamic-update-slice_fusion), channel_id=1, source_target_pairs={{0,32},{32,0},{64,96},{96,64},{1,33},{33,1},{65,97},{97,65},{2,34}... | collective-permute-start | bytes 393224 | tf_op jit(solution)/shard_map/ppermute | solution.py:377
  4.8 3.2 %collective-permute-done = bf16[64,1024]{1,0:T(8,128)(2,1)S(1)} collective-permute-done((bf16[64,1024]{1,0:T(8,128)(2,1)S(1)}, bf16[64,1024]{1,0:T(8,128)(2,1)S(1)}, u32[]{:S(2)}, u32[]{:S(2)}) %collective-permute-start) | collective-permute-done | bytes 131104 | tf_op jit(solution)/shard_map/ppermute | solution.py:377
  8.0 0.0 copy-start.3
  8.0 0.0 copy-start.2
  8.1 0.0 copy-start.4
  8.1 3.4 %collective-permute-start.1 = (bf16[128,1024]{1,0:T(8,128)(2,1)S(1)}, bf16[128,1024]{1,0:T(8,128)(2,1)S(1)}, u32[]{:S(2)}, u32[]{:S(2)}) collective-permute-start(bf16[128,1024]{1,0:T(8,128)(2,1)S(1)} %pad_maximum_fusion.1), channel_id=1, source_target_pairs={{0,96},{96,0},{32,64},{64,32},{1,97},{97,1},{33,65},{65,33},{2,98}... | collective-permute-start | bytes 786440 | tf_op jit(solution)/shard_map/ppermute | solution.py:380
  11.4 1.6 add_bitcast_fusion.adj_ref
  13.0 41.9 %aggregate.1 = bf16[128,2048]{1,0:T(8,128)(2,1)} custom-call(bf16[32,4096]{1,0:T(8,128)(2,1)} %feat_ref.1, s32[16,2048]{1,0:T(8,128)} %add_bitcast_fusion.adj_ref, s32[1,2048]{1,0:T(1,128)} %bitcast.19, s32[1,2048]{1,0:T(1,128)} %bitcast.20), custom_call_target="tpu_custom_call" | custom-call | flops 40000000 | bytes 3000000 | tf_op jit(solution)/shard_map/aggregate/pallas_call | solution.py:128
  54.9 0.5 broadcast.1
  55.5 2.0 reduce.1
  57.5 1.2 reshape.17
  58.6 8.3 %all-to-all-start = ((bf16[128,2,1024]{2,1,0:T(2,128)(2,1)}), bf16[128,2,1024]{2,1,0:T(2,128)(2,1)S(1)}, u32[]{:S(2)}, u32[]{:S(2)}) async-start(bf16[128,2,1024]{2,1,0:T(2,128)(2,1)} %reshape.17), calls=%async_computation | async-start | bytes 1048576 | tf_op jit(solution)/shard_map/all_to_all | solution.py:386
  67.0 0.0 copy-done.3
  67.0 0.9 copy.35.count_ref
  67.9 0.0 copy-done.2
  67.9 0.9 copy.33.adj_ref
  68.7 0.0 copy-done.4
  68.7 0.9 copy.34.center_ref
  69.6 11.0 %picks.1 = (bf16[1024,1024]{1,0:T(8,128)(2,1)}, bf16[1024,1024]{1,0:T(8,128)(2,1)}) custom-call(s32[512,10]{1,0:T(8,128)} %copy.33.adj_ref, s32[512,1]{1,0:T(8,128)} %copy.34.center_ref, s32[512,1]{1,0:T(8,128)} %copy.35.count_ref), custom_call_target="tpu_custom_call" | custom-call | flops 20000000 | bytes 5000000 | tf_op jit(solution)/shard_map/picks/pallas_call | solution.py:180
  80.6 0.0 collective-permute-done.1
  80.6 0.1 broadcast_select_fusion.1
  80.7 0.8 pad_maximum_fusion.first_ref
  81.5 0.0 all-to-all-done
  81.5 0.4 reshape.18
  82.0 1.1 copy.39
  83.1 27.6 %owner_step.1 = (bf16[512,1024]{1,0:T(8,128)(2,1)}, bf16[64,152,128]{2,1,0:T(8,128)(2,1)}, bf16[64,152,128]{2,1,0:T(8,128)(2,1)}) custom-call(s32[1]{0:T(128)} %bitcast.core_ref, bf16[128,2048]{1,0:T(8,128)(2,1)} %bitcast.18, bf16[256,1024]{1,0:T(8,128)(2,1)} %pad_maximum_fusion.first_ref, f32[1,1024]{1,0:T(1,128)} %bitcast.24, ...), custom_call_target="tpu_custom_call" | custom-call | flops 12000000000 | bytes 18000000 | tf_op jit(solution)/shard_map/owner_step/pallas_call | solution.py:307
  110.6 1.2 collective-permute-start.2
  111.9 4.6 %collective-permute-done.2 = bf16[64,152,128]{2,1,0:T(8,128)(2,1)S(1)} collective-permute-done((bf16[64,152,128]{2,1,0:T(8,128)(2,1)}, bf16[64,152,128]{2,1,0:T(8,128)(2,1)S(1)}, u32[]{:S(2)}, u32[]{:S(2)}) %collective-permute-start.2) | collective-permute-done | bytes 2490400 | tf_op jit(solution)/shard_map/ppermute | solution.py:420
  116.5 2.3 %add_convert_fusion = bf16[64,152,128]{2,1,0:T(8,128)(2,1)S(1)} fusion(bf16[64,152,128]{2,1,0:T(8,128)(2,1)S(1)} %collective-permute-done.2, bf16[64,152,128]{2,1,0:T(8,128)(2,1)} %get-tuple-element.21), kind=kLoop, calls=%fused_computation | loop fusion | flops 4980736 | bytes 7471104 | tf_op jit(solution)/shard_map/convert_element_type | solution.py:421
  118.8 42.9 %all_to_all.21 = bf16[64,152,128]{2,1,0:T(8,128)(2,1)S(1)} all-to-all(bf16[64,152,128]{2,1,0:T(8,128)(2,1)S(1)} %add_convert_fusion), channel_id=1, replica_groups=mesh['z'=4,'x'=4,'y'=4,'core'=2] {'z','x','y'}, dimensions={0} | all-to-all | bytes 4980736 | tf_op jit(solution)/shard_map/all_to_all | solution.py:386
  161.7 0.4 reduce_sum.12
  162.0 0.3 broadcast_in_dim.42
  162.4 38.1 %all_to_all.22.kept_ref = bf16[64,152,128]{2,1,0:T(8,128)(2,1)S(1)} all-to-all(bf16[64,152,128]{2,1,0:T(8,128)(2,1)S(1)} %broadcast_in_dim.42), channel_id=1, replica_groups=mesh['z'=4,'x'=4,'y'=4,'core'=2] {'z','x','y'}, dimensions={0} | all-to-all | bytes 4980736 | tf_op jit(solution)/shard_map/all_to_all | solution.py:386
  200.5 0.0 copy-start
  200.5 2.9 %collective-permute-start.3 = (bf16[64,152,128]{2,1,0:T(8,128)(2,1)S(1)}, bf16[64,152,128]{2,1,0:T(8,128)(2,1)S(1)}, u32[]{:S(2)}, u32[]{:S(2)}) collective-permute-start(bf16[64,152,128]{2,1,0:T(8,128)(2,1)S(1)} %all_to_all.22.kept_ref), channel_id=1, source_target_pairs={{0,1},{1,0},{2,3},{3,2},{4,5},{5,4},{6,7},{7,6},{8,9},{9,8},{10,11... | collective-permute-start | bytes 7471112 | tf_op jit(solution)/shard_map/ppermute | solution.py:425
  203.4 4.3 %collective-permute-done.3.other_ref = bf16[64,152,128]{2,1,0:T(8,128)(2,1)S(1)} collective-permute-done((bf16[64,152,128]{2,1,0:T(8,128)(2,1)S(1)}, bf16[64,152,128]{2,1,0:T(8,128)(2,1)S(1)}, u32[]{:S(2)}, u32[]{:S(2)}) %collective-permute-start.3) | collective-permute-done | bytes 2490400 | tf_op jit(solution)/shard_map/ppermute | solution.py:425
  207.7 0.0 copy-start.1
  207.7 1.5 copy-done.1
  209.2 0.0 copy-done
  209.2 6.7 %spread.1 = (f32[1024,1024]{1,0:T(8,128)}, f32[1024,1024]{1,0:T(8,128)}, f32[32,1024]{1,0:T(8,128)}, f32[32,1024]{1,0:T(8,128)}, f32[1,1024]{1,0:T(1,128)}, /*index=5*/f32[1,1024]{1,0:T(1,128)}) custom-call(s32[1]{0:T(128)} %bitcast.core_ref, s32[1]{0:T(128)} %bitcast.10.z_ref, bf16[64,152,128]{2,1,0:T(8,128)(2,1)} %copy-done, bf16[64,152,128]{2,1,0:T(8,128)(2,1)} %copy-done.1), custom_call_target="tpu_custom_call" | custom-call | tf_op jit(solution)/shard_map/spread/pallas_call | solution.py:367
  (2 shorter events, 0.0 us)
Async XLA Ops:
  2.3 5.7 %collective-permute-start = (bf16[64,1024]{1,0:T(8,128)(2,1)S(1)}, bf16[64,1024]{1,0:T(8,128)(2,1)S(1)}, u32[]{:S(2)}, u32[]{:S(2)}) collective-permute-start(bf16[64,1024]{1,0:T(8,128)(2,1)S(1)} %constant_dynamic-update-slice_fusion), channel_id=1, source_target_pairs={{0,32},{32,0},{64,96},{96,64},{1,33},{33,1},{65,97},{97,65},{2,34}... | collective-permute-start | bytes 393224 | tf_op jit(solution)/shard_map/ppermute | solution.py:377
  8.0 59.0 %copy-start.3 = (s32[512]{0:T(512)S(1)}, s32[512]{0:T(512)}, u32[]{:S(2)}) copy-start(s32[512]{0:T(512)} %param.25) | copy-start | bytes 6148
  8.0 59.9 %copy-start.2 = (s32[512,10]{0,1:T(8,128)S(1)}, s32[512,10]{0,1:T(8,128)}, u32[]{:S(2)}) copy-start(s32[512,10]{0,1:T(8,128)} %param.23) | copy-start | bytes 61444
  8.1 60.7 %copy-start.4 = (s32[512]{0:T(512)S(1)}, s32[512]{0:T(512)}, u32[]{:S(2)}) copy-start(s32[512]{0:T(512)} %param.24) | copy-start | bytes 6148
  8.1 72.5 %collective-permute-start.1 = (bf16[128,1024]{1,0:T(8,128)(2,1)S(1)}, bf16[128,1024]{1,0:T(8,128)(2,1)S(1)}, u32[]{:S(2)}, u32[]{:S(2)}) collective-permute-start(bf16[128,1024]{1,0:T(8,128)(2,1)S(1)} %pad_maximum_fusion.1), channel_id=1, source_target_pairs={{0,96},{96,0},{32,64},{64,32},{1,97},{97,1},{33,65},{65,33},{2,98}... | collective-permute-start | bytes 786440 | tf_op jit(solution)/shard_map/ppermute | solution.py:380
  58.6 22.9 %all-to-all-start = ((bf16[128,2,1024]{2,1,0:T(2,128)(2,1)}), bf16[128,2,1024]{2,1,0:T(2,128)(2,1)S(1)}, u32[]{:S(2)}, u32[]{:S(2)}) async-start(bf16[128,2,1024]{2,1,0:T(2,128)(2,1)} %reshape.17), calls=%async_computation | async-start | bytes 1048576 | tf_op jit(solution)/shard_map/all_to_all | solution.py:386
  110.6 5.8 %collective-permute-start.2 = (bf16[64,152,128]{2,1,0:T(8,128)(2,1)}, bf16[64,152,128]{2,1,0:T(8,128)(2,1)S(1)}, u32[]{:S(2)}, u32[]{:S(2)}) collective-permute-start(bf16[64,152,128]{2,1,0:T(8,128)(2,1)} %get-tuple-element.22), channel_id=1, source_target_pairs={{0,1},{1,0},{2,3},{3,2},{4,5},{5,4},{6,7},{7,6},{8,9},{9,8},{10,11... | collective-permute-start | bytes 7471112 | tf_op jit(solution)/shard_map/ppermute | solution.py:420
  200.5 8.7 %copy-start = (bf16[64,152,128]{2,1,0:T(8,128)(2,1)}, bf16[64,152,128]{2,1,0:T(8,128)(2,1)S(1)}, u32[]{:S(2)}) copy-start(bf16[64,152,128]{2,1,0:T(8,128)(2,1)S(1)} %all_to_all.22.kept_ref) | copy-start | bytes 7471108
  200.5 7.2 %collective-permute-start.3 = (bf16[64,152,128]{2,1,0:T(8,128)(2,1)S(1)}, bf16[64,152,128]{2,1,0:T(8,128)(2,1)S(1)}, u32[]{:S(2)}, u32[]{:S(2)}) collective-permute-start(bf16[64,152,128]{2,1,0:T(8,128)(2,1)S(1)} %all_to_all.22.kept_ref), channel_id=1, source_target_pairs={{0,1},{1,0},{2,3},{3,2},{4,5},{5,4},{6,7},{7,6},{8,9},{9,8},{10,11... | collective-permute-start | bytes 7471112 | tf_op jit(solution)/shard_map/ppermute | solution.py:425
  207.7 1.5 copy-start.1

commit v2 on v1

--- a/solution.py
+++ b/solution.py
@@ -11,6 +11,13 @@
 CHIPS = ("z", "x", "y")
 CHUNK = 152
 VMEM = pl.BlockSpec(memory_space=pltpu.VMEM)
+ALONG_LANES = lax.GatherDimensionNumbers(
+    offset_dims=(),
+    collapsed_slice_dims=(1,),
+    start_index_map=(1,),
+    operand_batching_dims=(0,),
+    start_indices_batching_dims=(0,),
+)
 SMEM = pl.BlockSpec(memory_space=pltpu.SMEM)
 
 
@@ -34,41 +41,66 @@
     return jnp.dot(left, right, preferred_element_type=jnp.float32)
 
 
-def aggregate_kernel(feat_ref, adj_ref, count_ref, owner_ref, out_ref, table, rows, places, stage):
+def take_lanes(rows, index):
+    return lax.gather(
+        rows, index[..., None], ALONG_LANES, (1, 1), mode=lax.GatherScatterMode.PROMISE_IN_BOUNDS
+    )
+
+
+def find(load, high, low, chunks, parts):
+    bits = [lax.bitwise_and(high, jnp.int16(1 << b)) != jnp.int16(0) for b in range(5)]
+
+    def among(start, size, bit):
+        if size == 1:
+            return [take_lanes(load(start, v), low) for v in range(parts)]
+        first = among(start, size // 2, bit - 1)
+        last = among(start + size // 2, size // 2, bit - 1)
+        return [jnp.where(bits[bit], q, p) for p, q in zip(first, last)]
+
+    return among(0, chunks, chunks.bit_length() - 2)
+
+
+def aggregate_kernel(feat_ref, adj_ref, count_ref, owner_ref, out_ref, index, rows, places, stage, wide):
     width, inputs = feat_ref.shape
     nodes = owner_ref.shape[1]
     owners = out_ref.shape[0]
     fan = adj_ref.shape[0] - 1
     chunks = inputs // LANES
     groups = nodes // LANES
-    parts = width // 8
-    for c in range(chunks):
-        table[c] = feat_ref[:, c * LANES : (c + 1) * LANES].astype(jnp.float32)
+    parts = width // 16
+    steps = (fan + 1) // 4
+    i16, bf16, f32 = jnp.int16, jnp.bfloat16, jnp.float32
+    for g in range(groups):
+        for s in range(steps):
+            index[g * steps + s, 0:4] = adj_ref[s * 4 : s * 4 + 4, g * LANES : (g + 1) * LANES]
 
     def one_group(g, carry):
         count = count_ref[:, lanes_at(g)]
-        total = [jnp.zeros((8, LANES), jnp.float32) for _ in range(parts)]
-        for k in range(fan + 1):
-            index = jnp.broadcast_to(adj_ref[k : k + 1, lanes_at(g)], (8, LANES))
-            high = lax.shift_right_logical(index, 7)
-            low = lax.bitwise_and(index, LANES - 1)
-            found = [jnp.zeros((8, LANES), jnp.float32) for _ in range(parts)]
-            for c in range(chunks):
-                here = high == c
+
+        def four(s, total):
+            total = list(total)
+            for j in range(4):
+                at = index[g * steps + s, j : j + 1, :]
+                high = jnp.broadcast_to(lax.shift_right_logical(at, 7), (16, LANES)).astype(i16)
+                low = jnp.broadcast_to(lax.bitwise_and(at, LANES - 1), (16, LANES)).astype(i16)
+                valid = jnp.broadcast_to(s * 4 + j < count, (16, LANES))
+                found = find(
+                    lambda c, v: feat_ref[v * 16 : (v + 1) * 16, c * LANES : (c + 1) * LANES],
+                    high, low, chunks, parts,
+                )
+                if j == 3:
+                    for v in range(parts):
+                        rows[v * 16 : (v + 1) * 16, lanes_at(g)] = found[v]
                 for v in range(parts):
-                    got = jnp.take_along_axis(
-                        table[c, v * 8 : (v + 1) * 8, :], low, axis=1, mode="promise_in_bounds"
-                    )
-                    found[v] = jnp.where(here, got, found[v])
-            if k < fan:
-                valid = jnp.broadcast_to(k < count, (8, LANES))
-                total = [a + jnp.where(valid, b, 0.0) for a, b in zip(total, found)]
-            else:
-                for v in range(parts):
-                    rows[v * 8 : (v + 1) * 8, lanes_at(g)] = found[v]
-        divisor = jnp.broadcast_to(count.astype(jnp.float32), (8, LANES))
+                    total[v] = total[v] + jnp.where(valid, found[v].astype(f32), 0.0)
+            return tuple(total)
+
+        zero = jnp.zeros((16, LANES), f32)
+        total = lax.fori_loop(0, steps, four, (zero,) * parts)
+        divisor = jnp.broadcast_to(count.astype(f32), (16, LANES))
         for v in range(parts):
-            rows[width + v * 8 : width + (v + 1) * 8, lanes_at(g)] = total[v] / divisor
+            near = (total[v] / divisor).astype(bf16)
+            rows[width + v * 16 : width + (v + 1) * 16, lanes_at(g)] = near
         return carry
 
     lax.fori_loop(0, groups, one_group, 0)
@@ -77,14 +109,14 @@
     before = (
         lax.broadcasted_iota(jnp.int32, (span, span), 0)
         < lax.broadcasted_iota(jnp.int32, (span, span), 1)
-    ).astype(jnp.bfloat16)
+    ).astype(bf16)
     owner_ids = lax.broadcasted_iota(jnp.int32, (owners, span), 0)
     ranks = lax.broadcasted_iota(jnp.int32, (CAP, span), 0)
-    seen = jnp.zeros((owners, 1), jnp.float32)
-    found_at = jnp.zeros((3 * CAP, owners), jnp.float32)
+    seen = jnp.zeros((owners, 1), f32)
+    found_at = jnp.zeros((3 * CAP, owners), f32)
     for b in range(nodes // span):
         hit = owner_ids == owner_ref[:, b * span : (b + 1) * span]
-        picked = hit.astype(jnp.bfloat16)
+        picked = hit.astype(bf16)
         earlier = matmul(picked, before) + seen
         rank = jnp.sum(jnp.where(hit, earlier, 0.0), axis=0, keepdims=True).astype(jnp.int32)
         seen = seen + jnp.sum(jnp.where(hit, 1.0, 0.0), axis=1, keepdims=True)
@@ -92,34 +124,45 @@
         mine = ranks == rank
         weights = jnp.concatenate(
             [
-                jnp.where(mine, lax.shift_right_logical(node, 7), 0).astype(jnp.float32),
-                jnp.where(mine, lax.bitwise_and(node, LANES - 1), 0).astype(jnp.float32),
+                jnp.where(mine, lax.shift_right_logical(node, 7), 0).astype(f32),
+                jnp.where(mine, lax.bitwise_and(node, LANES - 1), 0).astype(f32),
                 jnp.where(mine, 1.0, 0.0),
             ],
             axis=0,
-        ).astype(jnp.bfloat16)
+        ).astype(bf16)
         found_at = found_at + along(weights, picked)
-    places[...] = found_at.astype(jnp.int32)
+    found_at = found_at.astype(jnp.int32)
+    for q in range(CAP // 4):
+        for kind in range(3):
+            at = kind * CAP + q * 4
+            places[q, kind * 4 : (kind + 1) * 4] = found_at[at : at + 4]
 
     half = 2 * width
-    for pair in range(CAP // 2):
-        for j in range(2):
-            r = pair * 2 + j
-            high = jnp.broadcast_to(places[r : r + 1, :], (8, owners))
-            low = jnp.broadcast_to(places[CAP + r : CAP + r + 1, :], (8, owners))
-            filled = jnp.broadcast_to(places[2 * CAP + r : 2 * CAP + r + 1, :], (8, owners)) > 0
-            for v in range(half // 8):
-                found = jnp.zeros((8, owners), jnp.float32)
-                for g in range(groups):
-                    got = jnp.take_along_axis(
-                        rows[v * 8 : (v + 1) * 8, g * LANES : (g + 1) * LANES],
-                        low,
-                        axis=1,
-                        mode="promise_in_bounds",
-                    )
-                    found = jnp.where(high == g, got, found)
-                stage[j * half + v * 8 : j * half + (v + 1) * 8, :] = jnp.where(filled, found, 0.0)
-        out_ref[:, pair * LANES : (pair + 1) * LANES] = stage[...].T.astype(out_ref.dtype)
+
+    def four_ranks(q, carry):
+        for j in range(4):
+            high = jnp.broadcast_to(places[q, j : j + 1, :], (16, owners)).astype(i16)
+            low = jnp.broadcast_to(places[q, 4 + j : 5 + j, :], (16, owners)).astype(i16)
+            filled = jnp.broadcast_to(places[q, 8 + j : 9 + j, :], (16, owners)) > 0
+            found = find(
+                lambda c, v: rows[v * 16 : (v + 1) * 16, c * LANES : (c + 1) * LANES],
+                high, low, groups, half // 16,
+            )
+            for v in range(half // 16):
+                at = (j % 2) * half + v * 16
+                stage[j // 2, at : at + 16, :] = jnp.where(filled, found[v].astype(f32), 0.0)
+        for pair in range(2):
+            wide[pl.ds(q * 2 + pair, owners, stride=16), :] = stage[pair].T
+        return carry
+
+    lax.fori_loop(0, CAP // 4, four_ranks, 0)
+
+    def finish(t, carry):
+        at = pl.ds(pl.multiple_of(t * 8, 8), 8)
+        out_ref[at] = wide[lanes_at(t), :].astype(bf16).reshape(8, 16, LANES)
+        return carry
+
+    lax.fori_loop(0, owners // 8, finish, 0)
 
 
 def aggregate(features, adjacent, count, owner, owners):
@@ -127,14 +170,15 @@
     nodes = owner.shape[1]
     return pl.pallas_call(
         aggregate_kernel,
-        out_shape=jax.ShapeDtypeStruct((owners, CAP * 2 * width), jnp.bfloat16),
+        out_shape=jax.ShapeDtypeStruct((owners, 16, LANES), jnp.bfloat16),
         in_specs=[VMEM] * 4,
         out_specs=VMEM,
         scratch_shapes=[
-            pltpu.VMEM((inputs // LANES, width, LANES), jnp.float32),
-            pltpu.VMEM((2 * width, nodes), jnp.float32),
-            pltpu.VMEM((3 * CAP, owners), jnp.int32),
-            pltpu.VMEM((4 * width, owners), jnp.float32),
+            pltpu.VMEM((nodes // LANES * 4, 4, LANES), jnp.int32),
+            pltpu.VMEM((2 * width, nodes), jnp.bfloat16),
+            pltpu.VMEM((CAP // 4, 12, LANES), jnp.int32),
+            pltpu.VMEM((2, 4 * width, owners), jnp.float32),
+            pltpu.VMEM((16 * owners, LANES), jnp.float32),
         ],
         name="aggregate",
         cost_estimate=pl.CostEstimate(flops=40_000_000, bytes_accessed=3_000_000, transcendentals=0),
@@ -146,7 +190,9 @@
     slots = out_ref.shape[1]
 
     def table_row(slot):
-        return lax.bitwise_and(slot, CAP - 1) * (slots // CAP) + lax.shift_right_logical(slot, 5)
+        odd = lax.shift_left(lax.bitwise_and(slot, 1), 4)
+        pair = lax.bitwise_and(lax.shift_right_logical(slot, 1), 15)
+        return lax.bitwise_and(slot, -CAP) + odd + pair
 
     def one_tile(t, carry):
         at = pl.ds(pl.multiple_of(t * 16, 16), 16)
@@ -202,12 +248,17 @@
     quarter = depth // 4
     sources = slots // CAP
     tile = 256
-    for r in range(CAP):
-        pieces = [
-            arrived_ref[f * sources : (f + 1) * sources, r * quarter : (r + 1) * quarter]
-            for f in range(4)
-        ]
-        inputs[r * sources : (r + 1) * sources, :] = jnp.concatenate(pieces, axis=1)
+
+    def one_source(t, carry):
+        for e in range(2):
+            pieces = [
+                arrived_ref[f * sources + t, :, e * quarter : (e + 1) * quarter] for f in range(4)
+            ]
+            at = pl.ds(pl.multiple_of(t * CAP + e * 16, 16), 16)
+            inputs[at, :] = jnp.concatenate(pieces, axis=1)
+        return carry
+
+    lax.fori_loop(0, sources, one_source, 0)
     for t in range(slots // tile):
         inputs_flip[:, t * tile : (t + 1) * tile] = inputs[t * tile : (t + 1) * tile, :].T
 
@@ -373,10 +424,13 @@
     )(core, z, kept, other)
 
 
-def weights_of_all(own, z):
+def weights_of_pair(own, z):
     first = lax.ppermute(own, "z", [(0, 1), (1, 0), (2, 3), (3, 2)])
     odd = lax.bitwise_and(z, 1) == 1
-    pair = jnp.concatenate([jnp.where(odd, first, own), jnp.where(odd, own, first)], axis=0)
+    return jnp.concatenate([jnp.where(odd, first, own), jnp.where(odd, own, first)], axis=0)
+
+
+def weights_of_all(pair, z):
     second = lax.ppermute(pair, "z", [(0, 3), (3, 0), (1, 2), (2, 1)])
     late = z >= 2
     return jnp.concatenate([jnp.where(late, second, pair), jnp.where(late, pair, second)], axis=0)
@@ -407,9 +461,11 @@
     hidden_width = first_root.shape[1]
     z = lax.axis_index("z")
     core = lax.axis_index("core")[None]
-    first_all = weights_of_all(jnp.concatenate([first_root, first_near], axis=0), z)
+    pair = weights_of_pair(jnp.concatenate([first_root, first_near], axis=0), z)
     columns = jnp.concatenate([first_adjacent, first_center[:, None]], axis=1).T
     packed = aggregate(features, columns, first_count[None], owner_map[None], owners)
+    packed, pair = lax.optimization_barrier((packed, pair))
+    first_all = weights_of_all(pair, z)
     arrived = exchange(packed, AXES)
     count = second_count[:, None]
     picked, flipped = picks(second_adjacent, second_center[:, None], count, owners * 8)

time: 216 us -> 197 us (0.912)
  Pallas kernels: 87.1 us -> 76.6 us
  waiting for transfers between devices: 12.1 us -> 8.92 us
  local copies, waits for them, and re-layouts: 9.32 us -> 6.93 us
    pallas_call x1, Pallas kernels: 41.9 us -> 29.2 us  [aggregate(): pl.pallas_call(aggregate_kernel, out_shape=jax.ShapeDtypeStruct((owners,...]
    ppermute x1, waiting for transfers between devices: 3.2 us -> 0.01 us  [weights_of_pair(): first = lax.ppermute(own, 'z', [(0, 1), (1, 0), (2, 3), (3, 2)])]
    pallas_call x1, Pallas kernels: 27.6 us -> 29.8 us  [owner_step(): pl.pallas_call(owner_kernel, out_shape=(jax.ShapeDtypeStruct((nodes, hidd...]
    unnamed x15 -> x14, local copies, waits for them, and re-layouts: 5.91 us -> 4.03 us
  transfers between devices with their start and end apart: 5 -> 5, of which waited for: 3 -> 2; matrix products, arithmetic and copies ran while one was open for 4% -> 3% of each run, Pallas kernels for 24% -> 20%
where the time goes in v2:
time: 197 us
  blocking collectives  81.2 us (41%)
  Pallas kernels  76.6 us (39%)
  starting transfers between devices  17 us (9%)
  waiting for transfers between devices  8.92 us (5%)
  local copies, waits for them, and re-layouts  6.93 us (4%)
  other arithmetic  5.22 us (3%)
    all_to_all x2, blocking collectives, exchange(): return lax.all_to_all(value, axes, split_axis=0, concat_axis=0, tiled=True)  81.2 us
    pallas_call x1, Pallas kernels, owner_step(): pl.pallas_call(owner_kernel, out_shape=(jax.ShapeDtypeStruct((nodes, hidd...  29.8 us
    pallas_call x1, Pallas kernels, aggregate(): pl.pallas_call(aggregate_kernel, out_shape=jax.ShapeDtypeStruct((owners,...  29.2 us
    pallas_call x1, Pallas kernels, picks(): pl.pallas_call(picks_kernel, out_shape=(jax.ShapeDtypeStruct((2 * nodes,...  11 us
    all_to_all x1, starting transfers between devices, exchange(): return lax.all_to_all(value, axes, split_axis=0, concat_axis=0, tiled=True)  8.27 us
    pallas_call x1, Pallas kernels, spread(): pl.pallas_call(spread_kernel, out_shape=(square, square, slab, slab, line...  6.66 us
    ppermute x1, waiting for transfers between devices, local(): received = lax.ppermute(sent, 'core', [(0, 1), (1, 0)])  4.56 us
    ppermute x1, waiting for transfers between devices, local(): other = lax.ppermute(mine, 'core', [(0, 1), (1, 0)])  4.35 us
  transfers between devices with their start and end apart: 5, of which 2 were waited for; matrix products, arithmetic and copies ran while one was open for 3% of the time, Pallas kernels for 20%

profile of v2, /device:TPU:1, one launch (start us, length us, event | category | flops | bytes accessed | tf_op | source)
XLA Modules:
  0.0 196.6 jit_solution(8747880854773682860)
XLA Ops:
  0.6 0.0 copy-start.4
  0.6 0.0 copy-start.3
  0.7 0.0 copy-start.5
  0.7 0.9 constant_dynamic-update-slice_fusion.1
  1.5 0.8 constant_dynamic-update-slice_fusion
  2.4 2.5 %collective-permute-start = (bf16[64,1024]{1,0:T(8,128)(2,1)S(1)}, bf16[64,1024]{1,0:T(8,128)(2,1)S(1)}, u32[]{:S(2)}, u32[]{:S(2)}) collective-permute-start(bf16[64,1024]{1,0:T(8,128)(2,1)S(1)} %constant_dynamic-update-slice_fusion), channel_id=1, source_target_pairs={{0,32},{32,0},{64,96},{96,64},{1,33},{33,1},{65,97},{97,65},{2,34}... | collective-permute-start | bytes 393224 | tf_op jit(solution)/shard_map/ppermute | solution.py:428
  4.8 1.6 add_bitcast_fusion.adj_ref
  6.4 29.2 %aggregate.1 = bf16[128,16,128]{2,1,0:T(8,128)(2,1)} custom-call(bf16[32,4096]{1,0:T(8,128)(2,1)} %feat_ref.1, s32[16,2048]{1,0:T(8,128)} %add_bitcast_fusion.adj_ref, s32[1,2048]{1,0:T(1,128)} %bitcast.13, s32[1,2048]{1,0:T(1,128)} %bitcast.14), custom_call_target="tpu_custom_call" | custom-call | flops 40000000 | bytes 3000000 | tf_op jit(solution)/shard_map/aggregate/pallas_call | solution.py:171
  35.7 0.0 collective-permute-done
  35.7 2.3 %collective-permute-start.1 = (bf16[128,1024]{1,0:T(8,128)(2,1)S(1)}, bf16[128,1024]{1,0:T(8,128)(2,1)S(1)}, u32[]{:S(2)}, u32[]{:S(2)}) collective-permute-start(bf16[128,1024]{1,0:T(8,128)(2,1)S(1)} %pad_maximum_fusion.1), channel_id=1, source_target_pairs={{0,96},{96,0},{32,64},{64,32},{1,97},{97,1},{33,65},{65,33},{2,98}... | collective-permute-start | bytes 786440 | tf_op jit(solution)/shard_map/ppermute | solution.py:434
  38.0 8.3 %all-to-all-start = ((bf16[128,16,128]{2,1,0:T(8,128)(2,1)}), bf16[128,16,128]{2,1,0:T(8,128)(2,1)S(1)}, u32[]{:S(2)}, u32[]{:S(2)}) async-start(bf16[128,16,128]{2,1,0:T(8,128)(2,1)} %aggregate.1), calls=%async_computation | async-start | bytes 1048576 | tf_op jit(solution)/shard_map/all_to_all | solution.py:440
  46.3 0.0 copy-done.4
  46.3 0.9 copy.25.count_ref
  47.2 0.0 copy-done.3
  47.2 0.9 copy.23.adj_ref
  48.1 0.0 copy-done.5
  48.1 0.9 copy.24.center_ref
  48.9 11.0 %picks.1 = (bf16[1024,1024]{1,0:T(8,128)(2,1)}, bf16[1024,1024]{1,0:T(8,128)(2,1)}) custom-call(s32[512,10]{1,0:T(8,128)} %copy.23.adj_ref, s32[512,1]{1,0:T(8,128)} %copy.24.center_ref, s32[512,1]{1,0:T(8,128)} %copy.25.count_ref), custom_call_target="tpu_custom_call" | custom-call | flops 20000000 | bytes 5000000 | tf_op jit(solution)/shard_map/picks/pallas_call | solution.py:226
  59.9 0.0 collective-permute-done.1
  59.9 0.8 pad_maximum_fusion.first_ref
  60.8 0.0 all-to-all-done.arrived_ref
  60.8 0.0 copy-start.2
  60.8 0.8 copy-done.2
  61.6 29.8 %owner_step.1 = (bf16[512,1024]{1,0:T(8,128)(2,1)}, bf16[64,152,128]{2,1,0:T(8,128)(2,1)}, bf16[64,152,128]{2,1,0:T(8,128)(2,1)}) custom-call(s32[1]{0:T(128)} %bitcast.core_ref, bf16[128,16,128]{2,1,0:T(8,128)(2,1)} %copy-done.2, bf16[256,1024]{1,0:T(8,128)(2,1)} %pad_maximum_fusion.first_ref, f32[1,1024]{1,0:T(1,128)} %bitcast.18, ...), custom_call_target="tpu_custom_call" | custom-call | flops 12000000000 | bytes 18000000 | tf_op jit(solution)/shard_map/owner_step/pallas_call | solution.py:358
  91.4 1.1 collective-permute-start.2
  92.4 4.6 %collective-permute-done.2 = bf16[64,152,128]{2,1,0:T(8,128)(2,1)S(1)} collective-permute-done((bf16[64,152,128]{2,1,0:T(8,128)(2,1)}, bf16[64,152,128]{2,1,0:T(8,128)(2,1)S(1)}, u32[]{:S(2)}, u32[]{:S(2)}) %collective-permute-start.2) | collective-permute-done | bytes 2490400 | tf_op jit(solution)/shard_map/ppermute | solution.py:476
  97.0 2.3 %add_convert_fusion = bf16[64,152,128]{2,1,0:T(8,128)(2,1)S(1)} fusion(bf16[64,152,128]{2,1,0:T(8,128)(2,1)S(1)} %collective-permute-done.2, bf16[64,152,128]{2,1,0:T(8,128)(2,1)} %get-tuple-element.25), kind=kLoop, calls=%fused_computation | loop fusion | flops 4980736 | bytes 7471104 | tf_op jit(solution)/shard_map/convert_element_type | solution.py:477
  99.3 43.0 %all_to_all.15 = bf16[64,152,128]{2,1,0:T(8,128)(2,1)S(1)} all-to-all(bf16[64,152,128]{2,1,0:T(8,128)(2,1)S(1)} %add_convert_fusion), channel_id=1, replica_groups=mesh['z'=4,'x'=4,'y'=4,'core'=2] {'z','x','y'}, dimensions={0} | all-to-all | bytes 4980736 | tf_op jit(solution)/shard_map/all_to_all | solution.py:440
  142.4 0.4 reduce_sum.12
  142.7 0.3 broadcast_in_dim.42
  143.1 38.1 %all_to_all.16.kept_ref = bf16[64,152,128]{2,1,0:T(8,128)(2,1)S(1)} all-to-all(bf16[64,152,128]{2,1,0:T(8,128)(2,1)S(1)} %broadcast_in_dim.42), channel_id=1, replica_groups=mesh['z'=4,'x'=4,'y'=4,'core'=2] {'z','x','y'}, dimensions={0} | all-to-all | bytes 4980736 | tf_op jit(solution)/shard_map/all_to_all | solution.py:440
  181.2 0.0 copy-start
  181.2 2.9 %collective-permute-start.3 = (bf16[64,152,128]{2,1,0:T(8,128)(2,1)S(1)}, bf16[64,152,128]{2,1,0:T(8,128)(2,1)S(1)}, u32[]{:S(2)}, u32[]{:S(2)}) collective-permute-start(bf16[64,152,128]{2,1,0:T(8,128)(2,1)S(1)} %all_to_all.16.kept_ref), channel_id=1, source_target_pairs={{0,1},{1,0},{2,3},{3,2},{4,5},{5,4},{6,7},{7,6},{8,9},{9,8},{10,11... | collective-permute-start | bytes 7471112 | tf_op jit(solution)/shard_map/ppermute | solution.py:481
  184.1 4.3 %collective-permute-done.3.other_ref = bf16[64,152,128]{2,1,0:T(8,128)(2,1)S(1)} collective-permute-done((bf16[64,152,128]{2,1,0:T(8,128)(2,1)S(1)}, bf16[64,152,128]{2,1,0:T(8,128)(2,1)S(1)}, u32[]{:S(2)}, u32[]{:S(2)}) %collective-permute-start.3) | collective-permute-done | bytes 2490400 | tf_op jit(solution)/shard_map/ppermute | solution.py:481
  188.4 0.0 copy-start.1
  188.4 1.5 copy-done.1
  189.9 0.0 copy-done
  189.9 6.7 %spread.1 = (f32[1024,1024]{1,0:T(8,128)}, f32[1024,1024]{1,0:T(8,128)}, f32[32,1024]{1,0:T(8,128)}, f32[32,1024]{1,0:T(8,128)}, f32[1,1024]{1,0:T(1,128)}, /*index=5*/f32[1,1024]{1,0:T(1,128)}) custom-call(s32[1]{0:T(128)} %bitcast.core_ref, s32[1]{0:T(128)} %bitcast.9.z_ref, bf16[64,152,128]{2,1,0:T(8,128)(2,1)} %copy-done, bf16[64,152,128]{2,1,0:T(8,128)(2,1)} %copy-done.1), custom_call_target="tpu_custom_call" | custom-call | tf_op jit(solution)/shard_map/spread/pallas_call | solution.py:418
  (3 shorter events, 0.1 us)
Async XLA Ops:
  0.6 45.7 %copy-start.4 = (s32[512]{0:T(512)S(1)}, s32[512]{0:T(512)}, u32[]{:S(2)}) copy-start(s32[512]{0:T(512)} %param.25) | copy-start | bytes 6148
  0.6 46.6 %copy-start.3 = (s32[512,10]{0,1:T(8,128)S(1)}, s32[512,10]{0,1:T(8,128)}, u32[]{:S(2)}) copy-start(s32[512,10]{0,1:T(8,128)} %param.23) | copy-start | bytes 61444
  0.7 47.4 %copy-start.5 = (s32[512]{0:T(512)S(1)}, s32[512]{0:T(512)}, u32[]{:S(2)}) copy-start(s32[512]{0:T(512)} %param.24) | copy-start | bytes 6148
  2.4 33.3 %collective-permute-start = (bf16[64,1024]{1,0:T(8,128)(2,1)S(1)}, bf16[64,1024]{1,0:T(8,128)(2,1)S(1)}, u32[]{:S(2)}, u32[]{:S(2)}) collective-permute-start(bf16[64,1024]{1,0:T(8,128)(2,1)S(1)} %constant_dynamic-update-slice_fusion), channel_id=1, source_target_pairs={{0,32},{32,0},{64,96},{96,64},{1,33},{33,1},{65,97},{97,65},{2,34}... | collective-permute-start | bytes 393224 | tf_op jit(solution)/shard_map/ppermute | solution.py:428
  35.7 24.2 %collective-permute-start.1 = (bf16[128,1024]{1,0:T(8,128)(2,1)S(1)}, bf16[128,1024]{1,0:T(8,128)(2,1)S(1)}, u32[]{:S(2)}, u32[]{:S(2)}) collective-permute-start(bf16[128,1024]{1,0:T(8,128)(2,1)S(1)} %pad_maximum_fusion.1), channel_id=1, source_target_pairs={{0,96},{96,0},{32,64},{64,32},{1,97},{97,1},{33,65},{65,33},{2,98}... | collective-permute-start | bytes 786440 | tf_op jit(solution)/shard_map/ppermute | solution.py:434
  38.0 22.7 %all-to-all-start = ((bf16[128,16,128]{2,1,0:T(8,128)(2,1)}), bf16[128,16,128]{2,1,0:T(8,128)(2,1)S(1)}, u32[]{:S(2)}, u32[]{:S(2)}) async-start(bf16[128,16,128]{2,1,0:T(8,128)(2,1)} %aggregate.1), calls=%async_computation | async-start | bytes 1048576 | tf_op jit(solution)/shard_map/all_to_all | solution.py:440
  60.8 0.8 copy-start.2
  91.4 5.6 %collective-permute-start.2 = (bf16[64,152,128]{2,1,0:T(8,128)(2,1)}, bf16[64,152,128]{2,1,0:T(8,128)(2,1)S(1)}, u32[]{:S(2)}, u32[]{:S(2)}) collective-permute-start(bf16[64,152,128]{2,1,0:T(8,128)(2,1)} %get-tuple-element.26), channel_id=1, source_target_pairs={{0,1},{1,0},{2,3},{3,2},{4,5},{5,4},{6,7},{7,6},{8,9},{9,8},{10,11... | collective-permute-start | bytes 7471112 | tf_op jit(solution)/shard_map/ppermute | solution.py:476
  181.2 8.7 %copy-start = (bf16[64,152,128]{2,1,0:T(8,128)(2,1)}, bf16[64,152,128]{2,1,0:T(8,128)(2,1)S(1)}, u32[]{:S(2)}) copy-start(bf16[64,152,128]{2,1,0:T(8,128)(2,1)S(1)} %all_to_all.16.kept_ref) | copy-start | bytes 7471108
  181.2 7.2 %collective-permute-start.3 = (bf16[64,152,128]{2,1,0:T(8,128)(2,1)S(1)}, bf16[64,152,128]{2,1,0:T(8,128)(2,1)S(1)}, u32[]{:S(2)}, u32[]{:S(2)}) collective-permute-start(bf16[64,152,128]{2,1,0:T(8,128)(2,1)S(1)} %all_to_all.16.kept_ref), channel_id=1, source_target_pairs={{0,1},{1,0},{2,3},{3,2},{4,5},{5,4},{6,7},{7,6},{8,9},{9,8},{10,11... | collective-permute-start | bytes 7471112 | tf_op jit(solution)/shard_map/ppermute | solution.py:481
  188.4 1.5 copy-start.1

commit v3 on v2

--- a/solution.py
+++ b/solution.py
@@ -4,6 +4,7 @@
 from jax.experimental import pallas as pl
 from jax.experimental.pallas import tpu as pltpu
 from jax.sharding import Mesh, PartitionSpec as P
+
 
 CAP = 32
 LANES = 128
@@ -166,7 +167,7 @@
 
 
 def aggregate(features, adjacent, count, owner, owners):
-    width, inputs = features.shape
+    width, _ = features.shape
     nodes = owner.shape[1]
     return pl.pallas_call(
         aggregate_kernel,
@@ -181,6 +182,7 @@
             pltpu.VMEM((16 * owners, LANES), jnp.float32),
         ],
         name="aggregate",
+        compiler_params=pltpu.CompilerParams(vmem_limit_bytes=12 << 20),
         cost_estimate=pl.CostEstimate(flops=40_000_000, bytes_accessed=3_000_000, transcendentals=0),
     )(features, adjacent, count, owner)
 
@@ -232,16 +234,36 @@
         in_specs=[VMEM] * 3,
         out_specs=(VMEM, VMEM),
         name="picks",
+        compiler_params=pltpu.CompilerParams(vmem_limit_bytes=12 << 20),
         cost_estimate=pl.CostEstimate(flops=20_000_000, bytes_accessed=5_000_000, transcendentals=0),
     )(adjacent, center, count)
 
 
-def owner_kernel(
-    core_ref, arrived_ref, first_ref, bias_one_ref, picks_ref, flip_ref, count_ref, root_ref,
-    near_ref, bias_two_ref, upstream_ref, out_ref, kept_ref, sent_ref, inputs, inputs_flip,
-    hidden, rows, slope, back, bias_grads,
+def call(kernel, outs, ins, smem=0, scratch=(), limit=16, flops=0, moved=0, exps=0):
+    return pl.pallas_call(
+        kernel,
+        out_shape=outs,
+        in_specs=[SMEM] * smem + [VMEM] * (ins - smem),
+        out_specs=(VMEM,) * len(outs),
+        scratch_shapes=scratch,
+        compiler_params=pltpu.CompilerParams(vmem_limit_bytes=limit << 20),
+        cost_estimate=pl.CostEstimate(flops=flops, bytes_accessed=moved, transcendentals=exps),
+    )
+
+
+def put_chunks(to_ref, t, product):
+    for c in range(product.shape[0] // 16):
+        for lane in range(product.shape[1] // LANES):
+            to_ref[t * (product.shape[0] // 16) + c, lane * 16 : (lane + 1) * 16, :] = product[
+                c * 16 : (c + 1) * 16, lane * LANES : (lane + 1) * LANES
+            ]
+
+
+def forward_kernel(
+    core_ref, arrived_ref, first_ref, bias_one_ref, picks_ref, count_ref, root_ref, near_ref,
+    bias_two_ref, upstream_ref, out_ref, sent_ref, hidden, rows, slope, inputs_flip, bias_grad,
+    inputs,
 ):
-    core = core_ref[0]
     slots, depth = inputs.shape
     hidden_width = hidden.shape[1]
     nodes = slope.shape[0]
@@ -290,30 +312,59 @@
         grad = upstream_ref[:, cols].astype(jnp.float32) * gate * (1.0 + pre * (1.0 - gate))
         grad = grad.astype(jnp.bfloat16)
         slope[:, cols] = grad
-        bias_grads[0:1, cols] = jnp.sum(grad.astype(jnp.float32), axis=0, keepdims=True)
+        bias_grad[0:1, cols] = jnp.sum(grad.astype(jnp.float32), axis=0, keepdims=True)
         return carry
 
     lax.fori_loop(0, hidden_width // tile, second_layer, 0)
-
-    for place, to_ref in enumerate((kept_ref, sent_ref)):
-        which = core ^ place
-
-        def weight_grads(t, carry, to_ref=to_ref, which=which):
-            left = rows[pl.ds(pl.multiple_of(which * nodes, nodes), nodes), lanes_at(t, tile)]
-            product = across(left, slope[...]).astype(jnp.bfloat16)
-            for c in range(tile // 16):
-                for lane in range(hidden_width // LANES):
-                    to_ref[t * (tile // 16) + c, lane * 16 : (lane + 1) * 16, :] = product[
-                        c * 16 : (c + 1) * 16, lane * LANES : (lane + 1) * LANES
-                    ]
-            return carry
-
-        lax.fori_loop(0, hidden_width // tile, weight_grads, 0)
+    start = (core_ref[0] ^ 1) * nodes
+
+    def weight_grads(t, carry):
+        left = rows[pl.ds(pl.multiple_of(start, nodes), nodes), lanes_at(t, tile)]
+        put_chunks(sent_ref, t, across(left, slope[...]).astype(jnp.bfloat16))
+        return carry
+
+    lax.fori_loop(0, hidden_width // tile, weight_grads, 0)
+
+
+def kept_kernel(
+    core_ref, rows_ref, slope_ref, received_ref, kept_one_ref, received_one_ref, both_ref
+):
+    nodes, hidden_width = slope_ref.shape
+    tile = 256
+    start = core_ref[0] * nodes
+
+    def weight_grads(t, carry):
+        left = rows_ref[pl.ds(pl.multiple_of(start, nodes), nodes), lanes_at(t, tile)]
+        product = across(left, slope_ref[...])
+        for c in range(tile // 16):
+            chunk = t * (tile // 16) + c
+            for lane in range(hidden_width // LANES):
+                at = slice(lane * 16, (lane + 1) * 16)
+                mine = product[c * 16 : (c + 1) * 16, lane * LANES : (lane + 1) * LANES]
+                other = received_ref[chunk, at, :].astype(jnp.float32)
+                both_ref[chunk, at, :] = (mine + other).astype(jnp.bfloat16)
+            mine = kept_one_ref[chunk].astype(jnp.float32)
+            other = received_one_ref[chunk].astype(jnp.float32)
+            both_ref[chunk, LANES:, :] = (mine + other).astype(jnp.bfloat16)
+        return carry
+
+    lax.fori_loop(0, hidden_width // tile, weight_grads, 0)
+
+
+def backward_kernel(
+    core_ref, slope_ref, root_ref, near_ref, count_ref, flip_ref, hidden_ref, inputs_flip_ref,
+    bias_two_ref, kept_ref, sent_ref, back, bias_grads,
+):
+    core = core_ref[0]
+    nodes, hidden_width = slope_ref.shape
+    tile = 256
+    bias_grads[0:1, :] = bias_two_ref[0:1, :]
+    inverse = 1.0 / count_ref[...].astype(jnp.float32)
 
     def backward(t, carry):
         cols = lanes_at(t, tile)
-        back[:nodes, cols] = along(slope[...], root_ref[cols, :]).astype(jnp.bfloat16)
-        near = along(slope[...], near_ref[cols, :])
+        back[:nodes, cols] = along(slope_ref[...], root_ref[cols, :]).astype(jnp.bfloat16)
+        near = along(slope_ref[...], near_ref[cols, :])
         back[nodes:, cols] = (near * inverse).astype(jnp.bfloat16)
         return carry
 
@@ -322,17 +373,17 @@
     def first_grads(t, carry):
         cols = lanes_at(t, tile)
         table_grad = matmul(flip_ref[...], back[:, cols])
-        grad = table_grad * (1.0 - jnp.exp(-hidden[:, cols].astype(jnp.float32)))
+        grad = table_grad * (1.0 - jnp.exp(-hidden_ref[:, cols].astype(jnp.float32)))
         grad = grad.astype(jnp.bfloat16)
         bias_grads[1:2, cols] = jnp.sum(grad.astype(jnp.float32), axis=0, keepdims=True)
         for place, to_ref in enumerate((kept_ref, sent_ref)):
             which = core ^ place
-            left = inputs_flip[pl.ds(pl.multiple_of(which * LANES, LANES), LANES), :]
+            left = inputs_flip_ref[pl.ds(pl.multiple_of(which * LANES, LANES), LANES), :]
             product = matmul(left, grad).astype(jnp.bfloat16)
             for c in range(8):
                 for lane in range(tile // LANES):
                     chunk = c * 8 + t * (tile // LANES) + lane
-                    to_ref[chunk, LANES : LANES + 16, :] = product[
+                    to_ref[chunk, 0:16, :] = product[
                         c * 16 : (c + 1) * 16, lane * LANES : (lane + 1) * LANES
                     ]
         return carry
@@ -340,87 +391,73 @@
     lax.fori_loop(0, hidden_width // tile, first_grads, 0)
     for place, to_ref in enumerate((kept_ref, sent_ref)):
         which = core ^ place
-        to_ref[:, LANES + 16 :, :] = jnp.zeros((to_ref.shape[0], 8, LANES), jnp.bfloat16)
+        to_ref[:, 16:, :] = jnp.zeros((to_ref.shape[0], 8, LANES), jnp.bfloat16)
         for lane in range(8):
             cols = slice(lane * LANES, (lane + 1) * LANES)
             row = jnp.where(which == 0, bias_grads[0:1, cols], bias_grads[1:2, cols])
-            to_ref[lane, LANES + 16 :, :] = jnp.broadcast_to(row, (8, LANES)).astype(jnp.bfloat16)
-
-
-def owner_step(
-    core, arrived, first, bias_one, picked, flipped, count, root, near, bias_two, upstream
-):
-    nodes, hidden_width = upstream.shape
-    slots = picked.shape[1]
-    depth = first.shape[0]
-    bf16, f32 = jnp.bfloat16, jnp.float32
-    share = jax.ShapeDtypeStruct((64, CHUNK, LANES), bf16)
-    return pl.pallas_call(
-        owner_kernel,
-        out_shape=(jax.ShapeDtypeStruct((nodes, hidden_width), bf16), share, share),
-        in_specs=[SMEM] + [VMEM] * 10,
-        out_specs=(VMEM, VMEM, VMEM),
-        scratch_shapes=[
-            pltpu.VMEM((slots, depth), bf16),
-            pltpu.VMEM((depth, slots), bf16),
-            pltpu.VMEM((slots, hidden_width), bf16),
-            pltpu.VMEM((2 * nodes, hidden_width), bf16),
-            pltpu.VMEM((nodes, hidden_width), bf16),
-            pltpu.VMEM((2 * nodes, hidden_width), bf16),
-            pltpu.VMEM((8, hidden_width), f32),
-        ],
-        name="owner_step",
-        cost_estimate=pl.CostEstimate(
-            flops=12_000_000_000, bytes_accessed=18_000_000, transcendentals=3_000_000
-        ),
-    )(core, arrived, first, bias_one, picked, flipped, count, root, near, bias_two, upstream)
+            to_ref[lane, 16:, :] = jnp.broadcast_to(row, (8, LANES)).astype(jnp.bfloat16)
+
+
+def shaped(*shape, dtype=jnp.bfloat16):
+    return jax.ShapeDtypeStruct(shape, dtype)
 
 
 def spread_kernel(core_ref, z_ref, kept_ref, other_ref, root_ref, near_ref, first_root_ref, first_near_ref, bias_two_ref, bias_one_ref):
-    even = core_ref[0] == 0
-    z = z_ref[0]
-
-    def one_chunk(c, carry):
-        at = pl.ds(pl.multiple_of(c * 16, 16), 16)
+    core, z = core_ref[0], z_ref[0]
+    step = pl.program_id(0)
+    even = core == 0
+    for c in range(8):
         for lane in range(8):
             kept = kept_ref[c, lane * 16 : (lane + 1) * 16, :].astype(jnp.float32)
             other = other_ref[c, lane * 16 : (lane + 1) * 16, :].astype(jnp.float32)
-            cols = slice(lane * LANES, (lane + 1) * LANES)
+            at, cols = slice(c * 16, (c + 1) * 16), slice(lane * LANES, (lane + 1) * LANES)
             root_ref[at, cols] = jnp.where(even, kept, other)
             near_ref[at, cols] = jnp.where(even, other, kept)
-        return carry
-
-    lax.fori_loop(0, 64, one_chunk, 0)
-    here = lax.shift_right_logical(z, 1) == core_ref[0]
+
+    here = lax.shift_right_logical(z, 1) == core
     base = lax.bitwise_and(z, 1) * 4
     for j, to_ref in enumerate((first_root_ref, first_near_ref)):
         for i in range(2):
-            for lane in range(8):
-                chunk = (base + 2 * j + i) * 8 + lane
-                kept = kept_ref[chunk, LANES : LANES + 16, :].astype(jnp.float32)
-                other = other_ref[chunk, LANES : LANES + 16, :].astype(jnp.float32)
-                to_ref[i * 16 : (i + 1) * 16, lane * LANES : (lane + 1) * LANES] = jnp.where(
-                    here, kept, other
-                )
-    for lane in range(8):
-        kept = kept_ref[lane, LANES + 16 :, :].astype(jnp.float32)[0:1, :]
-        other = other_ref[lane, LANES + 16 :, :].astype(jnp.float32)[0:1, :]
-        cols = slice(lane * LANES, (lane + 1) * LANES)
-        bias_two_ref[:, cols] = jnp.where(even, kept, other)
-        bias_one_ref[:, cols] = jnp.where(even, other, kept)
+
+            @pl.when(step == base + 2 * j + i)
+            def _(to_ref=to_ref, i=i):
+                for lane in range(8):
+                    kept = kept_ref[lane, LANES : LANES + 16, :].astype(jnp.float32)
+                    other = other_ref[lane, LANES : LANES + 16, :].astype(jnp.float32)
+                    at, cols = slice(i * 16, (i + 1) * 16), slice(lane * LANES, (lane + 1) * LANES)
+                    to_ref[at, cols] = jnp.where(here, kept, other)
+
+    @pl.when(step == 0)
+    def _():
+        for lane in range(8):
+            kept = kept_ref[lane, LANES + 16 :, :].astype(jnp.float32)[0:1, :]
+            other = other_ref[lane, LANES + 16 :, :].astype(jnp.float32)[0:1, :]
+            cols = slice(lane * LANES, (lane + 1) * LANES)
+            bias_two_ref[:, cols] = jnp.where(even, kept, other)
+            bias_one_ref[:, cols] = jnp.where(even, other, kept)
 
 
 def spread(core, z, kept, other, hidden_width):
     f32 = jnp.float32
-    square = jax.ShapeDtypeStruct((hidden_width, hidden_width), f32)
-    slab = jax.ShapeDtypeStruct((32, hidden_width), f32)
-    line = jax.ShapeDtypeStruct((1, hidden_width), f32)
+    wide = pl.BlockSpec((LANES, hidden_width), lambda s: (s, 0))
+    slab = pl.BlockSpec((32, hidden_width), lambda s: (0, 0))
+    line = pl.BlockSpec((1, hidden_width), lambda s: (0, 0))
+    block = pl.BlockSpec((8, CHUNK, LANES), lambda s: (s, 0, 0))
     return pl.pallas_call(
         spread_kernel,
-        out_shape=(square, square, slab, slab, line, line),
-        in_specs=[SMEM, SMEM, VMEM, VMEM],
-        out_specs=(VMEM,) * 6,
+        grid=(8,),
+        out_shape=(
+            shaped(hidden_width, hidden_width, dtype=f32),
+            shaped(hidden_width, hidden_width, dtype=f32),
+            shaped(32, hidden_width, dtype=f32),
+            shaped(32, hidden_width, dtype=f32),
+            shaped(1, hidden_width, dtype=f32),
+            shaped(1, hidden_width, dtype=f32),
+        ),
+        in_specs=[SMEM, SMEM, block, block],
+        out_specs=(wide, wide, slab, slab, line, line),
         name="spread",
+        compiler_params=pltpu.CompilerParams(vmem_limit_bytes=16 << 20),
     )(core, z, kept, other)
 
 
@@ -440,7 +477,7 @@
     return lax.all_to_all(value, axes, split_axis=0, concat_axis=0, tiled=True)
 
 
-def local(
+def step(
     features,
     first_adjacent,
     first_center,
@@ -469,12 +506,44 @@
     arrived = exchange(packed, AXES)
     count = second_count[:, None]
     picked, flipped = picks(second_adjacent, second_center[:, None], count, owners * 8)
-    layer_output, kept, sent = owner_step(
-        core, arrived, first_all, first_bias[None], picked, flipped, count, second_root,
-        second_near, second_bias[None], upstream,
-    )
-    received = lax.ppermute(sent, "core", [(0, 1), (1, 0)])
-    both = (kept.astype(jnp.float32) + received.astype(jnp.float32)).astype(jnp.bfloat16)
+    slots, depth = picked.shape[1], first_all.shape[0]
+    nodes = upstream.shape[0]
+    layer_output, sent_two, hidden, rows, slope, inputs_flip, bias_grad = call(
+        forward_kernel,
+        (
+            shaped(nodes, hidden_width),
+            shaped(64, LANES, LANES),
+            shaped(slots, hidden_width),
+            shaped(2 * nodes, hidden_width),
+            shaped(nodes, hidden_width),
+            shaped(depth, slots),
+            shaped(8, hidden_width, dtype=jnp.float32),
+        ),
+        10,
+        smem=1,
+        scratch=[pltpu.VMEM((slots, depth), jnp.bfloat16)],
+        limit=28,
+        flops=6_000_000_000,
+        moved=18_000_000,
+        exps=3_000_000,
+    )(
+        core, arrived, first_all, first_bias[None], picked, count, second_root, second_near,
+        second_bias[None], upstream,
+    )
+    received = lax.ppermute(sent_two, "core", [(0, 1), (1, 0)])
+    kept_one, sent_one = call(
+        backward_kernel, (shaped(64, 24, LANES), shaped(64, 24, LANES)), 9, smem=1,
+        scratch=[
+            pltpu.VMEM((2 * nodes, hidden_width), jnp.bfloat16),
+            pltpu.VMEM((8, hidden_width), jnp.float32),
+        ],
+        limit=24, flops=4_700_000_000, moved=12_000_000, exps=1_000_000,
+    )(core, slope, second_root, second_near, count, flipped, hidden, inputs_flip, bias_grad)
+    received_one = lax.ppermute(sent_one, "core", [(0, 1), (1, 0)])
+    (both,) = call(
+        kept_kernel, (shaped(64, CHUNK, LANES),), 6, smem=1, limit=20,
+        flops=1_000_000_000, moved=7_000_000,
+    )(core, rows, slope, received, kept_one, received_one)
     terms = exchange(both, CHIPS)
     total = jnp.sum(terms.astype(jnp.float32), axis=0).astype(jnp.bfloat16)
     mine = exchange(jnp.broadcast_to(total[None], terms.shape), CHIPS)
@@ -489,7 +558,7 @@
     chips = Mesh(mesh.devices.reshape(4, 4, 4, 2), AXES)
     trainer = ("x", "y", "core")
     return jax.shard_map(
-        local,
+        step,
         mesh=chips,
         in_specs=(
             P("z", trainer),

time: 197 us -> 186 us (0.944)
  Pallas kernels: 76.6 us -> 64.9 us
  local copies, waits for them, and re-layouts: 6.93 us -> 11.9 us
  other arithmetic: 5.22 us -> 3.15 us
    pallas_call x2 -> x4, Pallas kernels: 36.4 us -> 28.7 us  [the longest x1 14.4 us: step(): call(forward_kernel, (shaped(nodes, hidden_width), shaped(64, LANES, LANE...]
    unnamed x14 -> x34, local copies, waits for them, and re-layouts: 4.03 us -> 10.4 us
    pallas_call x1, Pallas kernels: 11 us -> 8.03 us  [picks(): pl.pallas_call(picks_kernel, out_shape=(jax.ShapeDtypeStruct((2 * nodes,...]
    ppermute x2 -> x3, waiting for transfers between devices: 8.91 us -> 6.06 us  [the longest x1 4.35 us: step(): other = lax.ppermute(mine, 'core', [(0, 1), (1, 0)])]
    convert_element_type x1 -> x0, other arithmetic: 2.35 us -> none  [local(): (kept.astype(jnp.float32) + received.astype(jnp.float32)).astype(jnp.bflo...]
  transfers between devices with their start and end apart: 5 -> 6, of which waited for: 2 -> 3; matrix products, arithmetic and copies ran while one was open for 3% -> 1% of each run, Pallas kernels for 20% -> 24%
where the time goes in v3:
time: 186 us; the launch traced here: 185 us
  blocking collectives  80.2 us (43%)
  Pallas kernels  64.9 us (35%)
  starting transfers between devices  16.8 us (9%)
  local copies, waits for them, and re-layouts  11.9 us (6%)
  waiting for transfers between devices  7.3 us (4%)
  other arithmetic  3.15 us (2%)
    all_to_all x2, blocking collectives, exchange(): return lax.all_to_all(value, axes, split_axis=0, concat_axis=0, tiled=True)  80.2 us
    pallas_call x1, Pallas kernels, aggregate(): pl.pallas_call(aggregate_kernel, out_shape=jax.ShapeDtypeStruct((owners,...  28.1 us
    pallas_call x1, Pallas kernels, step(): call(forward_kernel, (shaped(nodes, hidden_width), shaped(64, LANES, LANE...  14.4 us
    unnamed x34, local copies, waits for them, and re-layouts  10.4 us
    all_to_all x1, starting transfers between devices, exchange(): return lax.all_to_all(value, axes, split_axis=0, concat_axis=0, tiled=True)  8.25 us
    pallas_call x1, Pallas kernels, picks(): pl.pallas_call(picks_kernel, out_shape=(jax.ShapeDtypeStruct((2 * nodes,...  8.03 us
    pallas_call x1, Pallas kernels, step(): call(backward_kernel, (shaped(64, 24, LANES), shaped(64, 24, LANES)), 9,...  7.73 us
    pallas_call x1, Pallas kernels, spread(): pl.pallas_call(spread_kernel, grid=(8,), out_shape=(shaped(hidden_width,...  4.62 us
  transfers between devices with their start and end apart: 6, of which 3 were waited for; matrix products, arithmetic and copies ran while one was open for 1% of the time, Pallas kernels for 24%

profile of v3, /device:TPU:1, one launch (start us, length us, event | category | flops | bytes accessed | tf_op | source)
XLA Modules:
  0.0 185.0 jit_solution(623578697576213837)
XLA Ops:
  0.6 0.0 copy-start.14
  0.6 0.0 copy-start.13
  0.7 0.0 copy-start.15
  0.7 0.9 constant_dynamic-update-slice_fusion.1
  1.5 0.8 constant_dynamic-update-slice_fusion
  2.4 2.5 %collective-permute-start = (bf16[64,1024]{1,0:T(8,128)(2,1)S(1)}, bf16[64,1024]{1,0:T(8,128)(2,1)S(1)}, u32[]{:S(2)}, u32[]{:S(2)}) collective-permute-start(bf16[64,1024]{1,0:T(8,128)(2,1)S(1)} %constant_dynamic-update-slice_fusion), channel_id=1, source_target_pairs={{0,32},{32,0},{64,96},{96,64},{1,33},{33,1},{65,97},{97,65},{2,34}... | collective-permute-start | bytes 393224 | tf_op jit(solution)/shard_map/ppermute | solution.py:465
  4.8 0.9 add_bitcast_fusion.adj_ref
  5.8 0.0 copy-start
  5.8 0.9 copy-done
  6.7 0.0 copy-start.1
  6.7 0.7 copy-done.1
  7.4 0.0 copy-start.2
  7.4 0.7 copy-done.2
  8.1 28.1 %aggregate.1 = bf16[128,16,128]{2,1,0:T(8,128)(2,1)} custom-call(bf16[32,4096]{1,0:T(8,128)(2,1)S(1)} %copy-done, s32[16,2048]{1,0:T(8,128)S(1)} %add_bitcast_fusion.adj_ref, s32[1,2048]{1,0:T(1,128)S(1)} %bitcast.13, s32[1,2048]{1,0:T(1,128)S(1)} %bitcast.14), custom_call_target="tpu_custom_call" | custom-call | flops 40000000 | bytes 3000000 | tf_op jit(solution)/shard_map/aggregate/pallas_call | solution.py:172
  36.2 0.0 collective-permute-done
  36.3 0.7 pad_maximum_fusion.1
  37.0 2.2 %collective-permute-start.1 = (bf16[128,1024]{1,0:T(8,128)(2,1)}, bf16[128,1024]{1,0:T(8,128)(2,1)}, u32[]{:S(2)}, u32[]{:S(2)}) collective-permute-start(bf16[128,1024]{1,0:T(8,128)(2,1)} %pad_maximum_fusion.1), channel_id=1, source_target_pairs={{0,96},{96,0},{32,64},{64,32},{1,97},{97,1},{33,65},{65,33},{2,98}... | collective-permute-start | bytes 786440 | tf_op jit(solution)/shard_map/ppermute | solution.py:471
  39.2 8.3 %all-to-all-start = ((bf16[128,16,128]{2,1,0:T(8,128)(2,1)}), bf16[128,16,128]{2,1,0:T(8,128)(2,1)S(1)}, u32[]{:S(2)}, u32[]{:S(2)}) async-start(bf16[128,16,128]{2,1,0:T(8,128)(2,1)} %aggregate.1), calls=%async_computation | async-start | bytes 1048576 | tf_op jit(solution)/shard_map/all_to_all | solution.py:477
  47.5 0.0 copy-start.3
  47.5 0.0 copy-start.11
  47.5 0.0 copy-start.12
  47.5 0.0 copy-done.14
  47.6 0.1 copy.25.count_ref
  47.7 0.0 copy-done.13
  47.7 0.1 copy.23.adj_ref
  47.9 0.0 copy-done.15
  47.9 0.1 copy.24.center_ref
  48.0 8.0 %picks.1 = (bf16[1024,1024]{1,0:T(8,128)(2,1)S(1)}, bf16[1024,1024]{1,0:T(8,128)(2,1)S(1)}) custom-call(s32[512,10]{1,0:T(8,128)S(1)} %copy.23.adj_ref, s32[512,1]{1,0:T(8,128)S(1)} %copy.24.center_ref, s32[512,1]{1,0:T(8,128)S(1)} %copy.25.count_ref), custom_call_target="tpu_custom_call" | custom-call | flops 20000000 | bytes 5000000 | tf_op jit(solution)/shard_map/picks/pallas_call | solution.py:228
  56.1 0.0 copy-start.6
  56.1 1.3 copy-done.6
  57.4 0.0 copy-start.8
  57.4 1.3 copy-done.8
  58.7 0.0 collective-permute-done.1
  58.7 1.1 broadcast_select_fusion.1
  59.8 1.2 all-to-all-done.arrived_ref
  61.0 0.0 copy-done.3
  61.1 0.0 copy-done.11
  61.1 0.0 copy-done.12
  61.1 0.0 copy-start.4
  61.1 1.6 copy-done.4
  62.7 0.0 copy-start.9
  62.7 1.6 copy-done.9
  64.2 0.0 copy-start.10
  64.2 1.2 copy-done.10
  65.5 0.0 copy-start.5
  65.5 0.0 copy-start.7
  65.5 14.4 %shard_map.198 = (bf16[512,1024]{1,0:T(8,128)(2,1)}, bf16[64,128,128]{2,1,0:T(8,128)(2,1)S(1)}, bf16[1024,1024]{1,0:T(8,128)(2,1)S(1)}, bf16[1024,1024]{1,0:T(8,...) custom-call(s32[1]{0:T(128)} %bitcast.core_ref, ...), custom_call_target="tpu_custom_call" | custom-call | flops 6000000000 | bytes 18000000 | tf_op jit(solution)/shard_map/pallas_call | solution.py:511
  79.9 1.0 collective-permute-start.2
  80.9 0.0 copy-done.5
  80.9 0.0 copy-done.7
  80.9 7.7 %shard_map.199 = (bf16[64,24,128]{2,1,0:T(8,128)(2,1)S(1)}, bf16[64,24,128]{2,1,0:T(8,128)(2,1)S(1)}) custom-call(s32[1]{0:T(128)} %bitcast.core_ref, bf16[512,1024]{1,0:T(8,128)(2,1)S(1)} %get-tuple-element.31.slope_ref, bf16[1024,1024]{1,0:T(8,128)(2,1)S(1)} %copy-done.3, bf16[1024,1024]{1,0:T(8,128)(2,1)S(1)} %copy-done.5, s32[512,1]{1,0:T(8,128)S(1)} %copy.25.count_ref, ...), custom_call_target="tpu_custom_call" | custom-call | flops 4700000256 | bytes 12000000 | tf_op jit(solution)/shard_map/pallas_call | solution.py:534
  88.6 0.1 collective-permute-start.3
  88.7 1.7 collective-permute-done.3.received_one_ref
  90.4 0.0 collective-permute-done.2.received_ref
  90.4 2.0 %shard_map.200 = bf16[64,152,128]{2,1,0:T(8,128)(2,1)S(1)} custom-call(s32[1]{0:T(128)} %bitcast.core_ref, bf16[1024,1024]{1,0:T(8,128)(2,1)S(1)} %get-tuple-element.30.rows_ref, bf16[512,1024]{1,0:T(8,128)(2,1)S(1)} %get-tuple-element.31.slope_ref, bf16[64,128,128]{2,1,0:T(8,128)(2,1)S(1)} %collective-permute-done.2.received_ref, ...), custom_call_target="tpu_custom_call" | custom-call | flops 1000000000 | bytes 7000000 | tf_op jit(solution)/shard_map/pallas_call | solution.py:543
  92.4 42.2 %all_to_all.15 = bf16[64,152,128]{2,1,0:T(8,128)(2,1)S(1)} all-to-all(bf16[64,152,128]{2,1,0:T(8,128)(2,1)S(1)} %shard_map.200), channel_id=1, replica_groups=mesh['z'=4,'x'=4,'y'=4,'core'=2] {'z','x','y'}, dimensions={0} | all-to-all | bytes 4980736 | tf_op jit(solution)/shard_map/all_to_all | solution.py:477
  134.6 0.4 reduce_sum.12
  134.9 0.3 broadcast_in_dim.42
  135.2 38.0 %all_to_all.16.kept_ref = bf16[64,152,128]{2,1,0:T(8,128)(2,1)S(1)} all-to-all(bf16[64,152,128]{2,1,0:T(8,128)(2,1)S(1)} %broadcast_in_dim.42), channel_id=1, replica_groups=mesh['z'=4,'x'=4,'y'=4,'core'=2] {'z','x','y'}, dimensions={0} | all-to-all | bytes 4980736 | tf_op jit(solution)/shard_map/all_to_all | solution.py:477
  173.2 2.8 %collective-permute-start.4 = (bf16[64,152,128]{2,1,0:T(8,128)(2,1)S(1)}, bf16[64,152,128]{2,1,0:T(8,128)(2,1)S(1)}, u32[]{:S(2)}, u32[]{:S(2)}) collective-permute-start(bf16[64,152,128]{2,1,0:T(8,128)(2,1)S(1)} %all_to_all.16.kept_ref), channel_id=1, source_target_pairs={{0,1},{1,0},{2,3},{3,2},{4,5},{5,4},{6,7},{7,6},{8,9},{9,8},{10,11... | collective-permute-start | bytes 7471112 | tf_op jit(solution)/shard_map/ppermute | solution.py:550
  176.0 4.3 %collective-permute-done.4.other_ref = bf16[64,152,128]{2,1,0:T(8,128)(2,1)S(1)} collective-permute-done((bf16[64,152,128]{2,1,0:T(8,128)(2,1)S(1)}, bf16[64,152,128]{2,1,0:T(8,128)(2,1)S(1)}, u32[]{:S(2)}, u32[]{:S(2)}) %collective-permute-start.4) | collective-permute-done | bytes 2490400 | tf_op jit(solution)/shard_map/ppermute | solution.py:550
  180.4 4.6 %spread.1 = (f32[1024,1024]{1,0:T(8,128)}, f32[1024,1024]{1,0:T(8,128)}, f32[32,1024]{1,0:T(8,128)}, f32[32,1024]{1,0:T(8,128)}, f32[1,1024]{1,0:T(1,128)}, /*index=5*/f32[1,1024]{1,0:T(1,128)}) custom-call(s32[1]{0:T(128)} %bitcast.core_ref, s32[1]{0:T(128)} %bitcast.9.z_ref, bf16[64,152,128]{2,1,0:T(8,128)(2,1)S(1)} %all_to_all.16.kept_ref, ...), custom_call_target="tpu_custom_call" | custom-call | tf_op jit(solution)/shard_map/spread/pallas_call | solution.py:446
  (2 shorter events, 0.1 us)
Async XLA Ops:
  0.6 46.9 %copy-start.14 = (s32[512]{0:T(512)S(1)}, s32[512]{0:T(512)}, u32[]{:S(2)}) copy-start(s32[512]{0:T(512)} %param.25) | copy-start | bytes 6148
  0.6 47.1 %copy-start.13 = (s32[512,10]{0,1:T(8,128)S(1)}, s32[512,10]{0,1:T(8,128)}, u32[]{:S(2)}) copy-start(s32[512,10]{0,1:T(8,128)} %param.23) | copy-start | bytes 61444
  0.7 47.2 %copy-start.15 = (s32[512]{0:T(512)S(1)}, s32[512]{0:T(512)}, u32[]{:S(2)}) copy-start(s32[512]{0:T(512)} %param.24) | copy-start | bytes 6148
  2.4 33.9 %collective-permute-start = (bf16[64,1024]{1,0:T(8,128)(2,1)S(1)}, bf16[64,1024]{1,0:T(8,128)(2,1)S(1)}, u32[]{:S(2)}, u32[]{:S(2)}) collective-permute-start(bf16[64,1024]{1,0:T(8,128)(2,1)S(1)} %constant_dynamic-update-slice_fusion), channel_id=1, source_target_pairs={{0,32},{32,0},{64,96},{96,64},{1,33},{33,1},{65,97},{97,65},{2,34}... | collective-permute-start | bytes 393224 | tf_op jit(solution)/shard_map/ppermute | solution.py:465
  5.8 1.0 copy-start
  6.7 0.7 copy-start.1
  7.4 0.7 copy-start.2
  37.0 21.7 %collective-permute-start.1 = (bf16[128,1024]{1,0:T(8,128)(2,1)}, bf16[128,1024]{1,0:T(8,128)(2,1)}, u32[]{:S(2)}, u32[]{:S(2)}) collective-permute-start(bf16[128,1024]{1,0:T(8,128)(2,1)} %pad_maximum_fusion.1), channel_id=1, source_target_pairs={{0,96},{96,0},{32,64},{64,32},{1,97},{97,1},{33,65},{65,33},{2,98}... | collective-permute-start | bytes 786440 | tf_op jit(solution)/shard_map/ppermute | solution.py:471
  39.2 21.8 %all-to-all-start = ((bf16[128,16,128]{2,1,0:T(8,128)(2,1)}), bf16[128,16,128]{2,1,0:T(8,128)(2,1)S(1)}, u32[]{:S(2)}, u32[]{:S(2)}) async-start(bf16[128,16,128]{2,1,0:T(8,128)(2,1)} %aggregate.1), calls=%async_computation | async-start | bytes 1048576 | tf_op jit(solution)/shard_map/all_to_all | solution.py:477
  47.5 13.6 %copy-start.3 = (bf16[1024,1024]{1,0:T(8,128)(2,1)S(1)}, bf16[1024,1024]{1,0:T(8,128)(2,1)}, u32[]{:S(2)}) copy-start(bf16[1024,1024]{1,0:T(8,128)(2,1)} %root_ref.3) | copy-start | bytes 6291460
  47.5 13.5 %copy-start.11 = (f32[1024]{0:T(1024)S(1)}, f32[1024]{0:T(1024)}, u32[]{:S(2)}) copy-start(f32[1024]{0:T(1024)} %param.22) | copy-start | bytes 12292
  47.5 13.5 %copy-start.12 = (f32[1024]{0:T(1024)S(1)}, f32[1024]{0:T(1024)}, u32[]{:S(2)}) copy-start(f32[1024]{0:T(1024)} %param.28) | copy-start | bytes 12292
  56.1 1.3 copy-start.6
  57.4 1.3 copy-start.8
  61.1 1.6 copy-start.4
  62.7 1.6 copy-start.9
  64.2 1.2 copy-start.10
  65.5 15.4 %copy-start.5 = (bf16[1024,1024]{1,0:T(8,128)(2,1)S(1)}, bf16[1024,1024]{1,0:T(8,128)(2,1)}, u32[]{:S(2)}) copy-start(bf16[1024,1024]{1,0:T(8,128)(2,1)} %near_ref.3) | copy-start | bytes 6291460
  65.5 15.4 %copy-start.7 = (bf16[1024,1024]{1,0:T(8,128)(2,1)S(1)}, bf16[1024,1024]{1,0:T(8,128)(2,1)}, u32[]{:S(2)}) copy-start(bf16[1024,1024]{1,0:T(8,128)(2,1)} %copy-done.6) | copy-start | bytes 6291460
  79.9 10.6 %collective-permute-start.2 = (bf16[64,128,128]{2,1,0:T(8,128)(2,1)S(1)}, bf16[64,128,128]{2,1,0:T(8,128)(2,1)S(1)}, u32[]{:S(2)}, u32[]{:S(2)}) collective-permute-start(bf16[64,128,128]{2,1,0:T(8,128)(2,1)S(1)} %get-tuple-element.32), channel_id=1, source_target_pairs={{0,1},{1,0},{2,3},{3,2},{4,5},{5,4},{6,7},{7,6},{8,9},{9,8},{10,11... | collective-permute-start | bytes 6291464 | tf_op jit(solution)/shard_map/ppermute | solution.py:533
  88.6 1.8 collective-permute-start.3
  173.2 7.2 %collective-permute-start.4 = (bf16[64,152,128]{2,1,0:T(8,128)(2,1)S(1)}, bf16[64,152,128]{2,1,0:T(8,128)(2,1)S(1)}, u32[]{:S(2)}, u32[]{:S(2)}) collective-permute-start(bf16[64,152,128]{2,1,0:T(8,128)(2,1)S(1)} %all_to_all.16.kept_ref), channel_id=1, source_target_pairs={{0,1},{1,0},{2,3},{3,2},{4,5},{5,4},{6,7},{7,6},{8,9},{9,8},{10,11... | collective-permute-start | bytes 7471112 | tf_op jit(solution)/shard_map/ppermute | solution.py:550

commit v4 on v3

--- a/solution.py
+++ b/solution.py
@@ -10,7 +10,6 @@
 LANES = 128
 AXES = ("z", "x", "y", "core")
 CHIPS = ("z", "x", "y")
-CHUNK = 152
 VMEM = pl.BlockSpec(memory_space=pltpu.VMEM)
 ALONG_LANES = lax.GatherDimensionNumbers(
     offset_dims=(),
@@ -260,7 +259,7 @@
 
 
 def forward_kernel(
-    core_ref, arrived_ref, first_ref, bias_one_ref, picks_ref, count_ref, root_ref, near_ref,
+    core_ref, z_ref, arrived_ref, pair_ref, other_pair_ref, bias_one_ref, picks_ref, count_ref, root_ref, near_ref,
     bias_two_ref, upstream_ref, out_ref, sent_ref, hidden, rows, slope, inputs_flip, bias_grad,
     inputs,
 ):
@@ -284,9 +283,14 @@
     for t in range(slots // tile):
         inputs_flip[:, t * tile : (t + 1) * tile] = inputs[t * tile : (t + 1) * tile, :].T
 
+    late = z_ref[0] >= 2
+
     def first_layer(t, carry):
         cols = lanes_at(t, tile)
-        pre = matmul(inputs[...], first_ref[:, cols]) + bias_one_ref[:, cols]
+        pair, other = pair_ref[:, cols], other_pair_ref[:, cols]
+        pre = matmul(inputs[:, : depth // 2], jnp.where(late, other, pair))
+        pre = pre + matmul(inputs[:, depth // 2 :], jnp.where(late, pair, other))
+        pre = pre + bias_one_ref[:, cols]
         value = jnp.maximum(pre, 0.0) + jnp.log1p(jnp.exp(-jnp.abs(pre)))
         hidden[:, cols] = value.astype(jnp.bfloat16)
         return carry
@@ -326,9 +330,7 @@
     lax.fori_loop(0, hidden_width // tile, weight_grads, 0)
 
 
-def kept_kernel(
-    core_ref, rows_ref, slope_ref, received_ref, kept_one_ref, received_one_ref, both_ref
-):
+def kept_kernel(core_ref, rows_ref, slope_ref, received_ref, both_ref):
     nodes, hidden_width = slope_ref.shape
     tile = 256
     start = core_ref[0] * nodes
@@ -343,69 +345,63 @@
                 mine = product[c * 16 : (c + 1) * 16, lane * LANES : (lane + 1) * LANES]
                 other = received_ref[chunk, at, :].astype(jnp.float32)
                 both_ref[chunk, at, :] = (mine + other).astype(jnp.bfloat16)
-            mine = kept_one_ref[chunk].astype(jnp.float32)
-            other = received_one_ref[chunk].astype(jnp.float32)
-            both_ref[chunk, LANES:, :] = (mine + other).astype(jnp.bfloat16)
         return carry
 
     lax.fori_loop(0, hidden_width // tile, weight_grads, 0)
 
 
-def backward_kernel(
-    core_ref, slope_ref, root_ref, near_ref, count_ref, flip_ref, hidden_ref, inputs_flip_ref,
-    bias_two_ref, kept_ref, sent_ref, back, bias_grads,
-):
-    core = core_ref[0]
+def backward_kernel(slope_ref, root_ref, near_ref, count_ref, back_ref):
     nodes, hidden_width = slope_ref.shape
     tile = 256
-    bias_grads[0:1, :] = bias_two_ref[0:1, :]
     inverse = 1.0 / count_ref[...].astype(jnp.float32)
 
     def backward(t, carry):
         cols = lanes_at(t, tile)
-        back[:nodes, cols] = along(slope_ref[...], root_ref[cols, :]).astype(jnp.bfloat16)
+        back_ref[:nodes, cols] = along(slope_ref[...], root_ref[cols, :]).astype(jnp.bfloat16)
         near = along(slope_ref[...], near_ref[cols, :])
-        back[nodes:, cols] = (near * inverse).astype(jnp.bfloat16)
+        back_ref[nodes:, cols] = (near * inverse).astype(jnp.bfloat16)
         return carry
 
     lax.fori_loop(0, hidden_width // tile, backward, 0)
+
+
+def first_grads_kernel(
+    core_ref, z_ref, flip_ref, back_ref, hidden_ref, inputs_flip_ref, bias_two_ref, kept_ref,
+    sent_ref, grads, bias_grads,
+):
+    core, z = core_ref[0], z_ref[0]
+    hidden_width = hidden_ref.shape[1]
+    depth = inputs_flip_ref.shape[0]
+    tile = 256
+    bias_grads[0:1, :] = bias_two_ref[0:1, :]
 
     def first_grads(t, carry):
         cols = lanes_at(t, tile)
-        table_grad = matmul(flip_ref[...], back[:, cols])
+        table_grad = matmul(flip_ref[...], back_ref[:, cols])
         grad = table_grad * (1.0 - jnp.exp(-hidden_ref[:, cols].astype(jnp.float32)))
         grad = grad.astype(jnp.bfloat16)
         bias_grads[1:2, cols] = jnp.sum(grad.astype(jnp.float32), axis=0, keepdims=True)
-        for place, to_ref in enumerate((kept_ref, sent_ref)):
-            which = core ^ place
-            left = inputs_flip_ref[pl.ds(pl.multiple_of(which * LANES, LANES), LANES), :]
-            product = matmul(left, grad).astype(jnp.bfloat16)
-            for c in range(8):
-                for lane in range(tile // LANES):
-                    chunk = c * 8 + t * (tile // LANES) + lane
-                    to_ref[chunk, 0:16, :] = product[
-                        c * 16 : (c + 1) * 16, lane * LANES : (lane + 1) * LANES
-                    ]
+        product = matmul(inputs_flip_ref[...], grad).astype(jnp.bfloat16)
+        for part in range(depth // 32):
+            grads[part, :, cols] = product[part * 32 : (part + 1) * 32, :]
         return carry
 
     lax.fori_loop(0, hidden_width // tile, first_grads, 0)
     for place, to_ref in enumerate((kept_ref, sent_ref)):
         which = core ^ place
-        to_ref[:, 16:, :] = jnp.zeros((to_ref.shape[0], 8, LANES), jnp.bfloat16)
-        for lane in range(8):
-            cols = slice(lane * LANES, (lane + 1) * LANES)
-            row = jnp.where(which == 0, bias_grads[0:1, cols], bias_grads[1:2, cols])
-            to_ref[lane, 16:, :] = jnp.broadcast_to(row, (8, LANES)).astype(jnp.bfloat16)
+        row = jnp.where(which == 0, bias_grads[0:1, :], bias_grads[1:2, :])
+        row = jnp.broadcast_to(row, (16, hidden_width)).astype(jnp.bfloat16)
+        for position, flip in enumerate((0, 3, 1, 2)):
+            to_ref[position, 0:32, :] = grads[(z ^ flip) * 2 + which]
+            to_ref[position, 32:48, :] = row
 
 
 def shaped(*shape, dtype=jnp.bfloat16):
     return jax.ShapeDtypeStruct(shape, dtype)
 
 
-def spread_kernel(core_ref, z_ref, kept_ref, other_ref, root_ref, near_ref, first_root_ref, first_near_ref, bias_two_ref, bias_one_ref):
-    core, z = core_ref[0], z_ref[0]
-    step = pl.program_id(0)
-    even = core == 0
+def spread_kernel(core_ref, kept_ref, other_ref, root_ref, near_ref):
+    even = core_ref[0] == 0
     for c in range(8):
         for lane in range(8):
             kept = kept_ref[c, lane * 16 : (lane + 1) * 16, :].astype(jnp.float32)
@@ -414,51 +410,27 @@
             root_ref[at, cols] = jnp.where(even, kept, other)
             near_ref[at, cols] = jnp.where(even, other, kept)
 
-    here = lax.shift_right_logical(z, 1) == core
-    base = lax.bitwise_and(z, 1) * 4
-    for j, to_ref in enumerate((first_root_ref, first_near_ref)):
-        for i in range(2):
-
-            @pl.when(step == base + 2 * j + i)
-            def _(to_ref=to_ref, i=i):
-                for lane in range(8):
-                    kept = kept_ref[lane, LANES : LANES + 16, :].astype(jnp.float32)
-                    other = other_ref[lane, LANES : LANES + 16, :].astype(jnp.float32)
-                    at, cols = slice(i * 16, (i + 1) * 16), slice(lane * LANES, (lane + 1) * LANES)
-                    to_ref[at, cols] = jnp.where(here, kept, other)
-
-    @pl.when(step == 0)
-    def _():
-        for lane in range(8):
-            kept = kept_ref[lane, LANES + 16 :, :].astype(jnp.float32)[0:1, :]
-            other = other_ref[lane, LANES + 16 :, :].astype(jnp.float32)[0:1, :]
-            cols = slice(lane * LANES, (lane + 1) * LANES)
-            bias_two_ref[:, cols] = jnp.where(even, kept, other)
-            bias_one_ref[:, cols] = jnp.where(even, other, kept)
-
-
-def spread(core, z, kept, other, hidden_width):
-    f32 = jnp.float32
+
+def spread(core, kept, other, hidden_width):
+    square = shaped(hidden_width, hidden_width, dtype=jnp.float32)
     wide = pl.BlockSpec((LANES, hidden_width), lambda s: (s, 0))
-    slab = pl.BlockSpec((32, hidden_width), lambda s: (0, 0))
-    line = pl.BlockSpec((1, hidden_width), lambda s: (0, 0))
-    block = pl.BlockSpec((8, CHUNK, LANES), lambda s: (s, 0, 0))
+    block = pl.BlockSpec((8, LANES, LANES), lambda s: (s, 0, 0))
     return pl.pallas_call(
         spread_kernel,
         grid=(8,),
-        out_shape=(
-            shaped(hidden_width, hidden_width, dtype=f32),
-            shaped(hidden_width, hidden_width, dtype=f32),
-            shaped(32, hidden_width, dtype=f32),
-            shaped(32, hidden_width, dtype=f32),
-            shaped(1, hidden_width, dtype=f32),
-            shaped(1, hidden_width, dtype=f32),
-        ),
-        in_specs=[SMEM, SMEM, block, block],
-        out_specs=(wide, wide, slab, slab, line, line),
+        out_shape=(square, square),
+        in_specs=[SMEM, block, block],
+        out_specs=(wide, wide),
         name="spread",
-        compiler_params=pltpu.CompilerParams(vmem_limit_bytes=16 << 20),
-    )(core, z, kept, other)
+        compiler_params=pltpu.CompilerParams(vmem_limit_bytes=8 << 20),
+    )(core, kept, other)
+
+
+PAIRS = {1: [(0, 1), (1, 0), (2, 3), (3, 2)], 3: [(0, 3), (3, 0), (1, 2), (2, 1)]}
+
+
+def plus(mine, other):
+    return (mine.astype(jnp.float32) + other.astype(jnp.float32)).astype(jnp.bfloat16)
 
 
 def weights_of_pair(own, z):
@@ -467,10 +439,8 @@
     return jnp.concatenate([jnp.where(odd, first, own), jnp.where(odd, own, first)], axis=0)
 
 
-def weights_of_all(pair, z):
-    second = lax.ppermute(pair, "z", [(0, 3), (3, 0), (1, 2), (2, 1)])
-    late = z >= 2
-    return jnp.concatenate([jnp.where(late, second, pair), jnp.where(late, pair, second)], axis=0)
+def weights_of_others(pair):
+    return lax.ppermute(pair, "z", [(0, 3), (3, 0), (1, 2), (2, 1)])
 
 
 def exchange(value, axes):
@@ -502,11 +472,11 @@
     columns = jnp.concatenate([first_adjacent, first_center[:, None]], axis=1).T
     packed = aggregate(features, columns, first_count[None], owner_map[None], owners)
     packed, pair = lax.optimization_barrier((packed, pair))
-    first_all = weights_of_all(pair, z)
+    other_pair = weights_of_others(pair)
     arrived = exchange(packed, AXES)
     count = second_count[:, None]
     picked, flipped = picks(second_adjacent, second_center[:, None], count, owners * 8)
-    slots, depth = picked.shape[1], first_all.shape[0]
+    slots, depth = picked.shape[1], 2 * pair.shape[0]
     nodes = upstream.shape[0]
     layer_output, sent_two, hidden, rows, slope, inputs_flip, bias_grad = call(
         forward_kernel,
@@ -519,39 +489,51 @@
             shaped(depth, slots),
             shaped(8, hidden_width, dtype=jnp.float32),
         ),
-        10,
-        smem=1,
+        12,
+        smem=2,
         scratch=[pltpu.VMEM((slots, depth), jnp.bfloat16)],
-        limit=28,
+        limit=14,
         flops=6_000_000_000,
         moved=18_000_000,
         exps=3_000_000,
     )(
-        core, arrived, first_all, first_bias[None], picked, count, second_root, second_near,
+        core, z[None], arrived, pair, other_pair, first_bias[None], picked, count, second_root, second_near,
         second_bias[None], upstream,
     )
     received = lax.ppermute(sent_two, "core", [(0, 1), (1, 0)])
+    (back,) = call(
+        backward_kernel, (shaped(2 * nodes, hidden_width),), 4, limit=10,
+        flops=2_100_000_000, moved=7_000_000,
+    )(slope, second_root, second_near, count)
+    (both,) = call(
+        kept_kernel, (shaped(64, LANES, LANES),), 4, smem=1, limit=10,
+        flops=1_000_000_000, moved=7_000_000,
+    )(core, rows, slope, received)
+    terms = exchange(both, CHIPS)
     kept_one, sent_one = call(
-        backward_kernel, (shaped(64, 24, LANES), shaped(64, 24, LANES)), 9, smem=1,
+        first_grads_kernel,
+        (shaped(4, 48, hidden_width), shaped(4, 48, hidden_width)), 7, smem=2,
         scratch=[
-            pltpu.VMEM((2 * nodes, hidden_width), jnp.bfloat16),
+            pltpu.VMEM((depth // 32, 32, hidden_width), jnp.bfloat16),
             pltpu.VMEM((8, hidden_width), jnp.float32),
         ],
-        limit=24, flops=4_700_000_000, moved=12_000_000, exps=1_000_000,
-    )(core, slope, second_root, second_near, count, flipped, hidden, inputs_flip, bias_grad)
-    received_one = lax.ppermute(sent_one, "core", [(0, 1), (1, 0)])
-    (both,) = call(
-        kept_kernel, (shaped(64, CHUNK, LANES),), 6, smem=1, limit=20,
-        flops=1_000_000_000, moved=7_000_000,
-    )(core, rows, slope, received, kept_one, received_one)
-    terms = exchange(both, CHIPS)
+        limit=10, flops=2_600_000_000, moved=7_500_000, exps=1_000_000,
+    )(core, z[None], flipped, back, hidden, inputs_flip, bias_grad)
     total = jnp.sum(terms.astype(jnp.float32), axis=0).astype(jnp.bfloat16)
     mine = exchange(jnp.broadcast_to(total[None], terms.shape), CHIPS)
+    part = plus(kept_one, lax.ppermute(sent_one, "core", [(0, 1), (1, 0)]))
+    part = plus(part[:2], lax.ppermute(part[2:], "z", PAIRS[1]))
+    part = plus(part[0], lax.ppermute(part[1], "z", PAIRS[3]))
+    for axis in ("x", "y"):
+        for step_size in (1, 3):
+            part = plus(part, lax.ppermute(part, axis, PAIRS[step_size]))
+    partner = lax.ppermute(part, "core", [(0, 1), (1, 0)])
+    even = core[0] == 0
+    first = jnp.where(even, part, partner).astype(jnp.float32)
+    second = jnp.where(even, partner, part).astype(jnp.float32)
     other = lax.ppermute(mine, "core", [(0, 1), (1, 0)])
-    root_two, near_two, root_one, near_one, bias_two, bias_one = spread(
-        core, z[None], mine, other, hidden_width
-    )
-    return (layer_output, root_two, near_two, bias_two[0], root_one, near_one, bias_one[0])
+    root_two, near_two = spread(core, mine, other, hidden_width)
+    return (layer_output, root_two, near_two, first[32], first[:32], second[:32], second[32])
 
 
 def solution(mesh):

time: 186 us -> 204 us (1.097)
  blocking collectives: 80.2 us -> 35 us
  waiting for transfers between devices: 7.3 us -> 36.4 us
  starting transfers between devices: 16.8 us -> 40.9 us
  local copies, waits for them, and re-layouts: 11.9 us -> 21.5 us
    all_to_all x2 -> x1, blocking collectives: 80.2 us -> 35 us  [exchange(): return lax.all_to_all(value, axes, split_axis=0, concat_axis=0, tiled=True)]
    ppermute x2 -> x9, waiting for transfers between devices: 1.71 us -> 32.6 us  [the longest x1 14.9 us: step(): part = plus(part[:2], lax.ppermute(part[2:], 'z', PAIRS[1]))]
    ppermute x2 -> x9, starting transfers between devices: 2.33 us -> 19.9 us  [the longest x1 5.64 us: step(): partner = lax.ppermute(part, 'core', [(0, 1), (1, 0)])]
    all_to_all x1 -> x2, starting transfers between devices: 8.25 us -> 17.1 us  [exchange(): return lax.all_to_all(value, axes, split_axis=0, concat_axis=0, tiled=True)]
    unnamed x34 -> x44, local copies, waits for them, and re-layouts: 10.4 us -> 16 us
    ppermute x1, waiting for transfers between devices: 4.35 us -> 0.01 us  [step(): other = lax.ppermute(mine, 'core', [(0, 1), (1, 0)])]
    ppermute x1, waiting for transfers between devices: 0.01 us -> 3.79 us  [step(): received = lax.ppermute(sent_two, 'core', [(0, 1), (1, 0)])]
    slice x0 -> x5, local copies, waits for them, and re-layouts: none -> 2.53 us  [the longest x1 0.66 us: step(): first[:32]]
  transfers between devices with their start and end apart: 6 -> 14, of which waited for: 3 -> 10; matrix products, arithmetic and copies ran while one was open for 1% -> 2% of each run, Pallas kernels for 24% -> 21%
where the time goes in v4:
time: 204 us; the launch traced here: 203 us
  Pallas kernels  66.6 us (33%)
  starting transfers between devices  40.9 us (20%)
  waiting for transfers between devices  36.4 us (18%)
  blocking collectives  35 us (17%)
  local copies, waits for them, and re-layouts  21.5 us (11%)
    all_to_all x1, blocking collectives, exchange(): return lax.all_to_all(value, axes, split_axis=0, concat_axis=0, tiled=True)  35 us
    pallas_call x1, Pallas kernels, aggregate(): pl.pallas_call(aggregate_kernel, out_shape=jax.ShapeDtypeStruct((owners,...  28.1 us
    all_to_all x2, starting transfers between devices, exchange(): return lax.all_to_all(value, axes, split_axis=0, concat_axis=0, tiled=True)  17.1 us
    unnamed x44, local copies, waits for them, and re-layouts  16 us
    ppermute x1, waiting for transfers between devices, step(): part = plus(part[:2], lax.ppermute(part[2:], 'z', PAIRS[1]))  14.9 us
    pallas_call x1, Pallas kernels, step(): call(forward_kernel, (shaped(nodes, hidden_width), shaped(64, LANES, LANE...  14.5 us
    ppermute x4, waiting for transfers between devices, step(): part = plus(part, lax.ppermute(part, axis, PAIRS[step_size]))  11.7 us
    pallas_call x1, Pallas kernels, picks(): pl.pallas_call(picks_kernel, out_shape=(jax.ShapeDtypeStruct((2 * nodes,...  8.03 us
  transfers between devices with their start and end apart: 14, of which 10 were waited for; matrix products, arithmetic and copies ran while one was open for 2% of the time, Pallas kernels for 21%

profile of v4, /device:TPU:1, one launch (start us, length us, event | category | flops | bytes accessed | tf_op | source)
XLA Modules:
  0.0 203.0 jit_solution(1728909229276835239)
XLA Ops:
  0.7 0.9 constant_dynamic-update-slice_fusion.1
  1.5 0.8 constant_dynamic-update-slice_fusion
  2.4 2.5 %collective-permute-start = (bf16[64,1024]{1,0:T(8,128)(2,1)S(1)}, bf16[64,1024]{1,0:T(8,128)(2,1)S(1)}, u32[]{:S(2)}, u32[]{:S(2)}) collective-permute-start(bf16[64,1024]{1,0:T(8,128)(2,1)S(1)} %constant_dynamic-update-slice_fusion), channel_id=1, source_target_pairs={{0,32},{32,0},{64,96},{96,64},{1,33},{33,1},{65,97},{97,65},{2,34}... | collective-permute-start | bytes 393224 | tf_op jit(solution)/shard_map/ppermute | solution.py:437
  4.8 0.9 add_bitcast_fusion.adj_ref
  5.8 0.0 copy-start
  5.8 0.9 copy-done
  6.7 0.7 copy-done.1
  7.4 0.7 copy-done.2
  8.1 28.1 %aggregate.1 = bf16[128,16,128]{2,1,0:T(8,128)(2,1)} custom-call(bf16[32,4096]{1,0:T(8,128)(2,1)S(1)} %copy-done, s32[16,2048]{1,0:T(8,128)S(1)} %add_bitcast_fusion.adj_ref, s32[1,2048]{1,0:T(1,128)S(1)} %bitcast.20, s32[1,2048]{1,0:T(1,128)S(1)} %bitcast.21), custom_call_target="tpu_custom_call" | custom-call | flops 40000000 | bytes 3000000 | tf_op jit(solution)/shard_map/aggregate/pallas_call | solution.py:171
  36.2 0.0 collective-permute-done
  36.3 10.5 %all-to-all-start = ((bf16[128,16,128]{2,1,0:T(8,128)(2,1)}), bf16[128,16,128]{2,1,0:T(8,128)(2,1)S(1)}, u32[]{:S(2)}, u32[]{:S(2)}) async-start(bf16[128,16,128]{2,1,0:T(8,128)(2,1)} %aggregate.1), calls=%async_computation | async-start | bytes 1048576 | tf_op jit(solution)/shard_map/all_to_all | solution.py:447
  46.8 3.3 %collective-permute-start.1 = (bf16[128,1024]{1,0:T(8,128)(2,1)S(1)}, bf16[128,1024]{1,0:T(8,128)(2,1)S(1)}, u32[]{:S(2)}, u32[]{:S(2)}) collective-permute-start(bf16[128,1024]{1,0:T(8,128)(2,1)S(1)} %pad_maximum_fusion.pair_ref), channel_id=1, source_target_pairs={{0,96},{96,0},{32,64},{64,32},{1,97},{97,1},{33,65},{65,33},{2,98}... | collective-permute-start | bytes 786440 | tf_op jit(solution)/shard_map/ppermute | solution.py:443
  50.1 0.1 copy.25.count_ref
  50.3 0.1 copy.23.adj_ref
  50.4 0.1 copy.24.center_ref
  50.6 8.0 %picks.1 = (bf16[1024,1024]{1,0:T(8,128)(2,1)S(1)}, bf16[1024,1024]{1,0:T(8,128)(2,1)S(1)}) custom-call(s32[512,10]{1,0:T(8,128)S(1)} %copy.23.adj_ref, s32[512,1]{1,0:T(8,128)S(1)} %copy.24.center_ref, s32[512,1]{1,0:T(8,128)S(1)} %copy.25.count_ref), custom_call_target="tpu_custom_call" | custom-call | flops 20000000 | bytes 5000000 | tf_op jit(solution)/shard_map/picks/pallas_call | solution.py:227
  58.6 0.0 copy-start.7
  58.6 1.3 copy-done.7
  60.0 1.3 copy-done.9
  61.3 0.5 collective-permute-done.1.other_pair_ref
  61.7 0.0 all-to-all-done.arrived_ref
  61.8 0.0 copy-start.3
  61.8 1.6 copy-done.3
  63.3 1.6 copy-done.5
  64.9 1.6 copy-done.10
  66.5 1.2 copy-done.11
  67.8 14.5 %shard_map.198 = (bf16[512,1024]{1,0:T(8,128)(2,1)}, bf16[64,128,128]{2,1,0:T(8,128)(2,1)S(1)}, bf16[1024,1024]{1,0:T(8,128)(2,1)S(1)}, bf16[1024,1024]{1,0:T(8,...) custom-call(s32[1]{0:T(128)} %bitcast.core_ref, ...), custom_call_target="tpu_custom_call" | custom-call | flops 6000000000 | bytes 18000000 | tf_op jit(solution)/shard_map/pallas_call | solution.py:481
  82.2 0.8 copy-done.16
  83.0 1.0 collective-permute-start.2
  84.0 3.8 %collective-permute-done.2.received_ref = bf16[64,128,128]{2,1,0:T(8,128)(2,1)S(1)} collective-permute-done((bf16[64,128,128]{2,1,0:T(8,128)(2,1)S(1)}, bf16[64,128,128]{2,1,0:T(8,128)(2,1)S(1)}, u32[]{:S(2)}, u32[]{:S(2)}) %collective-permute-start.2) | collective-permute-done | bytes 2097184 | tf_op jit(solution)/shard_map/ppermute | solution.py:503
  87.8 1.9 shard_map.199
  89.7 35.0 %all_to_all.15 = bf16[64,128,128]{2,1,0:T(8,128)(2,1)S(1)} all-to-all(bf16[64,128,128]{2,1,0:T(8,128)(2,1)S(1)} %shard_map.199), channel_id=1, replica_groups=mesh['z'=4,'x'=4,'y'=4,'core'=2] {'z','x','y'}, dimensions={0} | all-to-all | bytes 4194304 | tf_op jit(solution)/shard_map/all_to_all | solution.py:447
  124.8 0.3 reduce_sum.12
  125.1 1.8 broadcast_in_dim.43
  126.9 6.6 %all-to-all-start.2 = ((bf16[64,128,128]{2,1,0:T(8,128)(2,1)}), bf16[64,128,128]{2,1,0:T(8,128)(2,1)S(1)}, u32[]{:S(2)}, u32[]{:S(2)}) async-start(bf16[64,128,128]{2,1,0:T(8,128)(2,1)} %broadcast_in_dim.43), calls=%async_computation.2 | async-start | bytes 4194304 | tf_op jit(solution)/shard_map/all_to_all | solution.py:447
  133.5 0.0 copy-start.4
  133.5 1.6 copy-done.4
  135.1 1.6 copy-done.6
  136.7 3.0 %shard_map.200.back_ref = bf16[1024,1024]{1,0:T(8,128)(2,1)S(1)} custom-call(bf16[512,1024]{1,0:T(8,128)(2,1)S(1)} %get-tuple-element.27.slope_ref, bf16[1024,1024]{1,0:T(8,128)(2,1)S(1)} %copy-done.4, bf16[1024,1024]{1,0:T(8,128)(2,1)S(1)} %copy-done.6, s32[512,1]{1,0:T(8,128)S(1)} %copy.25.count_ref), custom_call_target="tpu_custom_call" | custom-call | flops 2100000000 | bytes 7000000 | tf_op jit(solution)/shard_map/pallas_call | solution.py:504
  139.7 4.4 %shard_map.201 = (bf16[4,48,1024]{2,1,0:T(8,128)(2,1)S(1)}, bf16[4,48,1024]{2,1,0:T(8,128)(2,1)S(1)}) custom-call(s32[1]{0:T(128)} %bitcast.core_ref, s32[1]{0:T(128)} %bitcast.1.z_ref, bf16[1024,1024]{1,0:T(8,128)(2,1)S(1)} %copy-done.8, bf16[1024,1024]{1,0:T(8,128)(2,1)S(1)} %shard_map.200.back_ref, bf16[1024,1024]{1,0:T(8,128)(2,1)S(1)} %copy-done.15, ...), custom_call_target="tpu_custom_call" | custom-call | flops 2600000000 | bytes 7500000 | tf_op jit(solution)/shard_map/pallas_call | solution.py:513
  144.2 2.3 %collective-permute-start.4 = (bf16[4,48,1024]{2,1,0:T(8,128)(2,1)S(1)}, bf16[4,48,1024]{2,1,0:T(8,128)(2,1)S(1)}, u32[]{:S(2)}, u32[]{:S(2)}) collective-permute-start(bf16[4,48,1024]{2,1,0:T(8,128)(2,1)S(1)} %get-tuple-element.36), channel_id=1, source_target_pairs={{0,1},{1,0},{2,3},{3,2},{4,5},{5,4},{6,7},{7,6},{8,9},{9,8},{10,11... | collective-permute-start | bytes 1179656 | tf_op jit(solution)/shard_map/ppermute | solution.py:524
  146.5 1.3 collective-permute-done.4
  147.8 0.1 add_convert_fusion
  148.0 1.4 collective-permute-start.5
  149.4 14.9 %collective-permute-done.5 = bf16[2,48,1024]{2,1,0:T(8,128)(2,1)S(1)} collective-permute-done((bf16[2,48,1024]{2,1,0:T(8,128)(2,1)S(1)}, bf16[2,48,1024]{2,1,0:T(8,128)(2,1)S(1)}, u32[]{:S(2)}, u32[]{:S(2)}) %collective-permute-start.5) | collective-permute-done | bytes 196640 | tf_op jit(solution)/shard_map/ppermute | solution.py:525
  164.4 0.0 all-to-all-done.2.kept_ref
  164.4 0.5 collective-permute-start.3
  164.9 2.4 %collective-permute-start.6 = (bf16[48,1024]{1,0:T(8,128)(2,1)S(1)}, bf16[48,1024]{1,0:T(8,128)(2,1)S(1)}, u32[]{:S(2)}, u32[]{:S(2)}) collective-permute-start(bf16[48,1024]{1,0:T(8,128)(2,1)S(1)} %slice_bitcast_fusion), channel_id=1, source_target_pairs={{0,96},{96,0},{32,64},{64,32},{1,97},{97,1},{33,65},{65,33},{2,98}... | collective-permute-start | bytes 294920 | tf_op jit(solution)/shard_map/ppermute | solution.py:526
  167.2 3.2 %collective-permute-done.6 = bf16[48,1024]{1,0:T(8,128)(2,1)S(1)} collective-permute-done((bf16[48,1024]{1,0:T(8,128)(2,1)S(1)}, bf16[48,1024]{1,0:T(8,128)(2,1)S(1)}, u32[]{:S(2)}, u32[]{:S(2)}) %collective-permute-start.6) | collective-permute-done | bytes 98336 | tf_op jit(solution)/shard_map/ppermute | solution.py:526
  170.4 0.9 collective-permute-start.7
  171.4 2.6 %collective-permute-done.7 = bf16[48,1024]{1,0:T(8,128)(2,1)S(1)} collective-permute-done((bf16[48,1024]{1,0:T(8,128)(2,1)S(1)}, bf16[48,1024]{1,0:T(8,128)(2,1)S(1)}, u32[]{:S(2)}, u32[]{:S(2)}) %collective-permute-start.7) | collective-permute-done | bytes 98336 | tf_op jit(solution)/shard_map/ppermute | solution.py:529
  174.0 2.6 %collective-permute-start.8 = (bf16[48,1024]{1,0:T(8,128)(2,1)S(1)}, bf16[48,1024]{1,0:T(8,128)(2,1)S(1)}, u32[]{:S(2)}, u32[]{:S(2)}) collective-permute-start(bf16[48,1024]{1,0:T(8,128)(2,1)S(1)} %add_convert_fusion.5), channel_id=1, source_target_pairs={{0,24},{24,0},{8,16},{16,8},{1,25},{25,1},{9,17},{17,9},{2,26},{26... | collective-permute-start | bytes 294920 | tf_op jit(solution)/shard_map/ppermute | solution.py:529
  176.6 2.2 %collective-permute-done.8 = bf16[48,1024]{1,0:T(8,128)(2,1)S(1)} collective-permute-done((bf16[48,1024]{1,0:T(8,128)(2,1)S(1)}, bf16[48,1024]{1,0:T(8,128)(2,1)S(1)}, u32[]{:S(2)}, u32[]{:S(2)}) %collective-permute-start.8) | collective-permute-done | bytes 98336 | tf_op jit(solution)/shard_map/ppermute | solution.py:529
  178.8 0.1 collective-permute-start.9
  178.9 3.5 %collective-permute-done.9 = bf16[48,1024]{1,0:T(8,128)(2,1)S(1)} collective-permute-done((bf16[48,1024]{1,0:T(8,128)(2,1)S(1)}, bf16[48,1024]{1,0:T(8,128)(2,1)S(1)}, u32[]{:S(2)}, u32[]{:S(2)}) %collective-permute-start.9) | collective-permute-done | bytes 98336 | tf_op jit(solution)/shard_map/ppermute | solution.py:529
  182.4 1.3 collective-permute-start.10
  183.6 3.5 %collective-permute-done.10 = bf16[48,1024]{1,0:T(8,128)(2,1)S(1)} collective-permute-done((bf16[48,1024]{1,0:T(8,128)(2,1)S(1)}, bf16[48,1024]{1,0:T(8,128)(2,1)S(1)}, u32[]{:S(2)}, u32[]{:S(2)}) %collective-permute-start.10) | collective-permute-done | bytes 98336 | tf_op jit(solution)/shard_map/ppermute | solution.py:529
  187.2 5.6 %collective-permute-start.11 = (bf16[48,1024]{1,0:T(8,128)(2,1)S(1)}, bf16[48,1024]{1,0:T(8,128)(2,1)S(1)}, u32[]{:S(2)}, u32[]{:S(2)}) collective-permute-start(bf16[48,1024]{1,0:T(8,128)(2,1)S(1)} %add_convert_fusion.2), channel_id=1, source_target_pairs={{0,1},{1,0},{2,3},{3,2},{4,5},{5,4},{6,7},{7,6},{8,9},{9,8},{10,11... | collective-permute-start | bytes 294920 | tf_op jit(solution)/shard_map/ppermute | solution.py:530
  192.8 0.9 collective-permute-done.11
  193.8 0.7 slice.37
  194.4 0.6 slice.36
  195.0 0.7 slice.38
  195.7 0.6 slice.39
  196.3 6.7 %spread.1 = (f32[1024,1024]{1,0:T(8,128)}, f32[1024,1024]{1,0:T(8,128)}) custom-call(s32[1]{0:T(128)} %bitcast.core_ref, bf16[64,128,128]{2,1,0:T(8,128)(2,1)S(1)} %all-to-all-done.2.kept_ref, bf16[64,128,128]{2,1,0:T(8,128)(2,1)} %collective-permute-done.3.other_ref), custom_call_target="tpu_custom_call" | custom-call | tf_op jit(solution)/shard_map/spread/pallas_call | solution.py:418
  (38 shorter events, 0.3 us)
Async XLA Ops:
  0.6 49.5 %copy-start.19 = (s32[512]{0:T(512)S(1)}, s32[512]{0:T(512)}, u32[]{:S(2)}) copy-start(s32[512]{0:T(512)} %param.25) | copy-start | bytes 6148
  0.6 49.6 %copy-start.18 = (s32[512,10]{0,1:T(8,128)S(1)}, s32[512,10]{0,1:T(8,128)}, u32[]{:S(2)}) copy-start(s32[512,10]{0,1:T(8,128)} %param.23) | copy-start | bytes 61444
  0.7 49.8 %copy-start.20 = (s32[512]{0:T(512)S(1)}, s32[512]{0:T(512)}, u32[]{:S(2)}) copy-start(s32[512]{0:T(512)} %param.24) | copy-start | bytes 6148
  2.4 33.9 %collective-permute-start = (bf16[64,1024]{1,0:T(8,128)(2,1)S(1)}, bf16[64,1024]{1,0:T(8,128)(2,1)S(1)}, u32[]{:S(2)}, u32[]{:S(2)}) collective-permute-start(bf16[64,1024]{1,0:T(8,128)(2,1)S(1)} %constant_dynamic-update-slice_fusion), channel_id=1, source_target_pairs={{0,32},{32,0},{64,96},{96,64},{1,33},{33,1},{65,97},{97,65},{2,34}... | collective-permute-start | bytes 393224 | tf_op jit(solution)/shard_map/ppermute | solution.py:437
  5.8 1.0 copy-start
  6.7 0.7 copy-start.1
  7.4 0.7 copy-start.2
  36.2 25.5 %copy-start.12 = (f32[1024]{0:T(1024)S(1)}, f32[1024]{0:T(1024)}, u32[]{:S(2)}) copy-start(f32[1024]{0:T(1024)} %param.22) | copy-start | bytes 12292
  36.2 25.5 %copy-start.13 = (f32[1024]{0:T(1024)S(1)}, f32[1024]{0:T(1024)}, u32[]{:S(2)}) copy-start(f32[1024]{0:T(1024)} %param.28) | copy-start | bytes 12292
  36.3 25.4 %all-to-all-start = ((bf16[128,16,128]{2,1,0:T(8,128)(2,1)}), bf16[128,16,128]{2,1,0:T(8,128)(2,1)S(1)}, u32[]{:S(2)}, u32[]{:S(2)}) async-start(bf16[128,16,128]{2,1,0:T(8,128)(2,1)} %aggregate.1), calls=%async_computation | async-start | bytes 1048576 | tf_op jit(solution)/shard_map/all_to_all | solution.py:447
  46.8 14.9 %collective-permute-start.1 = (bf16[128,1024]{1,0:T(8,128)(2,1)S(1)}, bf16[128,1024]{1,0:T(8,128)(2,1)S(1)}, u32[]{:S(2)}, u32[]{:S(2)}) collective-permute-start(bf16[128,1024]{1,0:T(8,128)(2,1)S(1)} %pad_maximum_fusion.pair_ref), channel_id=1, source_target_pairs={{0,96},{96,0},{32,64},{64,32},{1,97},{97,1},{33,65},{65,33},{2,98}... | collective-permute-start | bytes 786440 | tf_op jit(solution)/shard_map/ppermute | solution.py:443
  58.6 1.3 copy-start.7
  59.9 1.3 copy-start.9
  61.8 1.6 copy-start.3
  63.3 1.6 copy-start.5
  64.9 1.6 copy-start.10
  66.5 1.2 copy-start.11
  82.2 0.8 copy-start.16
  83.0 6.7 %copy-start.14 = (bf16[1024,1024]{1,0:T(8,128)(2,1)}, bf16[1024,1024]{1,0:T(8,128)(2,1)S(1)}, u32[]{:S(2)}) copy-start(bf16[1024,1024]{1,0:T(8,128)(2,1)S(1)} %get-tuple-element.32.hidden_ref) | copy-start | bytes 6291460
  83.0 4.8 %collective-permute-start.2 = (bf16[64,128,128]{2,1,0:T(8,128)(2,1)S(1)}, bf16[64,128,128]{2,1,0:T(8,128)(2,1)S(1)}, u32[]{:S(2)}, u32[]{:S(2)}) collective-permute-start(bf16[64,128,128]{2,1,0:T(8,128)(2,1)S(1)} %get-tuple-element.28), channel_id=1, source_target_pairs={{0,1},{1,0},{2,3},{3,2},{4,5},{5,4},{6,7},{7,6},{8,9},{9,8},{10,11... | collective-permute-start | bytes 6291464 | tf_op jit(solution)/shard_map/ppermute | solution.py:503
  126.9 37.5 %all-to-all-start.2 = ((bf16[64,128,128]{2,1,0:T(8,128)(2,1)}), bf16[64,128,128]{2,1,0:T(8,128)(2,1)S(1)}, u32[]{:S(2)}, u32[]{:S(2)}) async-start(bf16[64,128,128]{2,1,0:T(8,128)(2,1)} %broadcast_in_dim.43), calls=%async_computation.2 | async-start | bytes 4194304 | tf_op jit(solution)/shard_map/all_to_all | solution.py:447
  133.5 1.6 copy-start.4
  135.1 1.6 copy-start.6
  136.7 3.0 %copy-start.8 = (bf16[1024,1024]{1,0:T(8,128)(2,1)S(1)}, bf16[1024,1024]{1,0:T(8,128)(2,1)}, u32[]{:S(2)}) copy-start(bf16[1024,1024]{1,0:T(8,128)(2,1)} %copy-done.7) | copy-start | bytes 6291460
  136.7 3.0 %copy-start.15 = (bf16[1024,1024]{1,0:T(8,128)(2,1)S(1)}, bf16[1024,1024]{1,0:T(8,128)(2,1)}, u32[]{:S(2)}) copy-start(bf16[1024,1024]{1,0:T(8,128)(2,1)} %copy-done.14) | copy-start | bytes 6291460
  136.7 3.0 %copy-start.17 = (bf16[256,1024]{1,0:T(8,128)(2,1)S(1)}, bf16[256,1024]{1,0:T(8,128)(2,1)}, u32[]{:S(2)}) copy-start(bf16[256,1024]{1,0:T(8,128)(2,1)} %copy-done.16) | copy-start | bytes 1572868
  144.2 3.7 %collective-permute-start.4 = (bf16[4,48,1024]{2,1,0:T(8,128)(2,1)S(1)}, bf16[4,48,1024]{2,1,0:T(8,128)(2,1)S(1)}, u32[]{:S(2)}, u32[]{:S(2)}) collective-permute-start(bf16[4,48,1024]{2,1,0:T(8,128)(2,1)S(1)} %get-tuple-element.36), channel_id=1, source_target_pairs={{0,1},{1,0},{2,3},{3,2},{4,5},{5,4},{6,7},{7,6},{8,9},{9,8},{10,11... | collective-permute-start | bytes 1179656 | tf_op jit(solution)/shard_map/ppermute | solution.py:524
  148.0 16.3 %collective-permute-start.5 = (bf16[2,48,1024]{2,1,0:T(8,128)(2,1)S(1)}, bf16[2,48,1024]{2,1,0:T(8,128)(2,1)S(1)}, u32[]{:S(2)}, u32[]{:S(2)}) collective-permute-start(bf16[2,48,1024]{2,1,0:T(8,128)(2,1)S(1)} %slice.33), channel_id=1, source_target_pairs={{0,32},{32,0},{64,96},{96,64},{1,33},{33,1},{65,97},{97,65},{2,34}... | collective-permute-start | bytes 589832 | tf_op jit(solution)/shard_map/ppermute | solution.py:525
  164.4 31.9 %collective-permute-start.3 = (bf16[64,128,128]{2,1,0:T(8,128)(2,1)S(1)}, bf16[64,128,128]{2,1,0:T(8,128)(2,1)}, u32[]{:S(2)}, u32[]{:S(2)}) collective-permute-start(bf16[64,128,128]{2,1,0:T(8,128)(2,1)S(1)} %all-to-all-done.2.kept_ref), channel_id=1, source_target_pairs={{0,1},{1,0},{2,3},{3,2},{4,5},{5,4},{6,7},{7,6},{8,9},{9,8},{10,11... | collective-permute-start | bytes 6291464 | tf_op jit(solution)/shard_map/ppermute | solution.py:534
  164.9 5.5 %collective-permute-start.6 = (bf16[48,1024]{1,0:T(8,128)(2,1)S(1)}, bf16[48,1024]{1,0:T(8,128)(2,1)S(1)}, u32[]{:S(2)}, u32[]{:S(2)}) collective-permute-start(bf16[48,1024]{1,0:T(8,128)(2,1)S(1)} %slice_bitcast_fusion), channel_id=1, source_target_pairs={{0,96},{96,0},{32,64},{64,32},{1,97},{97,1},{33,65},{65,33},{2,98}... | collective-permute-start | bytes 294920 | tf_op jit(solution)/shard_map/ppermute | solution.py:526
  170.4 3.5 %collective-permute-start.7 = (bf16[48,1024]{1,0:T(8,128)(2,1)S(1)}, bf16[48,1024]{1,0:T(8,128)(2,1)S(1)}, u32[]{:S(2)}, u32[]{:S(2)}) collective-permute-start(bf16[48,1024]{1,0:T(8,128)(2,1)S(1)} %fusion), channel_id=1, source_target_pairs={{0,8},{8,0},{16,24},{24,16},{1,9},{9,1},{17,25},{25,17},{2,10},{10... | collective-permute-start | bytes 294920 | tf_op jit(solution)/shard_map/ppermute | solution.py:529
  174.0 4.8 %collective-permute-start.8 = (bf16[48,1024]{1,0:T(8,128)(2,1)S(1)}, bf16[48,1024]{1,0:T(8,128)(2,1)S(1)}, u32[]{:S(2)}, u32[]{:S(2)}) collective-permute-start(bf16[48,1024]{1,0:T(8,128)(2,1)S(1)} %add_convert_fusion.5), channel_id=1, source_target_pairs={{0,24},{24,0},{8,16},{16,8},{1,25},{25,1},{9,17},{17,9},{2,26},{26... | collective-permute-start | bytes 294920 | tf_op jit(solution)/shard_map/ppermute | solution.py:529
  178.8 3.5 %collective-permute-start.9 = (bf16[48,1024]{1,0:T(8,128)(2,1)S(1)}, bf16[48,1024]{1,0:T(8,128)(2,1)S(1)}, u32[]{:S(2)}, u32[]{:S(2)}) collective-permute-start(bf16[48,1024]{1,0:T(8,128)(2,1)S(1)} %add_convert_fusion.4), channel_id=1, source_target_pairs={{0,2},{2,0},{4,6},{6,4},{1,3},{3,1},{5,7},{7,5},{8,10},{10,8},{12,... | collective-permute-start | bytes 294920 | tf_op jit(solution)/shard_map/ppermute | solution.py:529
  182.4 4.8 %collective-permute-start.10 = (bf16[48,1024]{1,0:T(8,128)(2,1)S(1)}, bf16[48,1024]{1,0:T(8,128)(2,1)S(1)}, u32[]{:S(2)}, u32[]{:S(2)}) collective-permute-start(bf16[48,1024]{1,0:T(8,128)(2,1)S(1)} %add_convert_fusion.3), channel_id=1, source_target_pairs={{0,6},{6,0},{2,4},{4,2},{1,7},{7,1},{3,5},{5,3},{8,14},{14,8},{10,... | collective-permute-start | bytes 294920 | tf_op jit(solution)/shard_map/ppermute | solution.py:529
  187.2 6.6 %collective-permute-start.11 = (bf16[48,1024]{1,0:T(8,128)(2,1)S(1)}, bf16[48,1024]{1,0:T(8,128)(2,1)S(1)}, u32[]{:S(2)}, u32[]{:S(2)}) collective-permute-start(bf16[48,1024]{1,0:T(8,128)(2,1)S(1)} %add_convert_fusion.2), channel_id=1, source_target_pairs={{0,1},{1,0},{2,3},{3,2},{4,5},{5,4},{6,7},{7,6},{8,9},{9,8},{10,11... | collective-permute-start | bytes 294920 | tf_op jit(solution)/shard_map/ppermute | solution.py:530

commit v5 on v3

--- a/solution.py
+++ b/solution.py
@@ -20,6 +20,7 @@
     start_indices_batching_dims=(0,),
 )
 SMEM = pl.BlockSpec(memory_space=pltpu.SMEM)
+HBM = pl.BlockSpec(memory_space=pltpu.HBM)
 
 
 def lanes_at(at, size=LANES):
@@ -187,7 +188,7 @@
     )(features, adjacent, count, owner)
 
 
-def picks_kernel(adj_ref, center_ref, count_ref, out_ref, flip_ref):
+def picks_kernel(adj_ref, center_ref, count_ref, out_hbm, flip_hbm, out_ref, flip_ref, sent):
     nodes, fan = adj_ref.shape
     slots = out_ref.shape[1]
 
@@ -215,36 +216,44 @@
         return carry
 
     lax.fori_loop(0, nodes // 16, one_tile, 0)
+    straight = pltpu.make_async_copy(out_ref, out_hbm, sent.at[0])
+    straight.start()
 
     def one_flip(t, carry):
         flip_ref[:, lanes_at(t)] = out_ref[lanes_at(t), :].T
         return carry
 
     lax.fori_loop(0, 2 * nodes // LANES, one_flip, 0)
+    flipped = pltpu.make_async_copy(flip_ref, flip_hbm, sent.at[1])
+    flipped.start()
+    straight.wait()
+    flipped.wait()
 
 
 def picks(adjacent, center, count, slots):
     nodes = adjacent.shape[0]
     return pl.pallas_call(
         picks_kernel,
-        out_shape=(
-            jax.ShapeDtypeStruct((2 * nodes, slots), jnp.bfloat16),
-            jax.ShapeDtypeStruct((slots, 2 * nodes), jnp.bfloat16),
-        ),
+        out_shape=(shaped(2 * nodes, slots), shaped(slots, 2 * nodes)),
         in_specs=[VMEM] * 3,
-        out_specs=(VMEM, VMEM),
+        out_specs=(HBM, HBM),
+        scratch_shapes=[
+            pltpu.VMEM((2 * nodes, slots), jnp.bfloat16),
+            pltpu.VMEM((slots, 2 * nodes), jnp.bfloat16),
+            pltpu.SemaphoreType.DMA((2,)),
+        ],
         name="picks",
-        compiler_params=pltpu.CompilerParams(vmem_limit_bytes=12 << 20),
+        compiler_params=pltpu.CompilerParams(vmem_limit_bytes=60 << 20),
         cost_estimate=pl.CostEstimate(flops=20_000_000, bytes_accessed=5_000_000, transcendentals=0),
     )(adjacent, center, count)
 
 
-def call(kernel, outs, ins, smem=0, scratch=(), limit=16, flops=0, moved=0, exps=0):
+def call(kernel, outs, ins, smem=0, hbm=0, hbm_outs=0, scratch=(), limit=60, flops=0, moved=0, exps=0):
     return pl.pallas_call(
         kernel,
         out_shape=outs,
-        in_specs=[SMEM] * smem + [VMEM] * (ins - smem),
-        out_specs=(VMEM,) * len(outs),
+        in_specs=[SMEM] * smem + [VMEM] * (ins - smem - hbm) + [HBM] * hbm,
+        out_specs=(VMEM,) * (len(outs) - hbm_outs) + (HBM,) * hbm_outs,
         scratch_shapes=scratch,
         compiler_params=pltpu.CompilerParams(vmem_limit_bytes=limit << 20),
         cost_estimate=pl.CostEstimate(flops=flops, bytes_accessed=moved, transcendentals=exps),
@@ -260,10 +269,36 @@
 
 
 def forward_kernel(
-    core_ref, arrived_ref, first_ref, bias_one_ref, picks_ref, count_ref, root_ref, near_ref,
-    bias_two_ref, upstream_ref, out_ref, sent_ref, hidden, rows, slope, inputs_flip, bias_grad,
-    inputs,
+    core_ref, z_ref, arrived_ref, pair_ref, other_pair_ref, bias_one_ref, count_ref, bias_two_ref,
+    picks_hbm, root_hbm, near_hbm, upstream_hbm, bias_grad, out_hbm, sent_hbm, hidden_hbm,
+    rows_hbm, slope_hbm, inputs_flip_hbm, inputs, picks_ref, root_ref, near_ref, upstream_ref,
+    out_ref, sent_ref, hidden, rows, slope, inputs_flip, arrivals, departures, sendings,
 ):
+    leaving = {
+        name: pltpu.make_async_copy(source, target, departures.at[number])
+        for number, (name, source, target) in enumerate(
+            (
+                ("out", out_ref, out_hbm),
+                ("hidden", hidden, hidden_hbm),
+                ("rows", rows, rows_hbm),
+                ("slope", slope, slope_hbm),
+                ("inputs_flip", inputs_flip, inputs_flip_hbm),
+            )
+        )
+    }
+    copies = [
+        pltpu.make_async_copy(source, target, arrivals.at[number])
+        for number, (source, target) in enumerate(
+            (
+                (picks_hbm, picks_ref),
+                (root_hbm, root_ref),
+                (near_hbm, near_ref),
+                (upstream_hbm, upstream_ref),
+            )
+        )
+    ]
+    for copy in copies:
+        copy.start()
     slots, depth = inputs.shape
     hidden_width = hidden.shape[1]
     nodes = slope.shape[0]
@@ -283,16 +318,24 @@
     lax.fori_loop(0, sources, one_source, 0)
     for t in range(slots // tile):
         inputs_flip[:, t * tile : (t + 1) * tile] = inputs[t * tile : (t + 1) * tile, :].T
+    leaving["inputs_flip"].start()
+
+    late = z_ref[0] >= 2
 
     def first_layer(t, carry):
         cols = lanes_at(t, tile)
-        pre = matmul(inputs[...], first_ref[:, cols]) + bias_one_ref[:, cols]
+        pair, other = pair_ref[:, cols], other_pair_ref[:, cols]
+        pre = matmul(inputs[:, : depth // 2], jnp.where(late, other, pair))
+        pre = pre + matmul(inputs[:, depth // 2 :], jnp.where(late, pair, other))
+        pre = pre + bias_one_ref[:, cols]
         value = jnp.maximum(pre, 0.0) + jnp.log1p(jnp.exp(-jnp.abs(pre)))
         hidden[:, cols] = value.astype(jnp.bfloat16)
         return carry
 
     lax.fori_loop(0, hidden_width // tile, first_layer, 0)
+    leaving["hidden"].start()
     inverse = 1.0 / count_ref[...].astype(jnp.float32)
+    copies[0].wait()
 
     def select(t, carry):
         cols = lanes_at(t, tile)
@@ -302,6 +345,9 @@
         return carry
 
     lax.fori_loop(0, hidden_width // tile, select, 0)
+    leaving["rows"].start()
+    for copy in copies[1:]:
+        copy.wait()
 
     def second_layer(t, carry):
         cols = lanes_at(t, tile)
@@ -316,25 +362,53 @@
         return carry
 
     lax.fori_loop(0, hidden_width // tile, second_layer, 0)
+    leaving["slope"].start()
+    leaving["out"].start()
     start = (core_ref[0] ^ 1) * nodes
+    share = tile // 16
+
+    def sending(t):
+        part = pl.ds(t * share, share)
+        return pltpu.make_async_copy(sent_ref.at[part], sent_hbm.at[part], sendings.at[t])
 
     def weight_grads(t, carry):
         left = rows[pl.ds(pl.multiple_of(start, nodes), nodes), lanes_at(t, tile)]
         put_chunks(sent_ref, t, across(left, slope[...]).astype(jnp.bfloat16))
+        sending(t).start()
         return carry
 
     lax.fori_loop(0, hidden_width // tile, weight_grads, 0)
+    for copy in leaving.values():
+        copy.wait()
+    for t in range(hidden_width // tile):
+        sending(t).wait()
 
 
 def kept_kernel(
-    core_ref, rows_ref, slope_ref, received_ref, kept_one_ref, received_one_ref, both_ref
+    core_ref, kept_one_ref, received_one_ref, rows_hbm, slope_hbm, received_hbm, both_ref,
+    rows_ref, slope_ref, received_ref, arrivals,
 ):
     nodes, hidden_width = slope_ref.shape
     tile = 256
-    start = core_ref[0] * nodes
+    start = pl.ds(pl.multiple_of(core_ref[0] * nodes, nodes), nodes)
+    copies = [
+        pltpu.make_async_copy(source, target, arrivals.at[number])
+        for number, (source, target) in enumerate(
+            (
+                (rows_hbm.at[start], rows_ref),
+                (slope_hbm, slope_ref),
+                (received_hbm, received_ref),
+            )
+        )
+    ]
+    for copy in copies:
+        copy.start()
+    copies[0].wait()
+    copies[1].wait()
+    copies[2].wait()
 
     def weight_grads(t, carry):
-        left = rows_ref[pl.ds(pl.multiple_of(start, nodes), nodes), lanes_at(t, tile)]
+        left = rows_ref[:, lanes_at(t, tile)]
         product = across(left, slope_ref[...])
         for c in range(tile // 16):
             chunk = t * (tile // 16) + c
@@ -352,23 +426,49 @@
 
 
 def backward_kernel(
-    core_ref, slope_ref, root_ref, near_ref, count_ref, flip_ref, hidden_ref, inputs_flip_ref,
-    bias_two_ref, kept_ref, sent_ref, back, bias_grads,
+    core_ref, count_ref, bias_two_ref, slope_hbm, root_hbm, near_hbm, flip_hbm, hidden_hbm,
+    inputs_flip_hbm, kept_ref, sent_ref, back, bias_grads, slope_ref, root_ref, near_ref, flip_ref,
+    hidden_ref, inputs_flip_ref, arrivals,
 ):
+    copies = [
+        pltpu.make_async_copy(source, target, arrivals.at[number])
+        for number, (source, target) in enumerate(
+            (
+                (slope_hbm, slope_ref),
+                (root_hbm, root_ref),
+                (near_hbm, near_ref),
+                (flip_hbm, flip_ref),
+                (hidden_hbm, hidden_ref),
+                (inputs_flip_hbm, inputs_flip_ref),
+            )
+        )
+    ]
+    for copy in copies:
+        copy.start()
     core = core_ref[0]
     nodes, hidden_width = slope_ref.shape
     tile = 256
     bias_grads[0:1, :] = bias_two_ref[0:1, :]
     inverse = 1.0 / count_ref[...].astype(jnp.float32)
 
-    def backward(t, carry):
+    def through_root(t, carry):
         cols = lanes_at(t, tile)
         back[:nodes, cols] = along(slope_ref[...], root_ref[cols, :]).astype(jnp.bfloat16)
+        return carry
+
+    def through_near(t, carry):
+        cols = lanes_at(t, tile)
         near = along(slope_ref[...], near_ref[cols, :])
         back[nodes:, cols] = (near * inverse).astype(jnp.bfloat16)
         return carry
 
-    lax.fori_loop(0, hidden_width // tile, backward, 0)
+    copies[0].wait()
+    copies[1].wait()
+    lax.fori_loop(0, hidden_width // tile, through_root, 0)
+    copies[2].wait()
+    lax.fori_loop(0, hidden_width // tile, through_near, 0)
+    for copy in copies[3:]:
+        copy.wait()
 
     def first_grads(t, carry):
         cols = lanes_at(t, tile)
@@ -467,10 +567,8 @@
     return jnp.concatenate([jnp.where(odd, first, own), jnp.where(odd, own, first)], axis=0)
 
 
-def weights_of_all(pair, z):
-    second = lax.ppermute(pair, "z", [(0, 3), (3, 0), (1, 2), (2, 1)])
-    late = z >= 2
-    return jnp.concatenate([jnp.where(late, second, pair), jnp.where(late, pair, second)], axis=0)
+def weights_of_others(pair):
+    return lax.ppermute(pair, "z", [(0, 3), (3, 0), (1, 2), (2, 1)])
 
 
 def exchange(value, axes):
@@ -502,48 +600,80 @@
     columns = jnp.concatenate([first_adjacent, first_center[:, None]], axis=1).T
     packed = aggregate(features, columns, first_count[None], owner_map[None], owners)
     packed, pair = lax.optimization_barrier((packed, pair))
-    first_all = weights_of_all(pair, z)
+    other_pair = weights_of_others(pair)
     arrived = exchange(packed, AXES)
     count = second_count[:, None]
     picked, flipped = picks(second_adjacent, second_center[:, None], count, owners * 8)
-    slots, depth = picked.shape[1], first_all.shape[0]
+    slots, depth = picked.shape[1], 2 * pair.shape[0]
     nodes = upstream.shape[0]
-    layer_output, sent_two, hidden, rows, slope, inputs_flip, bias_grad = call(
+    bf16, f32 = jnp.bfloat16, jnp.float32
+    bias_grad, layer_output, sent_two, hidden, rows, slope, inputs_flip = call(
         forward_kernel,
         (
+            shaped(8, hidden_width, dtype=f32),
             shaped(nodes, hidden_width),
             shaped(64, LANES, LANES),
             shaped(slots, hidden_width),
             shaped(2 * nodes, hidden_width),
             shaped(nodes, hidden_width),
             shaped(depth, slots),
-            shaped(8, hidden_width, dtype=jnp.float32),
         ),
-        10,
-        smem=1,
-        scratch=[pltpu.VMEM((slots, depth), jnp.bfloat16)],
-        limit=28,
+        12,
+        smem=2,
+        hbm=4,
+        limit=60,
+        hbm_outs=6,
+        scratch=[
+            pltpu.VMEM((slots, depth), bf16),
+            pltpu.VMEM(picked.shape, bf16),
+            pltpu.VMEM(second_root.shape, bf16),
+            pltpu.VMEM(second_near.shape, bf16),
+            pltpu.VMEM(upstream.shape, bf16),
+            pltpu.VMEM((nodes, hidden_width), bf16),
+            pltpu.VMEM((64, LANES, LANES), bf16),
+            pltpu.VMEM((slots, hidden_width), bf16),
+            pltpu.VMEM((2 * nodes, hidden_width), bf16),
+            pltpu.VMEM((nodes, hidden_width), bf16),
+            pltpu.VMEM((depth, slots), bf16),
+            pltpu.SemaphoreType.DMA((4,)),
+            pltpu.SemaphoreType.DMA((5,)),
+            pltpu.SemaphoreType.DMA((4,)),
+        ],
         flops=6_000_000_000,
         moved=18_000_000,
         exps=3_000_000,
     )(
-        core, arrived, first_all, first_bias[None], picked, count, second_root, second_near,
-        second_bias[None], upstream,
+        core, z[None], arrived, pair, other_pair, first_bias[None], count, second_bias[None],
+        picked, second_root, second_near, upstream,
     )
     received = lax.ppermute(sent_two, "core", [(0, 1), (1, 0)])
     kept_one, sent_one = call(
         backward_kernel, (shaped(64, 24, LANES), shaped(64, 24, LANES)), 9, smem=1,
+        hbm=6,
         scratch=[
-            pltpu.VMEM((2 * nodes, hidden_width), jnp.bfloat16),
-            pltpu.VMEM((8, hidden_width), jnp.float32),
+            pltpu.VMEM((2 * nodes, hidden_width), bf16),
+            pltpu.VMEM((8, hidden_width), f32),
+            pltpu.VMEM((nodes, hidden_width), bf16),
+            pltpu.VMEM(second_root.shape, bf16),
+            pltpu.VMEM(second_near.shape, bf16),
+            pltpu.VMEM(flipped.shape, bf16),
+            pltpu.VMEM((slots, hidden_width), bf16),
+            pltpu.VMEM((depth, slots), bf16),
+            pltpu.SemaphoreType.DMA((6,)),
         ],
-        limit=24, flops=4_700_000_000, moved=12_000_000, exps=1_000_000,
-    )(core, slope, second_root, second_near, count, flipped, hidden, inputs_flip, bias_grad)
+        flops=4_700_000_000, moved=12_000_000, exps=1_000_000,
+    )(core, count, bias_grad, slope, second_root, second_near, flipped, hidden, inputs_flip)
     received_one = lax.ppermute(sent_one, "core", [(0, 1), (1, 0)])
     (both,) = call(
-        kept_kernel, (shaped(64, CHUNK, LANES),), 6, smem=1, limit=20,
+        kept_kernel, (shaped(64, CHUNK, LANES),), 6, smem=1, hbm=3, limit=24,
+        scratch=[
+            pltpu.VMEM((nodes, hidden_width), bf16),
+            pltpu.VMEM((nodes, hidden_width), bf16),
+            pltpu.VMEM((64, LANES, LANES), bf16),
+            pltpu.SemaphoreType.DMA((3,)),
+        ],
         flops=1_000_000_000, moved=7_000_000,
-    )(core, rows, slope, received, kept_one, received_one)
+    )(core, kept_one, received_one, rows, slope, received)
     terms = exchange(both, CHIPS)
     total = jnp.sum(terms.astype(jnp.float32), axis=0).astype(jnp.bfloat16)
     mine = exchange(jnp.broadcast_to(total[None], terms.shape), CHIPS)

time: 186 us -> 193 us (1.038)
  Pallas kernels: 64.9 us -> 76.2 us
  starting transfers between devices: 16.8 us -> 20 us
  local copies, waits for them, and re-layouts: 11.9 us -> 8.81 us
    pallas_call x3, Pallas kernels: 24.4 us -> 31 us  [the longest x1 16.8 us: step(): call(forward_kernel, (shaped(8, hidden_width, dtype=f32), shaped(nodes, h...]
    pallas_call x1, Pallas kernels: 7.73 us -> 12.5 us  [step(): call(backward_kernel, (shaped(64, 24, LANES), shaped(64, 24, LANES)), 9,...]
    unnamed x34 -> x26, local copies, waits for them, and re-layouts: 10.4 us -> 5.93 us
    all_to_all x1, starting transfers between devices: 8.25 us -> 10.5 us  [exchange(): return lax.all_to_all(value, axes, split_axis=0, concat_axis=0, tiled=True)]
  transfers between devices with their start and end apart: 6 -> 6, of which waited for: 3 -> 2; matrix products, arithmetic and copies ran while one was open for 1% -> 2% of each run, Pallas kernels for 24% -> 27%
where the time goes in v5:
time: 193 us; the launch traced here: 192 us
  blocking collectives  79 us (41%)
  Pallas kernels  76.2 us (39%)
  starting transfers between devices  20 us (10%)
  local copies, waits for them, and re-layouts  8.81 us (5%)
  waiting for transfers between devices  6.21 us (3%)
    all_to_all x2, blocking collectives, exchange(): return lax.all_to_all(value, axes, split_axis=0, concat_axis=0, tiled=True)  79 us
    pallas_call x1, Pallas kernels, aggregate(): pl.pallas_call(aggregate_kernel, out_shape=jax.ShapeDtypeStruct((owners,...  28.1 us
    pallas_call x1, Pallas kernels, step(): call(forward_kernel, (shaped(8, hidden_width, dtype=f32), shaped(nodes, h...  16.8 us
    pallas_call x1, Pallas kernels, step(): call(backward_kernel, (shaped(64, 24, LANES), shaped(64, 24, LANES)), 9,...  12.5 us
    all_to_all x1, starting transfers between devices, exchange(): return lax.all_to_all(value, axes, split_axis=0, concat_axis=0, tiled=True)  10.5 us
    pallas_call x1, Pallas kernels, picks(): pl.pallas_call(picks_kernel, out_shape=(shaped(2 * nodes, slots), shaped(...  10.5 us
    unnamed x26, local copies, waits for them, and re-layouts  5.93 us
    pallas_call x1, Pallas kernels, spread(): pl.pallas_call(spread_kernel, grid=(8,), out_shape=(shaped(hidden_width,...  4.62 us
  transfers between devices with their start and end apart: 6, of which 2 were waited for; matrix products, arithmetic and copies ran while one was open for 2% of the time, Pallas kernels for 27%

profile of v5, /device:TPU:1, one launch (start us, length us, event | category | flops | bytes accessed | tf_op | source)
XLA Modules:
  0.0 192.3 jit_solution(72543164328589133)
XLA Ops:
  0.6 0.0 copy-start.9
  0.6 0.0 copy-start.8
  0.7 0.0 copy-start.10
  0.7 0.9 constant_dynamic-update-slice_fusion.1
  1.5 0.8 constant_dynamic-update-slice_fusion
  2.4 2.5 %collective-permute-start = (bf16[64,1024]{1,0:T(8,128)(2,1)S(1)}, bf16[64,1024]{1,0:T(8,128)(2,1)S(1)}, u32[]{:S(2)}, u32[]{:S(2)}) collective-permute-start(bf16[64,1024]{1,0:T(8,128)(2,1)S(1)} %constant_dynamic-update-slice_fusion), channel_id=1, source_target_pairs={{0,32},{32,0},{64,96},{96,64},{1,33},{33,1},{65,97},{97,65},{2,34}... | collective-permute-start | bytes 393224 | tf_op jit(solution)/shard_map/ppermute | solution.py:565
  4.8 0.9 add_bitcast_fusion.adj_ref
  5.8 0.0 copy-start.3
  5.8 0.9 copy-done.3
  6.7 0.0 copy-start.4
  6.7 0.7 copy-done.4
  7.4 0.0 copy-start.5
  7.4 0.7 copy-done.5
  8.1 28.1 %aggregate.1 = bf16[128,16,128]{2,1,0:T(8,128)(2,1)} custom-call(bf16[32,4096]{1,0:T(8,128)(2,1)S(1)} %copy-done.3, s32[16,2048]{1,0:T(8,128)S(1)} %add_bitcast_fusion.adj_ref, s32[1,2048]{1,0:T(1,128)S(1)} %bitcast.13, s32[1,2048]{1,0:T(1,128)S(1)} %bitcast.14), custom_call_target="tpu_custom_call" | custom-call | flops 40000000 | bytes 3000000 | tf_op jit(solution)/shard_map/aggregate/pallas_call | solution.py:173
  36.2 0.0 collective-permute-done
  36.3 0.0 copy-start.7
  36.3 10.5 %all-to-all-start = ((bf16[128,16,128]{2,1,0:T(8,128)(2,1)}), bf16[128,16,128]{2,1,0:T(8,128)(2,1)S(1)}, u32[]{:S(2)}, u32[]{:S(2)}) async-start(bf16[128,16,128]{2,1,0:T(8,128)(2,1)} %aggregate.1), calls=%async_computation | async-start | bytes 1048576 | tf_op jit(solution)/shard_map/all_to_all | solution.py:575
  46.8 3.3 %collective-permute-start.1 = (bf16[128,1024]{1,0:T(8,128)(2,1)S(1)}, bf16[128,1024]{1,0:T(8,128)(2,1)S(1)}, u32[]{:S(2)}, u32[]{:S(2)}) collective-permute-start(bf16[128,1024]{1,0:T(8,128)(2,1)S(1)} %pad_maximum_fusion.pair_ref), channel_id=1, source_target_pairs={{0,96},{96,0},{32,64},{64,32},{1,97},{97,1},{33,65},{65,33},{2,98}... | collective-permute-start | bytes 786440 | tf_op jit(solution)/shard_map/ppermute | solution.py:571
  50.1 0.0 copy-done.9
  50.1 0.9 copy.26.count_ref
  51.0 0.0 copy-done.8
  51.0 0.8 copy.23.adj_ref
  51.8 0.0 copy-done.10
  51.8 0.8 copy.24.center_ref
  52.7 10.5 %picks.1 = (bf16[1024,1024]{1,0:T(8,128)(2,1)}, bf16[1024,1024]{1,0:T(8,128)(2,1)}) custom-call(s32[512,10]{1,0:T(8,128)} %copy.23.adj_ref, s32[512,1]{1,0:T(8,128)} %copy.24.center_ref, s32[512,1]{1,0:T(8,128)} %copy.26.count_ref), custom_call_target="tpu_custom_call" | custom-call | flops 20000000 | bytes 5000000 | tf_op jit(solution)/shard_map/picks/pallas_call | solution.py:235
  63.2 0.0 collective-permute-done.1.other_pair_ref
  63.2 0.0 copy-start.11
  63.2 0.0 all-to-all-done.arrived_ref
  63.2 0.0 copy-start.6
  63.2 0.0 copy-done.7
  63.2 0.7 copy-done.11
  63.9 0.2 copy-done.6
  64.1 16.8 %shard_map.198 = (f32[8,1024]{1,0:T(8,128)}, bf16[512,1024]{1,0:T(8,128)(2,1)}, bf16[64,128,128]{2,1,0:T(8,128)(2,1)}, bf16[1024,1024]{1,0:T(8,128)(2,1)}, bf16[...) custom-call(s32[1]{0:T(128)} %bitcast.core_ref, s32[1]{0:T(128)} %bitcast.1.z_ref, ...), custom_call_target="tpu_custom_call" | custom-call | flops 6000000000 | bytes 18000000 | tf_op jit(solution)/shard_map/pallas_call | solution.py:610
  80.9 0.7 collective-permute-start.3
  81.6 0.0 copy-start
  81.6 0.0 copy-start.1
  81.6 12.5 %shard_map.199 = (bf16[64,24,128]{2,1,0:T(8,128)(2,1)}, bf16[64,24,128]{2,1,0:T(8,128)(2,1)}) custom-call(s32[1]{0:T(128)} %bitcast.core_ref, s32[512,1]{1,0:T(8,128)} %copy.26.count_ref, f32[8,1024]{1,0:T(8,128)} %get-tuple-element.30.bias_two_ref, bf16[512,1024]{1,0:T(8,128)(2,1)} %get-tuple-element.31.slope_hbm, bf16[1024,1024]{1,0:T(8,128)(2,1)} %root_hbm.3, ...), custom_call_target="tpu_custom_call" | custom-call | flops 4700000256 | bytes 12000000 | tf_op jit(solution)/shard_map/pallas_call | solution.py:650
  94.1 0.2 collective-permute-start.2
  94.3 1.8 collective-permute-done.2.received_one_ref
  96.1 0.0 collective-permute-done.3.received_hbm
  96.1 0.0 copy-done
  96.1 0.0 copy-done.1
  96.1 0.0 copy-start.2
  96.1 1.0 copy-done.2
  97.1 3.7 %shard_map.200 = bf16[64,152,128]{2,1,0:T(8,128)(2,1)S(1)} custom-call(s32[1]{0:T(128)} %bitcast.core_ref, bf16[64,24,128]{2,1,0:T(8,128)(2,1)S(1)} %copy-done.2, bf16[64,24,128]{2,1,0:T(8,128)(2,1)S(1)} %collective-permute-done.2.received_one_ref, bf16[1024,1024]{1,0:T(8,128)(2,1)S(1)} %copy-done, bf16[512,1024]{1,0:T(8,128)(2,1)S(1)} %copy-done.1, ...), custom_call_target="tpu_custom_call" | custom-call | flops 1000000000 | bytes 7000000 | tf_op jit(solution)/shard_map/pallas_call | solution.py:667
  100.8 41.0 %all_to_all.15 = bf16[64,152,128]{2,1,0:T(8,128)(2,1)S(1)} all-to-all(bf16[64,152,128]{2,1,0:T(8,128)(2,1)S(1)} %shard_map.200), channel_id=1, replica_groups=mesh['z'=4,'x'=4,'y'=4,'core'=2] {'z','x','y'}, dimensions={0} | all-to-all | bytes 4980736 | tf_op jit(solution)/shard_map/all_to_all | solution.py:575
  141.9 0.4 reduce_sum.12
  142.2 0.3 broadcast_in_dim.43
  142.6 38.0 %all_to_all.16.kept_ref = bf16[64,152,128]{2,1,0:T(8,128)(2,1)S(1)} all-to-all(bf16[64,152,128]{2,1,0:T(8,128)(2,1)S(1)} %broadcast_in_dim.43), channel_id=1, replica_groups=mesh['z'=4,'x'=4,'y'=4,'core'=2] {'z','x','y'}, dimensions={0} | all-to-all | bytes 4980736 | tf_op jit(solution)/shard_map/all_to_all | solution.py:575
  180.5 2.8 %collective-permute-start.4 = (bf16[64,152,128]{2,1,0:T(8,128)(2,1)S(1)}, bf16[64,152,128]{2,1,0:T(8,128)(2,1)S(1)}, u32[]{:S(2)}, u32[]{:S(2)}) collective-permute-start(bf16[64,152,128]{2,1,0:T(8,128)(2,1)S(1)} %all_to_all.16.kept_ref), channel_id=1, source_target_pairs={{0,1},{1,0},{2,3},{3,2},{4,5},{5,4},{6,7},{7,6},{8,9},{9,8},{10,11... | collective-permute-start | bytes 7471112 | tf_op jit(solution)/shard_map/ppermute | solution.py:680
  183.4 4.3 %collective-permute-done.4.other_ref = bf16[64,152,128]{2,1,0:T(8,128)(2,1)S(1)} collective-permute-done((bf16[64,152,128]{2,1,0:T(8,128)(2,1)S(1)}, bf16[64,152,128]{2,1,0:T(8,128)(2,1)S(1)}, u32[]{:S(2)}, u32[]{:S(2)}) %collective-permute-start.4) | collective-permute-done | bytes 2490400 | tf_op jit(solution)/shard_map/ppermute | solution.py:680
  187.7 4.6 %spread.1 = (f32[1024,1024]{1,0:T(8,128)}, f32[1024,1024]{1,0:T(8,128)}, f32[32,1024]{1,0:T(8,128)}, f32[32,1024]{1,0:T(8,128)}, f32[1,1024]{1,0:T(1,128)}, /*index=5*/f32[1,1024]{1,0:T(1,128)}) custom-call(s32[1]{0:T(128)} %bitcast.core_ref, s32[1]{0:T(128)} %bitcast.1.z_ref, bf16[64,152,128]{2,1,0:T(8,128)(2,1)S(1)} %all_to_all.16.kept_ref, ...), custom_call_target="tpu_custom_call" | custom-call | tf_op jit(solution)/shard_map/spread/pallas_call | solution.py:546
  (2 shorter events, 0.0 us)
Async XLA Ops:
  0.6 49.5 %copy-start.9 = (s32[512]{0:T(512)S(1)}, s32[512]{0:T(512)}, u32[]{:S(2)}) copy-start(s32[512]{0:T(512)} %param.25) | copy-start | bytes 6148
  0.6 50.4 %copy-start.8 = (s32[512,10]{0,1:T(8,128)S(1)}, s32[512,10]{0,1:T(8,128)}, u32[]{:S(2)}) copy-start(s32[512,10]{0,1:T(8,128)} %param.23) | copy-start | bytes 61444
  0.7 51.2 %copy-start.10 = (s32[512]{0:T(512)S(1)}, s32[512]{0:T(512)}, u32[]{:S(2)}) copy-start(s32[512]{0:T(512)} %param.24) | copy-start | bytes 6148
  2.4 33.9 %collective-permute-start = (bf16[64,1024]{1,0:T(8,128)(2,1)S(1)}, bf16[64,1024]{1,0:T(8,128)(2,1)S(1)}, u32[]{:S(2)}, u32[]{:S(2)}) collective-permute-start(bf16[64,1024]{1,0:T(8,128)(2,1)S(1)} %constant_dynamic-update-slice_fusion), channel_id=1, source_target_pairs={{0,32},{32,0},{64,96},{96,64},{1,33},{33,1},{65,97},{97,65},{2,34}... | collective-permute-start | bytes 393224 | tf_op jit(solution)/shard_map/ppermute | solution.py:565
  5.8 1.0 copy-start.3
  6.7 0.7 copy-start.4
  7.4 0.7 copy-start.5
  36.3 26.9 %copy-start.7 = (bf16[128,1024]{1,0:T(8,128)(2,1)}, bf16[128,1024]{1,0:T(8,128)(2,1)S(1)}, u32[]{:S(2)}) copy-start(bf16[128,1024]{1,0:T(8,128)(2,1)S(1)} %pad_maximum_fusion.pair_ref) | copy-start | bytes 786436
  36.3 26.9 %all-to-all-start = ((bf16[128,16,128]{2,1,0:T(8,128)(2,1)}), bf16[128,16,128]{2,1,0:T(8,128)(2,1)S(1)}, u32[]{:S(2)}, u32[]{:S(2)}) async-start(bf16[128,16,128]{2,1,0:T(8,128)(2,1)} %aggregate.1), calls=%async_computation | async-start | bytes 1048576 | tf_op jit(solution)/shard_map/all_to_all | solution.py:575
  46.8 16.4 %collective-permute-start.1 = (bf16[128,1024]{1,0:T(8,128)(2,1)S(1)}, bf16[128,1024]{1,0:T(8,128)(2,1)S(1)}, u32[]{:S(2)}, u32[]{:S(2)}) collective-permute-start(bf16[128,1024]{1,0:T(8,128)(2,1)S(1)} %pad_maximum_fusion.pair_ref), channel_id=1, source_target_pairs={{0,96},{96,0},{32,64},{64,32},{1,97},{97,1},{33,65},{65,33},{2,98}... | collective-permute-start | bytes 786440 | tf_op jit(solution)/shard_map/ppermute | solution.py:571
  63.2 0.7 copy-start.11
  63.2 0.9 copy-start.6
  80.9 15.2 %collective-permute-start.3 = (bf16[64,128,128]{2,1,0:T(8,128)(2,1)}, bf16[64,128,128]{2,1,0:T(8,128)(2,1)}, u32[]{:S(2)}, u32[]{:S(2)}) collective-permute-start(bf16[64,128,128]{2,1,0:T(8,128)(2,1)} %get-tuple-element.38), channel_id=1, source_target_pairs={{0,1},{1,0},{2,3},{3,2},{4,5},{5,4},{6,7},{7,6},{8,9},{9,8},{10,11... | collective-permute-start | bytes 6291464 | tf_op jit(solution)/shard_map/ppermute | solution.py:649
  81.6 14.5 %copy-start = (bf16[1024,1024]{1,0:T(8,128)(2,1)S(1)}, bf16[1024,1024]{1,0:T(8,128)(2,1)}, u32[]{:S(2)}) copy-start(bf16[1024,1024]{1,0:T(8,128)(2,1)} %get-tuple-element.37.rows_hbm) | copy-start | bytes 6291460
  81.6 14.5 %copy-start.1 = (bf16[512,1024]{1,0:T(8,128)(2,1)S(1)}, bf16[512,1024]{1,0:T(8,128)(2,1)}, u32[]{:S(2)}) copy-start(bf16[512,1024]{1,0:T(8,128)(2,1)} %get-tuple-element.31.slope_hbm) | copy-start | bytes 3145732
  94.1 2.0 %collective-permute-start.2 = (bf16[64,24,128]{2,1,0:T(8,128)(2,1)}, bf16[64,24,128]{2,1,0:T(8,128)(2,1)S(1)}, u32[]{:S(2)}, u32[]{:S(2)}) collective-permute-start(bf16[64,24,128]{2,1,0:T(8,128)(2,1)} %get-tuple-element.36), channel_id=1, source_target_pairs={{0,1},{1,0},{2,3},{3,2},{4,5},{5,4},{6,7},{7,6},{8,9},{9,8},{10,11... | collective-permute-start | bytes 1179656 | tf_op jit(solution)/shard_map/ppermute | solution.py:666
  96.1 1.0 copy-start.2
  180.5 7.2 %collective-permute-start.4 = (bf16[64,152,128]{2,1,0:T(8,128)(2,1)S(1)}, bf16[64,152,128]{2,1,0:T(8,128)(2,1)S(1)}, u32[]{:S(2)}, u32[]{:S(2)}) collective-permute-start(bf16[64,152,128]{2,1,0:T(8,128)(2,1)S(1)} %all_to_all.16.kept_ref), channel_id=1, source_target_pairs={{0,1},{1,0},{2,3},{3,2},{4,5},{5,4},{6,7},{7,6},{8,9},{9,8},{10,11... | collective-permute-start | bytes 7471112 | tf_op jit(solution)/shard_map/ppermute | solution.py:680

commit v6 on v3

--- a/solution.py
+++ b/solution.py
@@ -20,6 +20,7 @@
     start_indices_batching_dims=(0,),
 )
 SMEM = pl.BlockSpec(memory_space=pltpu.SMEM)
+HBM = pl.BlockSpec(memory_space=pltpu.HBM)
 
 
 def lanes_at(at, size=LANES):
@@ -239,16 +240,20 @@
     )(adjacent, center, count)
 
 
-def call(kernel, outs, ins, smem=0, scratch=(), limit=16, flops=0, moved=0, exps=0):
+def call(kernel, outs, ins, smem=0, hbm=0, scratch=(), limit=16, flops=0, moved=0, exps=0):
     return pl.pallas_call(
         kernel,
         out_shape=outs,
-        in_specs=[SMEM] * smem + [VMEM] * (ins - smem),
+        in_specs=[SMEM] * smem + [VMEM] * (ins - smem - hbm) + [HBM] * hbm,
         out_specs=(VMEM,) * len(outs),
         scratch_shapes=scratch,
         compiler_params=pltpu.CompilerParams(vmem_limit_bytes=limit << 20),
         cost_estimate=pl.CostEstimate(flops=flops, bytes_accessed=moved, transcendentals=exps),
     )
+
+
+def in_hbm(value):
+    return pltpu.with_memory_space_constraint(value, pltpu.HBM)
 
 
 def put_chunks(to_ref, t, product):
@@ -260,10 +265,23 @@
 
 
 def forward_kernel(
-    core_ref, arrived_ref, first_ref, bias_one_ref, picks_ref, count_ref, root_ref, near_ref,
-    bias_two_ref, upstream_ref, out_ref, sent_ref, hidden, rows, slope, inputs_flip, bias_grad,
-    inputs,
+    core_ref, z_ref, arrived_ref, pair_ref, other_pair_ref, bias_one_ref, count_ref, bias_two_ref,
+    picks_hbm, root_hbm, near_hbm, upstream_hbm, out_ref, sent_ref, hidden, rows, slope,
+    inputs_flip, bias_grad, inputs, picks_ref, root_ref, near_ref, upstream_ref, arrivals,
 ):
+    copies = [
+        pltpu.make_async_copy(source, target, arrivals.at[number])
+        for number, (source, target) in enumerate(
+            (
+                (picks_hbm, picks_ref),
+                (root_hbm, root_ref),
+                (near_hbm, near_ref),
+                (upstream_hbm, upstream_ref),
+            )
+        )
+    ]
+    for copy in copies:
+        copy.start()
     slots, depth = inputs.shape
     hidden_width = hidden.shape[1]
     nodes = slope.shape[0]
@@ -284,15 +302,21 @@
     for t in range(slots // tile):
         inputs_flip[:, t * tile : (t + 1) * tile] = inputs[t * tile : (t + 1) * tile, :].T
 
+    late = z_ref[0] >= 2
+
     def first_layer(t, carry):
         cols = lanes_at(t, tile)
-        pre = matmul(inputs[...], first_ref[:, cols]) + bias_one_ref[:, cols]
+        pair, other = pair_ref[:, cols], other_pair_ref[:, cols]
+        pre = matmul(inputs[:, : depth // 2], jnp.where(late, other, pair))
+        pre = pre + matmul(inputs[:, depth // 2 :], jnp.where(late, pair, other))
+        pre = pre + bias_one_ref[:, cols]
         value = jnp.maximum(pre, 0.0) + jnp.log1p(jnp.exp(-jnp.abs(pre)))
         hidden[:, cols] = value.astype(jnp.bfloat16)
         return carry
 
     lax.fori_loop(0, hidden_width // tile, first_layer, 0)
     inverse = 1.0 / count_ref[...].astype(jnp.float32)
+    copies[0].wait()
 
     def select(t, carry):
         cols = lanes_at(t, tile)
@@ -302,6 +326,8 @@
         return carry
 
     lax.fori_loop(0, hidden_width // tile, select, 0)
+    for copy in copies[1:]:
+        copy.wait()
 
     def second_layer(t, carry):
         cols = lanes_at(t, tile)
@@ -467,10 +493,8 @@
     return jnp.concatenate([jnp.where(odd, first, own), jnp.where(odd, own, first)], axis=0)
 
 
-def weights_of_all(pair, z):
-    second = lax.ppermute(pair, "z", [(0, 3), (3, 0), (1, 2), (2, 1)])
-    late = z >= 2
-    return jnp.concatenate([jnp.where(late, second, pair), jnp.where(late, pair, second)], axis=0)
+def weights_of_others(pair):
+    return lax.ppermute(pair, "z", [(0, 3), (3, 0), (1, 2), (2, 1)])
 
 
 def exchange(value, axes):
@@ -502,11 +526,11 @@
     columns = jnp.concatenate([first_adjacent, first_center[:, None]], axis=1).T
     packed = aggregate(features, columns, first_count[None], owner_map[None], owners)
     packed, pair = lax.optimization_barrier((packed, pair))
-    first_all = weights_of_all(pair, z)
+    other_pair = weights_of_others(pair)
     arrived = exchange(packed, AXES)
     count = second_count[:, None]
     picked, flipped = picks(second_adjacent, second_center[:, None], count, owners * 8)
-    slots, depth = picked.shape[1], first_all.shape[0]
+    slots, depth = picked.shape[1], 2 * pair.shape[0]
     nodes = upstream.shape[0]
     layer_output, sent_two, hidden, rows, slope, inputs_flip, bias_grad = call(
         forward_kernel,
@@ -519,16 +543,24 @@
             shaped(depth, slots),
             shaped(8, hidden_width, dtype=jnp.float32),
         ),
-        10,
-        smem=1,
-        scratch=[pltpu.VMEM((slots, depth), jnp.bfloat16)],
-        limit=28,
+        12,
+        smem=2,
+        hbm=4,
+        scratch=[
+            pltpu.VMEM((slots, depth), jnp.bfloat16),
+            pltpu.VMEM(picked.shape, jnp.bfloat16),
+            pltpu.VMEM(second_root.shape, jnp.bfloat16),
+            pltpu.VMEM(second_near.shape, jnp.bfloat16),
+            pltpu.VMEM(upstream.shape, jnp.bfloat16),
+            pltpu.SemaphoreType.DMA((4,)),
+        ],
+        limit=24,
         flops=6_000_000_000,
         moved=18_000_000,
         exps=3_000_000,
     )(
-        core, arrived, first_all, first_bias[None], picked, count, second_root, second_near,
-        second_bias[None], upstream,
+        core, z[None], arrived, pair, other_pair, first_bias[None], count, second_bias[None],
+        in_hbm(picked), in_hbm(second_root), in_hbm(second_near), in_hbm(upstream),
     )
     received = lax.ppermute(sent_two, "core", [(0, 1), (1, 0)])
     kept_one, sent_one = call(

time: 186 us -> 181 us (0.973)
  local copies, waits for them, and re-layouts: 11.9 us -> 7.46 us
  starting transfers between devices: 16.8 us -> 20.3 us
    unnamed x34 -> x28, local copies, waits for them, and re-layouts: 10.4 us -> 6.01 us
    all_to_all x1, starting transfers between devices: 8.25 us -> 10.5 us  [exchange(): return lax.all_to_all(value, axes, split_axis=0, concat_axis=0, tiled=True)]
where the time goes in v6:
time: 181 us; the launch traced here: 180 us
  blocking collectives  78.7 us (43%)
  Pallas kernels  65 us (36%)
  starting transfers between devices  20.3 us (11%)
  local copies, waits for them, and re-layouts  7.46 us (4%)
  waiting for transfers between devices  6.52 us (4%)
    all_to_all x2, blocking collectives, exchange(): return lax.all_to_all(value, axes, split_axis=0, concat_axis=0, tiled=True)  78.7 us
    pallas_call x1, Pallas kernels, aggregate(): pl.pallas_call(aggregate_kernel, out_shape=jax.ShapeDtypeStruct((owners,...  28.1 us
    pallas_call x1, Pallas kernels, step(): call(forward_kernel, (shaped(nodes, hidden_width), shaped(64, LANES, LANE...  14.5 us
    all_to_all x1, starting transfers between devices, exchange(): return lax.all_to_all(value, axes, split_axis=0, concat_axis=0, tiled=True)  10.5 us
    pallas_call x1, Pallas kernels, picks(): pl.pallas_call(picks_kernel, out_shape=(jax.ShapeDtypeStruct((2 * nodes,...  8.03 us
    pallas_call x1, Pallas kernels, step(): call(backward_kernel, (shaped(64, 24, LANES), shaped(64, 24, LANES)), 9,...  7.73 us
    unnamed x28, local copies, waits for them, and re-layouts  6.01 us
    pallas_call x1, Pallas kernels, spread(): pl.pallas_call(spread_kernel, grid=(8,), out_shape=(shaped(hidden_width,...  4.62 us
  transfers between devices with their start and end apart: 6, of which 3 were waited for; matrix products, arithmetic and copies ran while one was open for 1% of the time, Pallas kernels for 24%

profile of v6, /device:TPU:1, one launch (start us, length us, event | category | flops | bytes accessed | tf_op | source)
XLA Modules:
  0.0 180.0 jit_solution(4898869689245249998)
XLA Ops:
  0.6 0.0 copy-start.11
  0.6 0.0 copy-start.10
  0.7 0.0 copy-start.12
  0.7 0.9 constant_dynamic-update-slice_fusion.1
  1.5 0.8 constant_dynamic-update-slice_fusion
  2.4 2.5 %collective-permute-start = (bf16[64,1024]{1,0:T(8,128)(2,1)S(1)}, bf16[64,1024]{1,0:T(8,128)(2,1)S(1)}, u32[]{:S(2)}, u32[]{:S(2)}) collective-permute-start(bf16[64,1024]{1,0:T(8,128)(2,1)S(1)} %constant_dynamic-update-slice_fusion), channel_id=1, source_target_pairs={{0,32},{32,0},{64,96},{96,64},{1,33},{33,1},{65,97},{97,65},{2,34}... | collective-permute-start | bytes 393224 | tf_op jit(solution)/shard_map/ppermute | solution.py:491
  4.8 0.9 add_bitcast_fusion.adj_ref
  5.8 0.0 copy-start
  5.8 0.9 copy-done
  6.7 0.0 copy-start.1
  6.7 0.7 copy-done.1
  7.4 0.0 copy-start.2
  7.4 0.7 copy-done.2
  8.1 28.1 %aggregate.1 = bf16[128,16,128]{2,1,0:T(8,128)(2,1)} custom-call(bf16[32,4096]{1,0:T(8,128)(2,1)S(1)} %copy-done, s32[16,2048]{1,0:T(8,128)S(1)} %add_bitcast_fusion.adj_ref, s32[1,2048]{1,0:T(1,128)S(1)} %bitcast.13, s32[1,2048]{1,0:T(1,128)S(1)} %bitcast.14), custom_call_target="tpu_custom_call" | custom-call | flops 40000000 | bytes 3000000 | tf_op jit(solution)/shard_map/aggregate/pallas_call | solution.py:173
  36.2 0.0 copy-start.8
  36.2 0.0 copy-start.9
  36.2 0.0 collective-permute-done
  36.3 10.5 %all-to-all-start = ((bf16[128,16,128]{2,1,0:T(8,128)(2,1)}), bf16[128,16,128]{2,1,0:T(8,128)(2,1)S(1)}, u32[]{:S(2)}, u32[]{:S(2)}) async-start(bf16[128,16,128]{2,1,0:T(8,128)(2,1)} %aggregate.1), calls=%async_computation | async-start | bytes 1048576 | tf_op jit(solution)/shard_map/all_to_all | solution.py:501
  46.8 3.3 %collective-permute-start.1 = (bf16[128,1024]{1,0:T(8,128)(2,1)S(1)}, bf16[128,1024]{1,0:T(8,128)(2,1)S(1)}, u32[]{:S(2)}, u32[]{:S(2)}) collective-permute-start(bf16[128,1024]{1,0:T(8,128)(2,1)S(1)} %pad_maximum_fusion.pair_ref), channel_id=1, source_target_pairs={{0,96},{96,0},{32,64},{64,32},{1,97},{97,1},{33,65},{65,33},{2,98}... | collective-permute-start | bytes 786440 | tf_op jit(solution)/shard_map/ppermute | solution.py:497
  50.1 0.0 copy-done.11
  50.1 0.1 copy.26.count_ref
  50.3 0.0 copy-done.10
  50.3 0.1 copy.23.adj_ref
  50.4 0.0 copy-done.12
  50.4 0.1 copy.24.center_ref
  50.6 8.0 %picks.1 = (bf16[1024,1024]{1,0:T(8,128)(2,1)S(1)}, bf16[1024,1024]{1,0:T(8,128)(2,1)S(1)}) custom-call(s32[512,10]{1,0:T(8,128)S(1)} %copy.23.adj_ref, s32[512,1]{1,0:T(8,128)S(1)} %copy.24.center_ref, s32[512,1]{1,0:T(8,128)S(1)} %copy.26.count_ref), custom_call_target="tpu_custom_call" | custom-call | flops 20000000 | bytes 5000000 | tf_op jit(solution)/shard_map/picks/pallas_call | solution.py:229
  58.6 0.0 copy-start.5
  58.6 1.3 copy-done.5
  59.9 0.0 copy-start.7
  60.0 1.3 copy-done.7
  61.3 0.5 collective-permute-done.1.other_pair_ref
  61.7 0.0 all-to-all-done.arrived_ref
  61.7 0.0 copy-done.8
  61.7 0.0 copy-done.9
  61.8 0.0 copy-start.3
  61.8 0.0 copy-start.4
  61.8 0.0 copy-start.6
  61.8 14.5 %shard_map.198 = (bf16[512,1024]{1,0:T(8,128)(2,1)}, bf16[64,128,128]{2,1,0:T(8,128)(2,1)S(1)}, bf16[1024,1024]{1,0:T(8,128)(2,1)S(1)}, bf16[1024,1024]{1,0:T(8,...) custom-call(s32[1]{0:T(128)} %bitcast.core_ref, ...), custom_call_target="tpu_custom_call" | custom-call | flops 6000000000 | bytes 18000000 | tf_op jit(solution)/shard_map/pallas_call | solution.py:535
  76.3 1.1 collective-permute-start.2
  77.4 0.0 copy-done.3
  77.4 0.0 copy-done.4
  77.4 0.0 copy-done.6
  77.4 7.7 %shard_map.199 = (bf16[64,24,128]{2,1,0:T(8,128)(2,1)S(1)}, bf16[64,24,128]{2,1,0:T(8,128)(2,1)S(1)}) custom-call(s32[1]{0:T(128)} %bitcast.core_ref, bf16[512,1024]{1,0:T(8,128)(2,1)S(1)} %get-tuple-element.31.slope_ref, bf16[1024,1024]{1,0:T(8,128)(2,1)S(1)} %copy-done.3, bf16[1024,1024]{1,0:T(8,128)(2,1)S(1)} %copy-done.4, s32[512,1]{1,0:T(8,128)S(1)} %copy.26.count_ref, ...), custom_call_target="tpu_custom_call" | custom-call | flops 4700000256 | bytes 12000000 | tf_op jit(solution)/shard_map/pallas_call | solution.py:566
  85.1 0.1 collective-permute-start.3
  85.2 1.7 collective-permute-done.3.received_one_ref
  86.9 0.0 collective-permute-done.2.received_ref
  86.9 2.0 %shard_map.200 = bf16[64,152,128]{2,1,0:T(8,128)(2,1)S(1)} custom-call(s32[1]{0:T(128)} %bitcast.core_ref, bf16[1024,1024]{1,0:T(8,128)(2,1)S(1)} %get-tuple-element.30.rows_ref, bf16[512,1024]{1,0:T(8,128)(2,1)S(1)} %get-tuple-element.31.slope_ref, bf16[64,128,128]{2,1,0:T(8,128)(2,1)S(1)} %collective-permute-done.2.received_ref, ...), custom_call_target="tpu_custom_call" | custom-call | flops 1000000000 | bytes 7000000 | tf_op jit(solution)/shard_map/pallas_call | solution.py:575
  88.9 40.7 %all_to_all.15 = bf16[64,152,128]{2,1,0:T(8,128)(2,1)S(1)} all-to-all(bf16[64,152,128]{2,1,0:T(8,128)(2,1)S(1)} %shard_map.200), channel_id=1, replica_groups=mesh['z'=4,'x'=4,'y'=4,'core'=2] {'z','x','y'}, dimensions={0} | all-to-all | bytes 4980736 | tf_op jit(solution)/shard_map/all_to_all | solution.py:501
  129.6 0.4 reduce_sum.12
  129.9 0.3 broadcast_in_dim.43
  130.3 38.0 %all_to_all.16.kept_ref = bf16[64,152,128]{2,1,0:T(8,128)(2,1)S(1)} all-to-all(bf16[64,152,128]{2,1,0:T(8,128)(2,1)S(1)} %broadcast_in_dim.43), channel_id=1, replica_groups=mesh['z'=4,'x'=4,'y'=4,'core'=2] {'z','x','y'}, dimensions={0} | all-to-all | bytes 4980736 | tf_op jit(solution)/shard_map/all_to_all | solution.py:501
  168.3 2.8 %collective-permute-start.4 = (bf16[64,152,128]{2,1,0:T(8,128)(2,1)S(1)}, bf16[64,152,128]{2,1,0:T(8,128)(2,1)S(1)}, u32[]{:S(2)}, u32[]{:S(2)}) collective-permute-start(bf16[64,152,128]{2,1,0:T(8,128)(2,1)S(1)} %all_to_all.16.kept_ref), channel_id=1, source_target_pairs={{0,1},{1,0},{2,3},{3,2},{4,5},{5,4},{6,7},{7,6},{8,9},{9,8},{10,11... | collective-permute-start | bytes 7471112 | tf_op jit(solution)/shard_map/ppermute | solution.py:582
  171.1 4.3 %collective-permute-done.4.other_ref = bf16[64,152,128]{2,1,0:T(8,128)(2,1)S(1)} collective-permute-done((bf16[64,152,128]{2,1,0:T(8,128)(2,1)S(1)}, bf16[64,152,128]{2,1,0:T(8,128)(2,1)S(1)}, u32[]{:S(2)}, u32[]{:S(2)}) %collective-permute-start.4) | collective-permute-done | bytes 2490400 | tf_op jit(solution)/shard_map/ppermute | solution.py:582
  175.4 4.6 %spread.1 = (f32[1024,1024]{1,0:T(8,128)}, f32[1024,1024]{1,0:T(8,128)}, f32[32,1024]{1,0:T(8,128)}, f32[32,1024]{1,0:T(8,128)}, f32[1,1024]{1,0:T(1,128)}, /*index=5*/f32[1,1024]{1,0:T(1,128)}) custom-call(s32[1]{0:T(128)} %bitcast.core_ref, s32[1]{0:T(128)} %bitcast.1.z_ref, bf16[64,152,128]{2,1,0:T(8,128)(2,1)S(1)} %all_to_all.16.kept_ref, ...), custom_call_target="tpu_custom_call" | custom-call | tf_op jit(solution)/shard_map/spread/pallas_call | solution.py:472
  (2 shorter events, 0.0 us)
Async XLA Ops:
  0.6 49.5 %copy-start.11 = (s32[512]{0:T(512)S(1)}, s32[512]{0:T(512)}, u32[]{:S(2)}) copy-start(s32[512]{0:T(512)} %param.25) | copy-start | bytes 6148
  0.6 49.6 %copy-start.10 = (s32[512,10]{0,1:T(8,128)S(1)}, s32[512,10]{0,1:T(8,128)}, u32[]{:S(2)}) copy-start(s32[512,10]{0,1:T(8,128)} %param.23) | copy-start | bytes 61444
  0.7 49.8 %copy-start.12 = (s32[512]{0:T(512)S(1)}, s32[512]{0:T(512)}, u32[]{:S(2)}) copy-start(s32[512]{0:T(512)} %param.24) | copy-start | bytes 6148
  2.4 33.9 %collective-permute-start = (bf16[64,1024]{1,0:T(8,128)(2,1)S(1)}, bf16[64,1024]{1,0:T(8,128)(2,1)S(1)}, u32[]{:S(2)}, u32[]{:S(2)}) collective-permute-start(bf16[64,1024]{1,0:T(8,128)(2,1)S(1)} %constant_dynamic-update-slice_fusion), channel_id=1, source_target_pairs={{0,32},{32,0},{64,96},{96,64},{1,33},{33,1},{65,97},{97,65},{2,34}... | collective-permute-start | bytes 393224 | tf_op jit(solution)/shard_map/ppermute | solution.py:491
  5.8 1.0 copy-start
  6.7 0.7 copy-start.1
  7.4 0.7 copy-start.2
  36.2 25.5 %copy-start.8 = (f32[1024]{0:T(1024)S(1)}, f32[1024]{0:T(1024)}, u32[]{:S(2)}) copy-start(f32[1024]{0:T(1024)} %param.22) | copy-start | bytes 12292
  36.2 25.5 %copy-start.9 = (f32[1024]{0:T(1024)S(1)}, f32[1024]{0:T(1024)}, u32[]{:S(2)}) copy-start(f32[1024]{0:T(1024)} %param.28) | copy-start | bytes 12292
  36.3 25.4 %all-to-all-start = ((bf16[128,16,128]{2,1,0:T(8,128)(2,1)}), bf16[128,16,128]{2,1,0:T(8,128)(2,1)S(1)}, u32[]{:S(2)}, u32[]{:S(2)}) async-start(bf16[128,16,128]{2,1,0:T(8,128)(2,1)} %aggregate.1), calls=%async_computation | async-start | bytes 1048576 | tf_op jit(solution)/shard_map/all_to_all | solution.py:501
  46.8 14.9 %collective-permute-start.1 = (bf16[128,1024]{1,0:T(8,128)(2,1)S(1)}, bf16[128,1024]{1,0:T(8,128)(2,1)S(1)}, u32[]{:S(2)}, u32[]{:S(2)}) collective-permute-start(bf16[128,1024]{1,0:T(8,128)(2,1)S(1)} %pad_maximum_fusion.pair_ref), channel_id=1, source_target_pairs={{0,96},{96,0},{32,64},{64,32},{1,97},{97,1},{33,65},{65,33},{2,98}... | collective-permute-start | bytes 786440 | tf_op jit(solution)/shard_map/ppermute | solution.py:497
  58.6 1.3 copy-start.5
  59.9 1.3 copy-start.7
  61.8 15.6 %copy-start.3 = (bf16[1024,1024]{1,0:T(8,128)(2,1)S(1)}, bf16[1024,1024]{1,0:T(8,128)(2,1)}, u32[]{:S(2)}) copy-start(bf16[1024,1024]{1,0:T(8,128)(2,1)} %root_ref.1) | copy-start | bytes 6291460
  61.8 15.6 %copy-start.4 = (bf16[1024,1024]{1,0:T(8,128)(2,1)S(1)}, bf16[1024,1024]{1,0:T(8,128)(2,1)}, u32[]{:S(2)}) copy-start(bf16[1024,1024]{1,0:T(8,128)(2,1)} %near_ref.1) | copy-start | bytes 6291460
  61.8 15.6 %copy-start.6 = (bf16[1024,1024]{1,0:T(8,128)(2,1)S(1)}, bf16[1024,1024]{1,0:T(8,128)(2,1)}, u32[]{:S(2)}) copy-start(bf16[1024,1024]{1,0:T(8,128)(2,1)} %copy-done.5) | copy-start | bytes 6291460
  76.3 10.6 %collective-permute-start.2 = (bf16[64,128,128]{2,1,0:T(8,128)(2,1)S(1)}, bf16[64,128,128]{2,1,0:T(8,128)(2,1)S(1)}, u32[]{:S(2)}, u32[]{:S(2)}) collective-permute-start(bf16[64,128,128]{2,1,0:T(8,128)(2,1)S(1)} %get-tuple-element.32), channel_id=1, source_target_pairs={{0,1},{1,0},{2,3},{3,2},{4,5},{5,4},{6,7},{7,6},{8,9},{9,8},{10,11... | collective-permute-start | bytes 6291464 | tf_op jit(solution)/shard_map/ppermute | solution.py:565
  85.1 1.8 %collective-permute-start.3 = (bf16[64,24,128]{2,1,0:T(8,128)(2,1)S(1)}, bf16[64,24,128]{2,1,0:T(8,128)(2,1)S(1)}, u32[]{:S(2)}, u32[]{:S(2)}) collective-permute-start(bf16[64,24,128]{2,1,0:T(8,128)(2,1)S(1)} %get-tuple-element.38), channel_id=1, source_target_pairs={{0,1},{1,0},{2,3},{3,2},{4,5},{5,4},{6,7},{7,6},{8,9},{9,8},{10,11... | collective-permute-start | bytes 1179656 | tf_op jit(solution)/shard_map/ppermute | solution.py:574
  168.3 7.2 %collective-permute-start.4 = (bf16[64,152,128]{2,1,0:T(8,128)(2,1)S(1)}, bf16[64,152,128]{2,1,0:T(8,128)(2,1)S(1)}, u32[]{:S(2)}, u32[]{:S(2)}) collective-permute-start(bf16[64,152,128]{2,1,0:T(8,128)(2,1)S(1)} %all_to_all.16.kept_ref), channel_id=1, source_target_pairs={{0,1},{1,0},{2,3},{3,2},{4,5},{5,4},{6,7},{7,6},{8,9},{9,8},{10,11... | collective-permute-start | bytes 7471112 | tf_op jit(solution)/shard_map/ppermute | solution.py:582

commit v7 on v6

--- a/solution.py
+++ b/solution.py
@@ -62,7 +62,7 @@
     return among(0, chunks, chunks.bit_length() - 2)
 
 
-def aggregate_kernel(feat_ref, adj_ref, count_ref, owner_ref, out_ref, index, rows, places, stage, wide):
+def aggregate_kernel(feat_ref, adj_ref, count_ref, owner_ref, out_ref, index, counts, rows, places, stage, wide):
     width, inputs = feat_ref.shape
     nodes = owner_ref.shape[1]
     owners = out_ref.shape[0]
@@ -71,34 +71,79 @@
     groups = nodes // LANES
     parts = width // 16
     steps = (fan + 1) // 4
-    i16, bf16, f32 = jnp.int16, jnp.bfloat16, jnp.float32
+    i16, i32, bf16, f32 = jnp.int16, jnp.int32, jnp.bfloat16, jnp.float32
+    span = 256
+    before = (
+        lax.broadcasted_iota(i32, (span, span), 0) < lax.broadcasted_iota(i32, (span, span), 1)
+    ).astype(bf16)
+
+    def ones(hit, axis):
+        return jnp.sum(jnp.where(hit, 1.0, 0.0), axis=axis, keepdims=True)
+
+    kinds = lax.broadcasted_iota(i32, (16, span), 0)
+    blocks = [slice(b * span, (b + 1) * span) for b in range(nodes // span)]
+    start = jnp.zeros((16, 1), f32)
+    for at in blocks:
+        start = start + ones(fan - count_ref[:, at] < kinds, 1)
+    order, seen = [], start
+    for at in blocks:
+        hit = fan - count_ref[:, at] == kinds
+        earlier = matmul(hit.astype(bf16), before) + seen
+        order.append(jnp.sum(jnp.where(hit, earlier, 0.0), axis=0, keepdims=True).astype(i32))
+        seen = seen + ones(hit, 1)
+    node_at = jnp.zeros((2 * groups, LANES), f32)
+    group_ids = lax.broadcasted_iota(i32, (groups, span), 0)
+    lane_ids = lax.broadcasted_iota(i32, (LANES, span), 0)
+    for b, place in enumerate(order):
+        node = lax.broadcasted_iota(i32, (groups, span), 1) + b * span
+        mine = group_ids == lax.shift_right_logical(place, 7)
+        weights = jnp.concatenate(
+            [
+                jnp.where(mine, lax.shift_right_logical(node, 7), 0).astype(f32),
+                jnp.where(mine, lax.bitwise_and(node, LANES - 1), 0).astype(f32),
+            ],
+            axis=0,
+        ).astype(bf16)
+        picked = (lane_ids == lax.bitwise_and(place, LANES - 1)).astype(bf16)
+        node_at = node_at + along(weights, picked)
+    node_at = node_at.astype(i32)
     for g in range(groups):
+        high = jnp.broadcast_to(node_at[g : g + 1], (16, LANES)).astype(i16)
+        low = jnp.broadcast_to(node_at[groups + g : groups + g + 1], (16, LANES)).astype(i16)
+        (columns,) = find(
+            lambda c, v: adj_ref[:, c * LANES : (c + 1) * LANES].astype(i16), high, low, groups, 1
+        )
+        columns = columns.astype(i32)
         for s in range(steps):
-            index[g * steps + s, 0:4] = adj_ref[s * 4 : s * 4 + 4, g * LANES : (g + 1) * LANES]
+            index[g * steps + s, 0:4] = columns[s * 4 : s * 4 + 4]
+        place = lax.broadcasted_iota(i32, (16, LANES), 1) + g * LANES
+        counts[g] = (fan + 1) - ones(start.astype(i32) <= place, 0).astype(i32)
 
     def one_group(g, carry):
-        count = count_ref[:, lanes_at(g)]
-
-        def four(s, total):
+        count = counts[g]
+
+        def four(s, total, first):
             total = list(total)
             for j in range(4):
                 at = index[g * steps + s, j : j + 1, :]
                 high = jnp.broadcast_to(lax.shift_right_logical(at, 7), (16, LANES)).astype(i16)
                 low = jnp.broadcast_to(lax.bitwise_and(at, LANES - 1), (16, LANES)).astype(i16)
-                valid = jnp.broadcast_to(s * 4 + j < count, (16, LANES))
                 found = find(
                     lambda c, v: feat_ref[v * 16 : (v + 1) * 16, c * LANES : (c + 1) * LANES],
                     high, low, chunks, parts,
                 )
-                if j == 3:
+                if first and j == 0:
                     for v in range(parts):
                         rows[v * 16 : (v + 1) * 16, lanes_at(g)] = found[v]
+                    continue
+                valid = jnp.broadcast_to(s * 4 + j <= count, (16, LANES))
                 for v in range(parts):
                     total[v] = total[v] + jnp.where(valid, found[v].astype(f32), 0.0)
             return tuple(total)
 
-        zero = jnp.zeros((16, LANES), f32)
-        total = lax.fori_loop(0, steps, four, (zero,) * parts)
+        total = four(0, (jnp.zeros((16, LANES), f32),) * parts, True)
+        needed = lax.shift_right_logical(jnp.max(count) + 4, 2)
+        total = lax.fori_loop(1, needed, lambda s, t: four(s, t, False), total)
         divisor = jnp.broadcast_to(count.astype(f32), (16, LANES))
         for v in range(parts):
             near = (total[v] / divisor).astype(bf16)
@@ -107,33 +152,27 @@
 
     lax.fori_loop(0, groups, one_group, 0)
 
-    span = 256
-    before = (
-        lax.broadcasted_iota(jnp.int32, (span, span), 0)
-        < lax.broadcasted_iota(jnp.int32, (span, span), 1)
-    ).astype(bf16)
-    owner_ids = lax.broadcasted_iota(jnp.int32, (owners, span), 0)
-    ranks = lax.broadcasted_iota(jnp.int32, (CAP, span), 0)
+    owner_ids = lax.broadcasted_iota(i32, (owners, span), 0)
+    ranks = lax.broadcasted_iota(i32, (CAP, span), 0)
     seen = jnp.zeros((owners, 1), f32)
     found_at = jnp.zeros((3 * CAP, owners), f32)
-    for b in range(nodes // span):
-        hit = owner_ids == owner_ref[:, b * span : (b + 1) * span]
+    for at, place in zip(blocks, order):
+        hit = owner_ids == owner_ref[:, at]
         picked = hit.astype(bf16)
         earlier = matmul(picked, before) + seen
-        rank = jnp.sum(jnp.where(hit, earlier, 0.0), axis=0, keepdims=True).astype(jnp.int32)
-        seen = seen + jnp.sum(jnp.where(hit, 1.0, 0.0), axis=1, keepdims=True)
-        node = lax.broadcasted_iota(jnp.int32, (CAP, span), 1) + b * span
+        rank = jnp.sum(jnp.where(hit, earlier, 0.0), axis=0, keepdims=True).astype(i32)
+        seen = seen + ones(hit, 1)
         mine = ranks == rank
         weights = jnp.concatenate(
             [
-                jnp.where(mine, lax.shift_right_logical(node, 7), 0).astype(f32),
-                jnp.where(mine, lax.bitwise_and(node, LANES - 1), 0).astype(f32),
+                jnp.where(mine, lax.shift_right_logical(place, 7), 0).astype(f32),
+                jnp.where(mine, lax.bitwise_and(place, LANES - 1), 0).astype(f32),
                 jnp.where(mine, 1.0, 0.0),
             ],
             axis=0,
         ).astype(bf16)
         found_at = found_at + along(weights, picked)
-    found_at = found_at.astype(jnp.int32)
+    found_at = found_at.astype(i32)
     for q in range(CAP // 4):
         for kind in range(3):
             at = kind * CAP + q * 4
@@ -177,6 +216,7 @@
         out_specs=VMEM,
         scratch_shapes=[
             pltpu.VMEM((nodes // LANES * 4, 4, LANES), jnp.int32),
+            pltpu.VMEM((nodes // LANES, 1, LANES), jnp.int32),
             pltpu.VMEM((2 * width, nodes), jnp.bfloat16),
             pltpu.VMEM((CAP // 4, 12, LANES), jnp.int32),
             pltpu.VMEM((2, 4 * width, owners), jnp.float32),
@@ -523,7 +563,7 @@
     z = lax.axis_index("z")
     core = lax.axis_index("core")[None]
     pair = weights_of_pair(jnp.concatenate([first_root, first_near], axis=0), z)
-    columns = jnp.concatenate([first_adjacent, first_center[:, None]], axis=1).T
+    columns = jnp.concatenate([first_center[:, None], first_adjacent], axis=1).T
     packed = aggregate(features, columns, first_count[None], owner_map[None], owners)
     packed, pair = lax.optimization_barrier((packed, pair))
     other_pair = weights_of_others(pair)

time: 181 us -> 176 us (0.972)
  Pallas kernels: 65 us -> 60.6 us
    pallas_call x1, Pallas kernels: 28.1 us -> 23.7 us  [aggregate(): pl.pallas_call(aggregate_kernel, out_shape=jax.ShapeDtypeStruct((owners,...]
  transfers between devices with their start and end apart: 6 -> 6, of which waited for: 3 -> 3; matrix products, arithmetic and copies ran while one was open for 1% -> 1% of each run, Pallas kernels for 24% -> 22%
where the time goes in v7:
time: 176 us; the launch traced here: 175 us
  blocking collectives  78.7 us (45%)
  Pallas kernels  60.6 us (34%)
  starting transfers between devices  20.1 us (11%)
  local copies, waits for them, and re-layouts  7.46 us (4%)
  waiting for transfers between devices  6.52 us (4%)
    all_to_all x2, blocking collectives, exchange(): return lax.all_to_all(value, axes, split_axis=0, concat_axis=0, tiled=True)  78.7 us
    pallas_call x1, Pallas kernels, aggregate(): pl.pallas_call(aggregate_kernel, out_shape=jax.ShapeDtypeStruct((owners,...  23.7 us
    pallas_call x1, Pallas kernels, step(): call(forward_kernel, (shaped(nodes, hidden_width), shaped(64, LANES, LANE...  14.6 us
    all_to_all x1, starting transfers between devices, exchange(): return lax.all_to_all(value, axes, split_axis=0, concat_axis=0, tiled=True)  10.3 us
    pallas_call x1, Pallas kernels, picks(): pl.pallas_call(picks_kernel, out_shape=(jax.ShapeDtypeStruct((2 * nodes,...  8.03 us
    pallas_call x1, Pallas kernels, step(): call(backward_kernel, (shaped(64, 24, LANES), shaped(64, 24, LANES)), 9,...  7.73 us
    unnamed x28, local copies, waits for them, and re-layouts  6.01 us
    pallas_call x1, Pallas kernels, spread(): pl.pallas_call(spread_kernel, grid=(8,), out_shape=(shaped(hidden_width,...  4.62 us
  transfers between devices with their start and end apart: 6, of which 3 were waited for; matrix products, arithmetic and copies ran while one was open for 1% of the time, Pallas kernels for 22%

profile of v7, /device:TPU:1, one launch (start us, length us, event | category | flops | bytes accessed | tf_op | source)
XLA Modules:
  0.0 175.5 jit_solution(7275885521340053372)
XLA Ops:
  0.6 0.0 copy-start.11
  0.6 0.0 copy-start.10
  0.7 0.0 copy-start.12
  0.7 0.9 constant_dynamic-update-slice_fusion.1
  1.5 0.8 constant_dynamic-update-slice_fusion
  2.4 2.5 %collective-permute-start = (bf16[64,1024]{1,0:T(8,128)(2,1)S(1)}, bf16[64,1024]{1,0:T(8,128)(2,1)S(1)}, u32[]{:S(2)}, u32[]{:S(2)}) collective-permute-start(bf16[64,1024]{1,0:T(8,128)(2,1)S(1)} %constant_dynamic-update-slice_fusion), channel_id=1, source_target_pairs={{0,32},{32,0},{64,96},{96,64},{1,33},{33,1},{65,97},{97,65},{2,34}... | collective-permute-start | bytes 393224 | tf_op jit(solution)/shard_map/ppermute | solution.py:531
  4.8 0.9 add_bitcast_fusion.adj_ref
  5.8 0.0 copy-start
  5.8 0.9 copy-done
  6.7 0.0 copy-start.1
  6.7 0.7 copy-done.1
  7.4 0.0 copy-start.2
  7.4 0.7 copy-done.2
  8.1 23.7 %aggregate.1 = bf16[128,16,128]{2,1,0:T(8,128)(2,1)} custom-call(bf16[32,4096]{1,0:T(8,128)(2,1)S(1)} %copy-done, s32[16,2048]{1,0:T(8,128)S(1)} %add_bitcast_fusion.adj_ref, s32[1,2048]{1,0:T(1,128)S(1)} %bitcast.13, s32[1,2048]{1,0:T(1,128)S(1)} %bitcast.14), custom_call_target="tpu_custom_call" | custom-call | flops 40000000 | bytes 3000000 | tf_op jit(solution)/shard_map/aggregate/pallas_call | solution.py:212
  31.8 0.0 copy-start.8
  31.8 0.0 copy-start.9
  31.8 0.0 collective-permute-done
  31.9 10.3 %all-to-all-start = ((bf16[128,16,128]{2,1,0:T(8,128)(2,1)}), bf16[128,16,128]{2,1,0:T(8,128)(2,1)S(1)}, u32[]{:S(2)}, u32[]{:S(2)}) async-start(bf16[128,16,128]{2,1,0:T(8,128)(2,1)} %aggregate.1), calls=%async_computation | async-start | bytes 1048576 | tf_op jit(solution)/shard_map/all_to_all | solution.py:541
  42.2 3.3 %collective-permute-start.1 = (bf16[128,1024]{1,0:T(8,128)(2,1)S(1)}, bf16[128,1024]{1,0:T(8,128)(2,1)S(1)}, u32[]{:S(2)}, u32[]{:S(2)}) collective-permute-start(bf16[128,1024]{1,0:T(8,128)(2,1)S(1)} %pad_maximum_fusion.pair_ref), channel_id=1, source_target_pairs={{0,96},{96,0},{32,64},{64,32},{1,97},{97,1},{33,65},{65,33},{2,98}... | collective-permute-start | bytes 786440 | tf_op jit(solution)/shard_map/ppermute | solution.py:537
  45.5 0.0 copy-done.11
  45.5 0.1 copy.26.count_ref
  45.7 0.0 copy-done.10
  45.7 0.1 copy.23.adj_ref
  45.8 0.0 copy-done.12
  45.8 0.1 copy.24.center_ref
  46.0 8.0 %picks.1 = (bf16[1024,1024]{1,0:T(8,128)(2,1)S(1)}, bf16[1024,1024]{1,0:T(8,128)(2,1)S(1)}) custom-call(s32[512,10]{1,0:T(8,128)S(1)} %copy.23.adj_ref, s32[512,1]{1,0:T(8,128)S(1)} %copy.24.center_ref, s32[512,1]{1,0:T(8,128)S(1)} %copy.26.count_ref), custom_call_target="tpu_custom_call" | custom-call | flops 20000000 | bytes 5000000 | tf_op jit(solution)/shard_map/picks/pallas_call | solution.py:269
  54.0 0.0 copy-start.5
  54.0 1.3 copy-done.5
  55.4 0.0 copy-start.7
  55.4 1.3 copy-done.7
  56.7 0.5 collective-permute-done.1.other_pair_ref
  57.1 0.0 all-to-all-done.arrived_ref
  57.1 0.0 copy-done.8
  57.1 0.0 copy-done.9
  57.2 0.0 copy-start.3
  57.2 0.0 copy-start.4
  57.2 0.0 copy-start.6
  57.2 14.6 %shard_map.198 = (bf16[512,1024]{1,0:T(8,128)(2,1)}, bf16[64,128,128]{2,1,0:T(8,128)(2,1)S(1)}, bf16[1024,1024]{1,0:T(8,128)(2,1)S(1)}, bf16[1024,1024]{1,0:T(8,...) custom-call(s32[1]{0:T(128)} %bitcast.core_ref, ...), custom_call_target="tpu_custom_call" | custom-call | flops 6000000000 | bytes 18000000 | tf_op jit(solution)/shard_map/pallas_call | solution.py:575
  71.7 1.0 collective-permute-start.2
  72.8 0.0 copy-done.3
  72.8 0.0 copy-done.4
  72.8 0.0 copy-done.6
  72.8 7.7 %shard_map.199 = (bf16[64,24,128]{2,1,0:T(8,128)(2,1)S(1)}, bf16[64,24,128]{2,1,0:T(8,128)(2,1)S(1)}) custom-call(s32[1]{0:T(128)} %bitcast.core_ref, bf16[512,1024]{1,0:T(8,128)(2,1)S(1)} %get-tuple-element.31.slope_ref, bf16[1024,1024]{1,0:T(8,128)(2,1)S(1)} %copy-done.3, bf16[1024,1024]{1,0:T(8,128)(2,1)S(1)} %copy-done.4, s32[512,1]{1,0:T(8,128)S(1)} %copy.26.count_ref, ...), custom_call_target="tpu_custom_call" | custom-call | flops 4700000256 | bytes 12000000 | tf_op jit(solution)/shard_map/pallas_call | solution.py:606
  80.5 0.1 collective-permute-start.3
  80.7 1.7 collective-permute-done.3.received_one_ref
  82.3 0.0 collective-permute-done.2.received_ref
  82.3 2.0 %shard_map.200 = bf16[64,152,128]{2,1,0:T(8,128)(2,1)S(1)} custom-call(s32[1]{0:T(128)} %bitcast.core_ref, bf16[1024,1024]{1,0:T(8,128)(2,1)S(1)} %get-tuple-element.30.rows_ref, bf16[512,1024]{1,0:T(8,128)(2,1)S(1)} %get-tuple-element.31.slope_ref, bf16[64,128,128]{2,1,0:T(8,128)(2,1)S(1)} %collective-permute-done.2.received_ref, ...), custom_call_target="tpu_custom_call" | custom-call | flops 1000000000 | bytes 7000000 | tf_op jit(solution)/shard_map/pallas_call | solution.py:615
  84.3 40.7 %all_to_all.15 = bf16[64,152,128]{2,1,0:T(8,128)(2,1)S(1)} all-to-all(bf16[64,152,128]{2,1,0:T(8,128)(2,1)S(1)} %shard_map.200), channel_id=1, replica_groups=mesh['z'=4,'x'=4,'y'=4,'core'=2] {'z','x','y'}, dimensions={0} | all-to-all | bytes 4980736 | tf_op jit(solution)/shard_map/all_to_all | solution.py:541
  125.0 0.4 reduce_sum.12
  125.4 0.3 broadcast_in_dim.43
  125.7 38.0 %all_to_all.16.kept_ref = bf16[64,152,128]{2,1,0:T(8,128)(2,1)S(1)} all-to-all(bf16[64,152,128]{2,1,0:T(8,128)(2,1)S(1)} %broadcast_in_dim.43), channel_id=1, replica_groups=mesh['z'=4,'x'=4,'y'=4,'core'=2] {'z','x','y'}, dimensions={0} | all-to-all | bytes 4980736 | tf_op jit(solution)/shard_map/all_to_all | solution.py:541
  163.7 2.8 %collective-permute-start.4 = (bf16[64,152,128]{2,1,0:T(8,128)(2,1)S(1)}, bf16[64,152,128]{2,1,0:T(8,128)(2,1)S(1)}, u32[]{:S(2)}, u32[]{:S(2)}) collective-permute-start(bf16[64,152,128]{2,1,0:T(8,128)(2,1)S(1)} %all_to_all.16.kept_ref), channel_id=1, source_target_pairs={{0,1},{1,0},{2,3},{3,2},{4,5},{5,4},{6,7},{7,6},{8,9},{9,8},{10,11... | collective-permute-start | bytes 7471112 | tf_op jit(solution)/shard_map/ppermute | solution.py:622
  166.5 4.3 %collective-permute-done.4.other_ref = bf16[64,152,128]{2,1,0:T(8,128)(2,1)S(1)} collective-permute-done((bf16[64,152,128]{2,1,0:T(8,128)(2,1)S(1)}, bf16[64,152,128]{2,1,0:T(8,128)(2,1)S(1)}, u32[]{:S(2)}, u32[]{:S(2)}) %collective-permute-start.4) | collective-permute-done | bytes 2490400 | tf_op jit(solution)/shard_map/ppermute | solution.py:622
  170.9 4.6 %spread.1 = (f32[1024,1024]{1,0:T(8,128)}, f32[1024,1024]{1,0:T(8,128)}, f32[32,1024]{1,0:T(8,128)}, f32[32,1024]{1,0:T(8,128)}, f32[1,1024]{1,0:T(1,128)}, /*index=5*/f32[1,1024]{1,0:T(1,128)}) custom-call(s32[1]{0:T(128)} %bitcast.core_ref, s32[1]{0:T(128)} %bitcast.1.z_ref, bf16[64,152,128]{2,1,0:T(8,128)(2,1)S(1)} %all_to_all.16.kept_ref, ...), custom_call_target="tpu_custom_call" | custom-call | tf_op jit(solution)/shard_map/spread/pallas_call | solution.py:512
  (2 shorter events, 0.0 us)
Async XLA Ops:
  0.6 44.9 %copy-start.11 = (s32[512]{0:T(512)S(1)}, s32[512]{0:T(512)}, u32[]{:S(2)}) copy-start(s32[512]{0:T(512)} %param.25) | copy-start | bytes 6148
  0.6 45.0 %copy-start.10 = (s32[512,10]{0,1:T(8,128)S(1)}, s32[512,10]{0,1:T(8,128)}, u32[]{:S(2)}) copy-start(s32[512,10]{0,1:T(8,128)} %param.23) | copy-start | bytes 61444
  0.7 45.2 %copy-start.12 = (s32[512]{0:T(512)S(1)}, s32[512]{0:T(512)}, u32[]{:S(2)}) copy-start(s32[512]{0:T(512)} %param.24) | copy-start | bytes 6148
  2.4 29.5 %collective-permute-start = (bf16[64,1024]{1,0:T(8,128)(2,1)S(1)}, bf16[64,1024]{1,0:T(8,128)(2,1)S(1)}, u32[]{:S(2)}, u32[]{:S(2)}) collective-permute-start(bf16[64,1024]{1,0:T(8,128)(2,1)S(1)} %constant_dynamic-update-slice_fusion), channel_id=1, source_target_pairs={{0,32},{32,0},{64,96},{96,64},{1,33},{33,1},{65,97},{97,65},{2,34}... | collective-permute-start | bytes 393224 | tf_op jit(solution)/shard_map/ppermute | solution.py:531
  5.8 1.0 copy-start
  6.7 0.7 copy-start.1
  7.4 0.7 copy-start.2
  31.8 25.3 %copy-start.8 = (f32[1024]{0:T(1024)S(1)}, f32[1024]{0:T(1024)}, u32[]{:S(2)}) copy-start(f32[1024]{0:T(1024)} %param.22) | copy-start | bytes 12292
  31.8 25.3 %copy-start.9 = (f32[1024]{0:T(1024)S(1)}, f32[1024]{0:T(1024)}, u32[]{:S(2)}) copy-start(f32[1024]{0:T(1024)} %param.28) | copy-start | bytes 12292
  31.9 25.3 %all-to-all-start = ((bf16[128,16,128]{2,1,0:T(8,128)(2,1)}), bf16[128,16,128]{2,1,0:T(8,128)(2,1)S(1)}, u32[]{:S(2)}, u32[]{:S(2)}) async-start(bf16[128,16,128]{2,1,0:T(8,128)(2,1)} %aggregate.1), calls=%async_computation | async-start | bytes 1048576 | tf_op jit(solution)/shard_map/all_to_all | solution.py:541
  42.2 14.9 %collective-permute-start.1 = (bf16[128,1024]{1,0:T(8,128)(2,1)S(1)}, bf16[128,1024]{1,0:T(8,128)(2,1)S(1)}, u32[]{:S(2)}, u32[]{:S(2)}) collective-permute-start(bf16[128,1024]{1,0:T(8,128)(2,1)S(1)} %pad_maximum_fusion.pair_ref), channel_id=1, source_target_pairs={{0,96},{96,0},{32,64},{64,32},{1,97},{97,1},{33,65},{65,33},{2,98}... | collective-permute-start | bytes 786440 | tf_op jit(solution)/shard_map/ppermute | solution.py:537
  54.0 1.3 copy-start.5
  55.4 1.3 copy-start.7
  57.2 15.6 %copy-start.3 = (bf16[1024,1024]{1,0:T(8,128)(2,1)S(1)}, bf16[1024,1024]{1,0:T(8,128)(2,1)}, u32[]{:S(2)}) copy-start(bf16[1024,1024]{1,0:T(8,128)(2,1)} %root_ref.1) | copy-start | bytes 6291460
  57.2 15.6 %copy-start.4 = (bf16[1024,1024]{1,0:T(8,128)(2,1)S(1)}, bf16[1024,1024]{1,0:T(8,128)(2,1)}, u32[]{:S(2)}) copy-start(bf16[1024,1024]{1,0:T(8,128)(2,1)} %near_ref.1) | copy-start | bytes 6291460
  57.2 15.6 %copy-start.6 = (bf16[1024,1024]{1,0:T(8,128)(2,1)S(1)}, bf16[1024,1024]{1,0:T(8,128)(2,1)}, u32[]{:S(2)}) copy-start(bf16[1024,1024]{1,0:T(8,128)(2,1)} %copy-done.5) | copy-start | bytes 6291460
  71.7 10.6 %collective-permute-start.2 = (bf16[64,128,128]{2,1,0:T(8,128)(2,1)S(1)}, bf16[64,128,128]{2,1,0:T(8,128)(2,1)S(1)}, u32[]{:S(2)}, u32[]{:S(2)}) collective-permute-start(bf16[64,128,128]{2,1,0:T(8,128)(2,1)S(1)} %get-tuple-element.32), channel_id=1, source_target_pairs={{0,1},{1,0},{2,3},{3,2},{4,5},{5,4},{6,7},{7,6},{8,9},{9,8},{10,11... | collective-permute-start | bytes 6291464 | tf_op jit(solution)/shard_map/ppermute | solution.py:605
  80.5 1.8 %collective-permute-start.3 = (bf16[64,24,128]{2,1,0:T(8,128)(2,1)S(1)}, bf16[64,24,128]{2,1,0:T(8,128)(2,1)S(1)}, u32[]{:S(2)}, u32[]{:S(2)}) collective-permute-start(bf16[64,24,128]{2,1,0:T(8,128)(2,1)S(1)} %get-tuple-element.38), channel_id=1, source_target_pairs={{0,1},{1,0},{2,3},{3,2},{4,5},{5,4},{6,7},{7,6},{8,9},{9,8},{10,11... | collective-permute-start | bytes 1179656 | tf_op jit(solution)/shard_map/ppermute | solution.py:614
  163.7 7.2 %collective-permute-start.4 = (bf16[64,152,128]{2,1,0:T(8,128)(2,1)S(1)}, bf16[64,152,128]{2,1,0:T(8,128)(2,1)S(1)}, u32[]{:S(2)}, u32[]{:S(2)}) collective-permute-start(bf16[64,152,128]{2,1,0:T(8,128)(2,1)S(1)} %all_to_all.16.kept_ref), channel_id=1, source_target_pairs={{0,1},{1,0},{2,3},{3,2},{4,5},{5,4},{6,7},{7,6},{8,9},{9,8},{10,11... | collective-permute-start | bytes 7471112 | tf_op jit(solution)/shard_map/ppermute | solution.py:622

commit v8 on v7

--- a/solution.py
+++ b/solution.py
@@ -62,7 +62,19 @@
     return among(0, chunks, chunks.bit_length() - 2)
 
 
-def aggregate_kernel(feat_ref, adj_ref, count_ref, owner_ref, out_ref, index, counts, rows, places, stage, wide):
+def aggregate_kernel(
+    adj_ref, feat_hbm, count_hbm, owner_hbm, out_ref, index, counts, rows, places, stage, wide,
+    feat_ref, count_ref, owner_ref, arrivals,
+):
+    copies = [
+        pltpu.make_async_copy(source, target, arrivals.at[number])
+        for number, (source, target) in enumerate(
+            ((count_hbm, count_ref), (owner_hbm, owner_ref), (feat_hbm, feat_ref))
+        )
+    ]
+    for copy in copies:
+        copy.start()
+    copies[0].wait()
     width, inputs = feat_ref.shape
     nodes = owner_ref.shape[1]
     owners = out_ref.shape[0]
@@ -119,6 +131,9 @@
         place = lax.broadcasted_iota(i32, (16, LANES), 1) + g * LANES
         counts[g] = (fan + 1) - ones(start.astype(i32) <= place, 0).astype(i32)
 
+    copies[1].wait()
+    copies[2].wait()
+
     def one_group(g, carry):
         count = counts[g]
 
@@ -212,7 +227,7 @@
     return pl.pallas_call(
         aggregate_kernel,
         out_shape=jax.ShapeDtypeStruct((owners, 16, LANES), jnp.bfloat16),
-        in_specs=[VMEM] * 4,
+        in_specs=[VMEM] + [HBM] * 3,
         out_specs=VMEM,
         scratch_shapes=[
             pltpu.VMEM((nodes // LANES * 4, 4, LANES), jnp.int32),
@@ -221,11 +236,15 @@
             pltpu.VMEM((CAP // 4, 12, LANES), jnp.int32),
             pltpu.VMEM((2, 4 * width, owners), jnp.float32),
             pltpu.VMEM((16 * owners, LANES), jnp.float32),
+            pltpu.VMEM(features.shape, jnp.bfloat16),
+            pltpu.VMEM(count.shape, jnp.int32),
+            pltpu.VMEM(owner.shape, jnp.int32),
+            pltpu.SemaphoreType.DMA((3,)),
         ],
         name="aggregate",
         compiler_params=pltpu.CompilerParams(vmem_limit_bytes=12 << 20),
         cost_estimate=pl.CostEstimate(flops=40_000_000, bytes_accessed=3_000_000, transcendentals=0),
-    )(features, adjacent, count, owner)
+    )(adjacent, in_hbm(features), in_hbm(count), in_hbm(owner))
 
 
 def picks_kernel(adj_ref, center_ref, count_ref, out_ref, flip_ref):
@@ -468,63 +487,104 @@
     return jax.ShapeDtypeStruct(shape, dtype)
 
 
-def spread_kernel(core_ref, z_ref, kept_ref, other_ref, root_ref, near_ref, first_root_ref, first_near_ref, bias_two_ref, bias_one_ref):
+def widen(from_ref, wide, root_hbm, near_hbm, to_root, sent):
+    tiles = wide.shape[0] // LANES
+
+    def copy(t, target):
+        return pltpu.make_async_copy(wide.at[lanes_at(t)], target.at[lanes_at(t)], sent.at[t])
+
+    def one_tile(t, carry):
+        for c in range(8):
+            at = pl.ds(pl.multiple_of(t * LANES + c * 16, 16), 16)
+            for lane in range(8):
+                piece = from_ref[t * 8 + c, lane * 16 : (lane + 1) * 16, :]
+                wide[at, lane * LANES : (lane + 1) * LANES] = piece.astype(jnp.float32)
+
+        @pl.when(to_root)
+        def _():
+            copy(t, root_hbm).start()
+
+        @pl.when(jnp.logical_not(to_root))
+        def _():
+            copy(t, near_hbm).start()
+
+        return carry
+
+    lax.fori_loop(0, tiles, one_tile, 0)
+
+    def finish():
+        @pl.when(to_root)
+        def _():
+            for t in range(tiles):
+                copy(t, root_hbm).wait()
+
+        @pl.when(jnp.logical_not(to_root))
+        def _():
+            for t in range(tiles):
+                copy(t, near_hbm).wait()
+
+    return finish
+
+
+def own_half_kernel(core_ref, kept_ref, root_hbm, near_hbm, wide, sent):
+    widen(kept_ref, wide, root_hbm, near_hbm, core_ref[0] == 0, sent)()
+
+
+def other_half_kernel(
+    core_ref, z_ref, kept_ref, other_ref, root_in, near_in, root_hbm, near_hbm, first_root_ref,
+    first_near_ref, bias_two_ref, bias_one_ref, wide, sent,
+):
+    del root_in, near_in
     core, z = core_ref[0], z_ref[0]
-    step = pl.program_id(0)
     even = core == 0
-    for c in range(8):
-        for lane in range(8):
-            kept = kept_ref[c, lane * 16 : (lane + 1) * 16, :].astype(jnp.float32)
-            other = other_ref[c, lane * 16 : (lane + 1) * 16, :].astype(jnp.float32)
-            at, cols = slice(c * 16, (c + 1) * 16), slice(lane * LANES, (lane + 1) * LANES)
-            root_ref[at, cols] = jnp.where(even, kept, other)
-            near_ref[at, cols] = jnp.where(even, other, kept)
-
+    finish = widen(other_ref, wide, root_hbm, near_hbm, core != 0, sent)
     here = lax.shift_right_logical(z, 1) == core
     base = lax.bitwise_and(z, 1) * 4
     for j, to_ref in enumerate((first_root_ref, first_near_ref)):
         for i in range(2):
-
-            @pl.when(step == base + 2 * j + i)
-            def _(to_ref=to_ref, i=i):
-                for lane in range(8):
-                    kept = kept_ref[lane, LANES : LANES + 16, :].astype(jnp.float32)
-                    other = other_ref[lane, LANES : LANES + 16, :].astype(jnp.float32)
-                    at, cols = slice(i * 16, (i + 1) * 16), slice(lane * LANES, (lane + 1) * LANES)
-                    to_ref[at, cols] = jnp.where(here, kept, other)
-
-    @pl.when(step == 0)
-    def _():
-        for lane in range(8):
-            kept = kept_ref[lane, LANES + 16 :, :].astype(jnp.float32)[0:1, :]
-            other = other_ref[lane, LANES + 16 :, :].astype(jnp.float32)[0:1, :]
-            cols = slice(lane * LANES, (lane + 1) * LANES)
-            bias_two_ref[:, cols] = jnp.where(even, kept, other)
-            bias_one_ref[:, cols] = jnp.where(even, other, kept)
-
-
-def spread(core, z, kept, other, hidden_width):
+            for lane in range(8):
+                chunk = (base + 2 * j + i) * 8 + lane
+                kept = kept_ref[chunk, LANES : LANES + 16, :].astype(jnp.float32)
+                other = other_ref[chunk, LANES : LANES + 16, :].astype(jnp.float32)
+                at, cols = slice(i * 16, (i + 1) * 16), slice(lane * LANES, (lane + 1) * LANES)
+                to_ref[at, cols] = jnp.where(here, kept, other)
+    for lane in range(8):
+        kept = kept_ref[lane, LANES + 16 :, :].astype(jnp.float32)[0:1, :]
+        other = other_ref[lane, LANES + 16 :, :].astype(jnp.float32)[0:1, :]
+        cols = slice(lane * LANES, (lane + 1) * LANES)
+        bias_two_ref[:, cols] = jnp.where(even, kept, other)
+        bias_one_ref[:, cols] = jnp.where(even, other, kept)
+    finish()
+
+
+def spread(core, z, kept, hidden_width):
     f32 = jnp.float32
-    wide = pl.BlockSpec((LANES, hidden_width), lambda s: (s, 0))
-    slab = pl.BlockSpec((32, hidden_width), lambda s: (0, 0))
-    line = pl.BlockSpec((1, hidden_width), lambda s: (0, 0))
-    block = pl.BlockSpec((8, CHUNK, LANES), lambda s: (s, 0, 0))
+    square = shaped(hidden_width, hidden_width, dtype=f32)
+    slab = shaped(32, hidden_width, dtype=f32)
+    line = shaped(1, hidden_width, dtype=f32)
+    scratch = [pltpu.VMEM(square.shape, f32), pltpu.SemaphoreType.DMA((hidden_width // LANES,))]
+    other = lax.ppermute(kept, "core", [(0, 1), (1, 0)])
+    root, near = pl.pallas_call(
+        own_half_kernel,
+        out_shape=(square, square),
+        in_specs=[SMEM, VMEM],
+        out_specs=(HBM, HBM),
+        scratch_shapes=scratch,
+        name="own_half",
+        compiler_params=pltpu.CompilerParams(vmem_limit_bytes=8 << 20),
+        cost_estimate=pl.CostEstimate(flops=1_000_000, bytes_accessed=7_000_000, transcendentals=0),
+    )(core, kept)
     return pl.pallas_call(
-        spread_kernel,
-        grid=(8,),
-        out_shape=(
-            shaped(hidden_width, hidden_width, dtype=f32),
-            shaped(hidden_width, hidden_width, dtype=f32),
-            shaped(32, hidden_width, dtype=f32),
-            shaped(32, hidden_width, dtype=f32),
-            shaped(1, hidden_width, dtype=f32),
-            shaped(1, hidden_width, dtype=f32),
-        ),
-        in_specs=[SMEM, SMEM, block, block],
-        out_specs=(wide, wide, slab, slab, line, line),
-        name="spread",
-        compiler_params=pltpu.CompilerParams(vmem_limit_bytes=16 << 20),
-    )(core, z, kept, other)
+        other_half_kernel,
+        out_shape=(square, square, slab, slab, line, line),
+        in_specs=[SMEM, SMEM, VMEM, VMEM, HBM, HBM],
+        out_specs=(HBM, HBM) + (VMEM,) * 4,
+        scratch_shapes=scratch,
+        input_output_aliases={4: 0, 5: 1},
+        name="other_half",
+        compiler_params=pltpu.CompilerParams(vmem_limit_bytes=8 << 20),
+        cost_estimate=pl.CostEstimate(flops=1_000_000, bytes_accessed=9_000_000, transcendentals=0),
+    )(core, z, kept, other, root, near)
 
 
 def weights_of_pair(own, z):
@@ -619,9 +679,8 @@
     terms = exchange(both, CHIPS)
     total = jnp.sum(terms.astype(jnp.float32), axis=0).astype(jnp.bfloat16)
     mine = exchange(jnp.broadcast_to(total[None], terms.shape), CHIPS)
-    other = lax.ppermute(mine, "core", [(0, 1), (1, 0)])
     root_two, near_two, root_one, near_one, bias_two, bias_one = spread(
-        core, z[None], mine, other, hidden_width
+        core, z[None], mine, hidden_width
     )
     return (layer_output, root_two, near_two, bias_two[0], root_one, near_one, bias_one[0])
 

time: 176 us -> 173 us (0.983)
  local copies, waits for them, and re-layouts: 7.46 us -> 5.12 us
  waiting for transfers between devices: 6.52 us -> 4.4 us
    unnamed x28 -> x22, local copies, waits for them, and re-layouts: 6.01 us -> 3.67 us
    ppermute x1, waiting for transfers between devices: 4.35 us -> 2.24 us  [spread(): other = lax.ppermute(kept, 'core', [(0, 1), (1, 0)])]
    pallas_call x1 -> x2, Pallas kernels: 4.62 us -> 4.91 us  [the longest x1 2.81 us: spread(): pl.pallas_call(other_half_kernel, out_shape=(square, square, slab, slab,...]
  transfers between devices with their start and end apart: 6 -> 6, of which waited for: 3 -> 3; matrix products, arithmetic and copies ran while one was open for 1% -> 1% of each run, Pallas kernels for 22% -> 25%
where the time goes in v8:
time: 173 us; the launch traced here: 172 us
  blocking collectives  78.7 us (45%)
  Pallas kernels  61.6 us (36%)
  starting transfers between devices  20.2 us (12%)
  local copies, waits for them, and re-layouts  5.12 us (3%)
  waiting for transfers between devices  4.4 us (3%)
    all_to_all x2, blocking collectives, exchange(): return lax.all_to_all(value, axes, split_axis=0, concat_axis=0, tiled=True)  78.7 us
    pallas_call x1, Pallas kernels, aggregate(): pl.pallas_call(aggregate_kernel, out_shape=jax.ShapeDtypeStruct((owners,...  24.5 us
    pallas_call x1, Pallas kernels, step(): call(forward_kernel, (shaped(nodes, hidden_width), shaped(64, LANES, LANE...  14.5 us
    all_to_all x1, starting transfers between devices, exchange(): return lax.all_to_all(value, axes, split_axis=0, concat_axis=0, tiled=True)  10.3 us
    pallas_call x1, Pallas kernels, picks(): pl.pallas_call(picks_kernel, out_shape=(jax.ShapeDtypeStruct((2 * nodes,...  8.03 us
    pallas_call x1, Pallas kernels, step(): call(backward_kernel, (shaped(64, 24, LANES), shaped(64, 24, LANES)), 9,...  7.73 us
    unnamed x22, local copies, waits for them, and re-layouts  3.67 us
  transfers between devices with their start and end apart: 6, of which 3 were waited for; matrix products, arithmetic and copies ran while one was open for 1% of the time, Pallas kernels for 25%

profile of v8, /device:TPU:1, one launch (start us, length us, event | category | flops | bytes accessed | tf_op | source)
XLA Modules:
  0.0 172.2 jit_solution(2718803799468467772)
XLA Ops:
  0.6 0.0 copy-start.8
  0.6 0.0 copy-start.7
  0.7 0.0 copy-start.9
  0.7 0.9 constant_dynamic-update-slice_fusion.1
  1.5 0.8 constant_dynamic-update-slice_fusion
  2.4 0.0 copy-start.5
  2.4 0.0 copy-start.6
  2.4 2.5 %collective-permute-start = (bf16[64,1024]{1,0:T(8,128)(2,1)S(1)}, bf16[64,1024]{1,0:T(8,128)(2,1)S(1)}, u32[]{:S(2)}, u32[]{:S(2)}) collective-permute-start(bf16[64,1024]{1,0:T(8,128)(2,1)S(1)} %constant_dynamic-update-slice_fusion), channel_id=1, source_target_pairs={{0,32},{32,0},{64,96},{96,64},{1,33},{33,1},{65,97},{97,65},{2,34}... | collective-permute-start | bytes 393224 | tf_op jit(solution)/shard_map/ppermute | solution.py:591
  4.9 0.9 add_bitcast_fusion.adj_ref
  5.8 24.5 %aggregate.1 = bf16[128,16,128]{2,1,0:T(8,128)(2,1)} custom-call(s32[16,2048]{1,0:T(8,128)S(1)} %add_bitcast_fusion.adj_ref, bf16[32,4096]{1,0:T(8,128)(2,1)} %feat_hbm.1, s32[1,2048]{1,0:T(1,128)} %bitcast.15, s32[1,2048]{1,0:T(1,128)} %bitcast.16), custom_call_target="tpu_custom_call" | custom-call | flops 40000000 | bytes 3000000 | tf_op jit(solution)/shard_map/aggregate/pallas_call | solution.py:227
  30.3 0.0 collective-permute-done
  30.4 10.3 %all-to-all-start = ((bf16[128,16,128]{2,1,0:T(8,128)(2,1)}), bf16[128,16,128]{2,1,0:T(8,128)(2,1)S(1)}, u32[]{:S(2)}, u32[]{:S(2)}) async-start(bf16[128,16,128]{2,1,0:T(8,128)(2,1)} %aggregate.1), calls=%async_computation | async-start | bytes 1048576 | tf_op jit(solution)/shard_map/all_to_all | solution.py:601
  40.7 3.3 %collective-permute-start.1 = (bf16[128,1024]{1,0:T(8,128)(2,1)S(1)}, bf16[128,1024]{1,0:T(8,128)(2,1)S(1)}, u32[]{:S(2)}, u32[]{:S(2)}) collective-permute-start(bf16[128,1024]{1,0:T(8,128)(2,1)S(1)} %pad_maximum_fusion.pair_ref), channel_id=1, source_target_pairs={{0,96},{96,0},{32,64},{64,32},{1,97},{97,1},{33,65},{65,33},{2,98}... | collective-permute-start | bytes 786440 | tf_op jit(solution)/shard_map/ppermute | solution.py:597
  44.0 0.0 copy-done.8
  44.0 0.1 copy.28.count_ref
  44.2 0.0 copy-done.7
  44.2 0.1 copy.25.adj_ref
  44.3 0.0 copy-done.9
  44.3 0.1 copy.26.center_ref
  44.5 8.0 %picks.1 = (bf16[1024,1024]{1,0:T(8,128)(2,1)S(1)}, bf16[1024,1024]{1,0:T(8,128)(2,1)S(1)}) custom-call(s32[512,10]{1,0:T(8,128)S(1)} %copy.25.adj_ref, s32[512,1]{1,0:T(8,128)S(1)} %copy.26.center_ref, s32[512,1]{1,0:T(8,128)S(1)} %copy.28.count_ref), custom_call_target="tpu_custom_call" | custom-call | flops 20000000 | bytes 5000000 | tf_op jit(solution)/shard_map/picks/pallas_call | solution.py:288
  52.5 0.0 copy-start.2
  52.5 1.3 copy-done.2
  53.9 0.0 copy-start.4
  53.9 1.3 copy-done.4
  55.2 0.5 collective-permute-done.1.other_pair_ref
  55.6 0.0 all-to-all-done.arrived_ref
  55.6 0.0 copy-done.5
  55.7 0.0 copy-done.6
  55.7 0.0 copy-start
  55.7 0.0 copy-start.1
  55.7 0.0 copy-start.3
  55.7 14.5 %shard_map.198 = (bf16[512,1024]{1,0:T(8,128)(2,1)}, bf16[64,128,128]{2,1,0:T(8,128)(2,1)S(1)}, bf16[1024,1024]{1,0:T(8,128)(2,1)S(1)}, bf16[1024,1024]{1,0:T(8,...) custom-call(s32[1]{0:T(128)} %bitcast.core_ref, ...), custom_call_target="tpu_custom_call" | custom-call | flops 6000000000 | bytes 18000000 | tf_op jit(solution)/shard_map/pallas_call | solution.py:635
  70.2 1.1 collective-permute-start.2
  71.3 0.0 copy-done
  71.3 0.0 copy-done.1
  71.3 0.0 copy-done.3
  71.3 7.7 %shard_map.199 = (bf16[64,24,128]{2,1,0:T(8,128)(2,1)S(1)}, bf16[64,24,128]{2,1,0:T(8,128)(2,1)S(1)}) custom-call(s32[1]{0:T(128)} %bitcast.core_ref, bf16[512,1024]{1,0:T(8,128)(2,1)S(1)} %get-tuple-element.33.slope_ref, bf16[1024,1024]{1,0:T(8,128)(2,1)S(1)} %copy-done, bf16[1024,1024]{1,0:T(8,128)(2,1)S(1)} %copy-done.1, s32[512,1]{1,0:T(8,128)S(1)} %copy.28.count_ref, ...), custom_call_target="tpu_custom_call" | custom-call | flops 4700000256 | bytes 12000000 | tf_op jit(solution)/shard_map/pallas_call | solution.py:666
  79.1 0.1 collective-permute-start.3
  79.2 1.7 collective-permute-done.3.received_one_ref
  80.9 0.0 collective-permute-done.2.received_ref
  80.9 2.0 %shard_map.200 = bf16[64,152,128]{2,1,0:T(8,128)(2,1)S(1)} custom-call(s32[1]{0:T(128)} %bitcast.core_ref, bf16[1024,1024]{1,0:T(8,128)(2,1)S(1)} %get-tuple-element.32.rows_ref, bf16[512,1024]{1,0:T(8,128)(2,1)S(1)} %get-tuple-element.33.slope_ref, bf16[64,128,128]{2,1,0:T(8,128)(2,1)S(1)} %collective-permute-done.2.received_ref, ...), custom_call_target="tpu_custom_call" | custom-call | flops 1000000000 | bytes 7000000 | tf_op jit(solution)/shard_map/pallas_call | solution.py:675
  82.9 40.7 %all_to_all.15 = bf16[64,152,128]{2,1,0:T(8,128)(2,1)S(1)} all-to-all(bf16[64,152,128]{2,1,0:T(8,128)(2,1)S(1)} %shard_map.200), channel_id=1, replica_groups=mesh['z'=4,'x'=4,'y'=4,'core'=2] {'z','x','y'}, dimensions={0} | all-to-all | bytes 4980736 | tf_op jit(solution)/shard_map/all_to_all | solution.py:601
  123.5 0.4 reduce_sum.12
  123.9 0.3 broadcast_in_dim.43
  124.2 38.0 %all_to_all.16.kept_ref = bf16[64,152,128]{2,1,0:T(8,128)(2,1)S(1)} all-to-all(bf16[64,152,128]{2,1,0:T(8,128)(2,1)S(1)} %broadcast_in_dim.43), channel_id=1, replica_groups=mesh['z'=4,'x'=4,'y'=4,'core'=2] {'z','x','y'}, dimensions={0} | all-to-all | bytes 4980736 | tf_op jit(solution)/shard_map/all_to_all | solution.py:601
  162.2 2.8 %collective-permute-start.4 = (bf16[64,152,128]{2,1,0:T(8,128)(2,1)S(1)}, bf16[64,152,128]{2,1,0:T(8,128)(2,1)S(1)}, u32[]{:S(2)}, u32[]{:S(2)}) collective-permute-start(bf16[64,152,128]{2,1,0:T(8,128)(2,1)S(1)} %all_to_all.16.kept_ref), channel_id=1, source_target_pairs={{0,1},{1,0},{2,3},{3,2},{4,5},{5,4},{6,7},{7,6},{8,9},{9,8},{10,11... | collective-permute-start | bytes 7471112 | tf_op jit(solution)/shard_map/ppermute | solution.py:566
  165.0 2.1 %own_half.1 = (f32[1024,1024]{1,0:T(8,128)}, f32[1024,1024]{1,0:T(8,128)}) custom-call(s32[1]{0:T(128)} %bitcast.core_ref, bf16[64,152,128]{2,1,0:T(8,128)(2,1)S(1)} %all_to_all.16.kept_ref), custom_call_target="tpu_custom_call" | custom-call | flops 1000000 | bytes 7000000 | tf_op jit(solution)/shard_map/own_half/pallas_call | solution.py:567
  167.1 2.2 %collective-permute-done.4.other_ref = bf16[64,152,128]{2,1,0:T(8,128)(2,1)S(1)} collective-permute-done((bf16[64,152,128]{2,1,0:T(8,128)(2,1)S(1)}, bf16[64,152,128]{2,1,0:T(8,128)(2,1)S(1)}, u32[]{:S(2)}, u32[]{:S(2)}) %collective-permute-start.4) | collective-permute-done | bytes 2490400 | tf_op jit(solution)/shard_map/ppermute | solution.py:566
  169.4 2.8 %other_half.1 = (f32[1024,1024]{1,0:T(8,128)}, f32[1024,1024]{1,0:T(8,128)}, f32[32,1024]{1,0:T(8,128)}, f32[32,1024]{1,0:T(8,128)}, f32[1,1024]{1,0:T(1,128)}, /*index=5*/f32[1,1024]{1,0:T(1,128)}) custom-call(s32[1]{0:T(128)} %bitcast.core_ref, s32[1]{0:T(128)} %bitcast.1.z_ref, ...), custom_call_target="tpu_custom_call", output_to_operand_aliasing={{0}: (4, {}), {1}: (5, {})} | custom-call | flops 1000000 | bytes 9000000 | tf_op jit(solution)/shard_map/other_half/pallas_call | solution.py:577
  (2 shorter events, 0.0 us)
Async XLA Ops:
  0.6 43.4 %copy-start.8 = (s32[512]{0:T(512)S(1)}, s32[512]{0:T(512)}, u32[]{:S(2)}) copy-start(s32[512]{0:T(512)} %param.25) | copy-start | bytes 6148
  0.6 43.5 %copy-start.7 = (s32[512,10]{0,1:T(8,128)S(1)}, s32[512,10]{0,1:T(8,128)}, u32[]{:S(2)}) copy-start(s32[512,10]{0,1:T(8,128)} %param.23) | copy-start | bytes 61444
  0.7 43.7 %copy-start.9 = (s32[512]{0:T(512)S(1)}, s32[512]{0:T(512)}, u32[]{:S(2)}) copy-start(s32[512]{0:T(512)} %param.24) | copy-start | bytes 6148
  2.4 53.3 %copy-start.5 = (f32[1024]{0:T(1024)S(1)}, f32[1024]{0:T(1024)}, u32[]{:S(2)}) copy-start(f32[1024]{0:T(1024)} %param.22) | copy-start | bytes 12292
  2.4 53.3 %copy-start.6 = (f32[1024]{0:T(1024)S(1)}, f32[1024]{0:T(1024)}, u32[]{:S(2)}) copy-start(f32[1024]{0:T(1024)} %param.28) | copy-start | bytes 12292
  2.4 27.9 %collective-permute-start = (bf16[64,1024]{1,0:T(8,128)(2,1)S(1)}, bf16[64,1024]{1,0:T(8,128)(2,1)S(1)}, u32[]{:S(2)}, u32[]{:S(2)}) collective-permute-start(bf16[64,1024]{1,0:T(8,128)(2,1)S(1)} %constant_dynamic-update-slice_fusion), channel_id=1, source_target_pairs={{0,32},{32,0},{64,96},{96,64},{1,33},{33,1},{65,97},{97,65},{2,34}... | collective-permute-start | bytes 393224 | tf_op jit(solution)/shard_map/ppermute | solution.py:591
  30.4 25.3 %all-to-all-start = ((bf16[128,16,128]{2,1,0:T(8,128)(2,1)}), bf16[128,16,128]{2,1,0:T(8,128)(2,1)S(1)}, u32[]{:S(2)}, u32[]{:S(2)}) async-start(bf16[128,16,128]{2,1,0:T(8,128)(2,1)} %aggregate.1), calls=%async_computation | async-start | bytes 1048576 | tf_op jit(solution)/shard_map/all_to_all | solution.py:601
  40.7 14.9 %collective-permute-start.1 = (bf16[128,1024]{1,0:T(8,128)(2,1)S(1)}, bf16[128,1024]{1,0:T(8,128)(2,1)S(1)}, u32[]{:S(2)}, u32[]{:S(2)}) collective-permute-start(bf16[128,1024]{1,0:T(8,128)(2,1)S(1)} %pad_maximum_fusion.pair_ref), channel_id=1, source_target_pairs={{0,96},{96,0},{32,64},{64,32},{1,97},{97,1},{33,65},{65,33},{2,98}... | collective-permute-start | bytes 786440 | tf_op jit(solution)/shard_map/ppermute | solution.py:597
  52.5 1.3 copy-start.2
  53.9 1.3 copy-start.4
  55.7 15.7 %copy-start = (bf16[1024,1024]{1,0:T(8,128)(2,1)S(1)}, bf16[1024,1024]{1,0:T(8,128)(2,1)}, u32[]{:S(2)}) copy-start(bf16[1024,1024]{1,0:T(8,128)(2,1)} %root_ref.1) | copy-start | bytes 6291460
  55.7 15.7 %copy-start.1 = (bf16[1024,1024]{1,0:T(8,128)(2,1)S(1)}, bf16[1024,1024]{1,0:T(8,128)(2,1)}, u32[]{:S(2)}) copy-start(bf16[1024,1024]{1,0:T(8,128)(2,1)} %near_ref.1) | copy-start | bytes 6291460
  55.7 15.7 %copy-start.3 = (bf16[1024,1024]{1,0:T(8,128)(2,1)S(1)}, bf16[1024,1024]{1,0:T(8,128)(2,1)}, u32[]{:S(2)}) copy-start(bf16[1024,1024]{1,0:T(8,128)(2,1)} %copy-done.2) | copy-start | bytes 6291460
  70.2 10.7 %collective-permute-start.2 = (bf16[64,128,128]{2,1,0:T(8,128)(2,1)S(1)}, bf16[64,128,128]{2,1,0:T(8,128)(2,1)S(1)}, u32[]{:S(2)}, u32[]{:S(2)}) collective-permute-start(bf16[64,128,128]{2,1,0:T(8,128)(2,1)S(1)} %get-tuple-element.34), channel_id=1, source_target_pairs={{0,1},{1,0},{2,3},{3,2},{4,5},{5,4},{6,7},{7,6},{8,9},{9,8},{10,11... | collective-permute-start | bytes 6291464 | tf_op jit(solution)/shard_map/ppermute | solution.py:665
  79.1 1.8 %collective-permute-start.3 = (bf16[64,24,128]{2,1,0:T(8,128)(2,1)S(1)}, bf16[64,24,128]{2,1,0:T(8,128)(2,1)S(1)}, u32[]{:S(2)}, u32[]{:S(2)}) collective-permute-start(bf16[64,24,128]{2,1,0:T(8,128)(2,1)S(1)} %get-tuple-element.40), channel_id=1, source_target_pairs={{0,1},{1,0},{2,3},{3,2},{4,5},{5,4},{6,7},{7,6},{8,9},{9,8},{10,11... | collective-permute-start | bytes 1179656 | tf_op jit(solution)/shard_map/ppermute | solution.py:674
  162.2 7.2 %collective-permute-start.4 = (bf16[64,152,128]{2,1,0:T(8,128)(2,1)S(1)}, bf16[64,152,128]{2,1,0:T(8,128)(2,1)S(1)}, u32[]{:S(2)}, u32[]{:S(2)}) collective-permute-start(bf16[64,152,128]{2,1,0:T(8,128)(2,1)S(1)} %all_to_all.16.kept_ref), channel_id=1, source_target_pairs={{0,1},{1,0},{2,3},{3,2},{4,5},{5,4},{6,7},{7,6},{8,9},{9,8},{10,11... | collective-permute-start | bytes 7471112 | tf_op jit(solution)/shard_map/ppermute | solution.py:566

commit v9 on v8

--- a/solution.py
+++ b/solution.py
@@ -24,6 +24,8 @@
 
 
 def lanes_at(at, size=LANES):
+    if isinstance(at, int):
+        return slice(at * size, (at + 1) * size)
     return pl.ds(pl.multiple_of(at * size, size), size)
 
 
@@ -373,9 +375,7 @@
         hidden[:, cols] = value.astype(jnp.bfloat16)
         return carry
 
-    lax.fori_loop(0, hidden_width // tile, first_layer, 0)
     inverse = 1.0 / count_ref[...].astype(jnp.float32)
-    copies[0].wait()
 
     def select(t, carry):
         cols = lanes_at(t, tile)
@@ -384,7 +384,12 @@
         rows[nodes:, cols] = (total * inverse).astype(jnp.bfloat16)
         return carry
 
-    lax.fori_loop(0, hidden_width // tile, select, 0)
+    first_layer(0, 0)
+    copies[0].wait()
+    for t in range(1, hidden_width // tile):
+        first_layer(t, 0)
+        select(t - 1, 0)
+    select(hidden_width // tile - 1, 0)
     for copy in copies[1:]:
         copy.wait()
 
@@ -400,7 +405,8 @@
         bias_grad[0:1, cols] = jnp.sum(grad.astype(jnp.float32), axis=0, keepdims=True)
         return carry
 
-    lax.fori_loop(0, hidden_width // tile, second_layer, 0)
+    for t in range(hidden_width // tile):
+        second_layer(t, 0)
     start = (core_ref[0] ^ 1) * nodes
 
     def weight_grads(t, carry):
@@ -461,10 +467,10 @@
         grad = table_grad * (1.0 - jnp.exp(-hidden_ref[:, cols].astype(jnp.float32)))
         grad = grad.astype(jnp.bfloat16)
         bias_grads[1:2, cols] = jnp.sum(grad.astype(jnp.float32), axis=0, keepdims=True)
-        for place, to_ref in enumerate((kept_ref, sent_ref)):
-            which = core ^ place
-            left = inputs_flip_ref[pl.ds(pl.multiple_of(which * LANES, LANES), LANES), :]
-            product = matmul(left, grad).astype(jnp.bfloat16)
+        product = matmul(inputs_flip_ref[...], grad).astype(jnp.bfloat16)
+        low, high = product[:LANES], product[LANES:]
+        mine, partner = jnp.where(core == 0, low, high), jnp.where(core == 0, high, low)
+        for to_ref, product in ((kept_ref, mine), (sent_ref, partner)):
             for c in range(8):
                 for lane in range(tile // LANES):
                     chunk = c * 8 + t * (tile // LANES) + lane
@@ -473,7 +479,8 @@
                     ]
         return carry
 
-    lax.fori_loop(0, hidden_width // tile, first_grads, 0)
+    for t in range(hidden_width // tile):
+        first_grads(t, 0)
     for place, to_ref in enumerate((kept_ref, sent_ref)):
         which = core ^ place
         to_ref[:, 16:, :] = jnp.zeros((to_ref.shape[0], 8, LANES), jnp.bfloat16)

time: 173 us -> 172 us (level)
  no operation moved by 1% of the time
where the time goes in v9:
time: 172 us
  blocking collectives  78.7 us (46%)
  Pallas kernels  61.1 us (36%)
  starting transfers between devices  20.3 us (12%)
  local copies, waits for them, and re-layouts  5.12 us (3%)
  waiting for transfers between devices  4.4 us (3%)
    all_to_all x2, blocking collectives, exchange(): return lax.all_to_all(value, axes, split_axis=0, concat_axis=0, tiled=True)  78.7 us
    pallas_call x1, Pallas kernels, aggregate(): pl.pallas_call(aggregate_kernel, out_shape=jax.ShapeDtypeStruct((owners,...  24.5 us
    pallas_call x1, Pallas kernels, step(): call(forward_kernel, (shaped(nodes, hidden_width), shaped(64, LANES, LANE...  13.3 us
    all_to_all x1, starting transfers between devices, exchange(): return lax.all_to_all(value, axes, split_axis=0, concat_axis=0, tiled=True)  10.3 us
    pallas_call x1, Pallas kernels, step(): call(backward_kernel, (shaped(64, 24, LANES), shaped(64, 24, LANES)), 9,...  8.38 us
    pallas_call x1, Pallas kernels, picks(): pl.pallas_call(picks_kernel, out_shape=(jax.ShapeDtypeStruct((2 * nodes,...  8.03 us
    unnamed x22, local copies, waits for them, and re-layouts  3.67 us
  transfers between devices with their start and end apart: 6, of which 3 were waited for; matrix products, arithmetic and copies ran while one was open for 1% of the time, Pallas kernels for 25%

profile of v9, /device:TPU:1, one launch (start us, length us, event | category | flops | bytes accessed | tf_op | source)
XLA Modules:
  0.0 172.0 jit_solution(13682978647680021114)
XLA Ops:
  0.6 0.0 copy-start.8
  0.6 0.0 copy-start.7
  0.7 0.0 copy-start.9
  0.7 0.9 constant_dynamic-update-slice_fusion.1
  1.5 0.8 constant_dynamic-update-slice_fusion
  2.4 0.0 copy-start.5
  2.4 0.0 copy-start.6
  2.4 2.5 %collective-permute-start = (bf16[64,1024]{1,0:T(8,128)(2,1)S(1)}, bf16[64,1024]{1,0:T(8,128)(2,1)S(1)}, u32[]{:S(2)}, u32[]{:S(2)}) collective-permute-start(bf16[64,1024]{1,0:T(8,128)(2,1)S(1)} %constant_dynamic-update-slice_fusion), channel_id=1, source_target_pairs={{0,32},{32,0},{64,96},{96,64},{1,33},{33,1},{65,97},{97,65},{2,34}... | collective-permute-start | bytes 393224 | tf_op jit(solution)/shard_map/ppermute | solution.py:598
  4.9 0.9 add_bitcast_fusion.adj_ref
  5.8 24.5 %aggregate.1 = bf16[128,16,128]{2,1,0:T(8,128)(2,1)} custom-call(s32[16,2048]{1,0:T(8,128)S(1)} %add_bitcast_fusion.adj_ref, bf16[32,4096]{1,0:T(8,128)(2,1)} %feat_hbm.1, s32[1,2048]{1,0:T(1,128)} %bitcast.15, s32[1,2048]{1,0:T(1,128)} %bitcast.16), custom_call_target="tpu_custom_call" | custom-call | flops 40000000 | bytes 3000000 | tf_op jit(solution)/shard_map/aggregate/pallas_call | solution.py:229
  30.3 0.0 collective-permute-done
  30.4 10.3 %all-to-all-start = ((bf16[128,16,128]{2,1,0:T(8,128)(2,1)}), bf16[128,16,128]{2,1,0:T(8,128)(2,1)S(1)}, u32[]{:S(2)}, u32[]{:S(2)}) async-start(bf16[128,16,128]{2,1,0:T(8,128)(2,1)} %aggregate.1), calls=%async_computation | async-start | bytes 1048576 | tf_op jit(solution)/shard_map/all_to_all | solution.py:608
  40.7 3.3 %collective-permute-start.1 = (bf16[128,1024]{1,0:T(8,128)(2,1)S(1)}, bf16[128,1024]{1,0:T(8,128)(2,1)S(1)}, u32[]{:S(2)}, u32[]{:S(2)}) collective-permute-start(bf16[128,1024]{1,0:T(8,128)(2,1)S(1)} %pad_maximum_fusion.pair_ref), channel_id=1, source_target_pairs={{0,96},{96,0},{32,64},{64,32},{1,97},{97,1},{33,65},{65,33},{2,98}... | collective-permute-start | bytes 786440 | tf_op jit(solution)/shard_map/ppermute | solution.py:604
  44.0 0.0 copy-done.8
  44.0 0.1 copy.28.count_ref
  44.2 0.0 copy-done.7
  44.2 0.1 copy.25.adj_ref
  44.3 0.0 copy-done.9
  44.3 0.1 copy.26.center_ref
  44.5 8.0 %picks.1 = (bf16[1024,1024]{1,0:T(8,128)(2,1)S(1)}, bf16[1024,1024]{1,0:T(8,128)(2,1)S(1)}) custom-call(s32[512,10]{1,0:T(8,128)S(1)} %copy.25.adj_ref, s32[512,1]{1,0:T(8,128)S(1)} %copy.26.center_ref, s32[512,1]{1,0:T(8,128)S(1)} %copy.28.count_ref), custom_call_target="tpu_custom_call" | custom-call | flops 20000000 | bytes 5000000 | tf_op jit(solution)/shard_map/picks/pallas_call | solution.py:290
  52.5 0.0 copy-start.2
  52.5 1.3 copy-done.2
  53.9 0.0 copy-start.4
  53.9 1.3 copy-done.4
  55.2 0.5 collective-permute-done.1.other_pair_ref
  55.6 0.0 all-to-all-done.arrived_ref
  55.7 0.0 copy-done.5
  55.7 0.0 copy-done.6
  55.7 0.0 copy-start
  55.7 0.0 copy-start.1
  55.7 0.0 copy-start.3
  55.7 13.3 %shard_map.198 = (bf16[512,1024]{1,0:T(8,128)(2,1)}, bf16[64,128,128]{2,1,0:T(8,128)(2,1)S(1)}, bf16[1024,1024]{1,0:T(8,128)(2,1)S(1)}, bf16[1024,1024]{1,0:T(8,...) custom-call(s32[1]{0:T(128)} %bitcast.core_ref, ...), custom_call_target="tpu_custom_call" | custom-call | flops 6000000000 | bytes 18000000 | tf_op jit(solution)/shard_map/pallas_call | solution.py:642
  69.0 1.3 collective-permute-start.2
  70.3 0.0 copy-done
  70.3 0.0 copy-done.1
  70.3 0.0 copy-done.3
  70.3 8.4 %shard_map.199 = (bf16[64,24,128]{2,1,0:T(8,128)(2,1)S(1)}, bf16[64,24,128]{2,1,0:T(8,128)(2,1)S(1)}) custom-call(s32[1]{0:T(128)} %bitcast.core_ref, bf16[512,1024]{1,0:T(8,128)(2,1)S(1)} %get-tuple-element.33.slope_ref, bf16[1024,1024]{1,0:T(8,128)(2,1)S(1)} %copy-done, bf16[1024,1024]{1,0:T(8,128)(2,1)S(1)} %copy-done.1, s32[512,1]{1,0:T(8,128)S(1)} %copy.28.count_ref, ...), custom_call_target="tpu_custom_call" | custom-call | flops 4700000256 | bytes 12000000 | tf_op jit(solution)/shard_map/pallas_call | solution.py:673
  78.7 0.1 collective-permute-start.3
  78.8 1.7 collective-permute-done.3.received_one_ref
  80.5 0.0 collective-permute-done.2.received_ref
  80.5 2.0 %shard_map.200 = bf16[64,152,128]{2,1,0:T(8,128)(2,1)S(1)} custom-call(s32[1]{0:T(128)} %bitcast.core_ref, bf16[1024,1024]{1,0:T(8,128)(2,1)S(1)} %get-tuple-element.32.rows_ref, bf16[512,1024]{1,0:T(8,128)(2,1)S(1)} %get-tuple-element.33.slope_ref, bf16[64,128,128]{2,1,0:T(8,128)(2,1)S(1)} %collective-permute-done.2.received_ref, ...), custom_call_target="tpu_custom_call" | custom-call | flops 1000000000 | bytes 7000000 | tf_op jit(solution)/shard_map/pallas_call | solution.py:682
  82.5 40.7 %all_to_all.15 = bf16[64,152,128]{2,1,0:T(8,128)(2,1)S(1)} all-to-all(bf16[64,152,128]{2,1,0:T(8,128)(2,1)S(1)} %shard_map.200), channel_id=1, replica_groups=mesh['z'=4,'x'=4,'y'=4,'core'=2] {'z','x','y'}, dimensions={0} | all-to-all | bytes 4980736 | tf_op jit(solution)/shard_map/all_to_all | solution.py:608
  123.2 0.4 reduce_sum.12
  123.5 0.3 broadcast_in_dim.43
  123.8 38.0 %all_to_all.16.kept_ref = bf16[64,152,128]{2,1,0:T(8,128)(2,1)S(1)} all-to-all(bf16[64,152,128]{2,1,0:T(8,128)(2,1)S(1)} %broadcast_in_dim.43), channel_id=1, replica_groups=mesh['z'=4,'x'=4,'y'=4,'core'=2] {'z','x','y'}, dimensions={0} | all-to-all | bytes 4980736 | tf_op jit(solution)/shard_map/all_to_all | solution.py:608
  161.8 2.8 %collective-permute-start.4 = (bf16[64,152,128]{2,1,0:T(8,128)(2,1)S(1)}, bf16[64,152,128]{2,1,0:T(8,128)(2,1)S(1)}, u32[]{:S(2)}, u32[]{:S(2)}) collective-permute-start(bf16[64,152,128]{2,1,0:T(8,128)(2,1)S(1)} %all_to_all.16.kept_ref), channel_id=1, source_target_pairs={{0,1},{1,0},{2,3},{3,2},{4,5},{5,4},{6,7},{7,6},{8,9},{9,8},{10,11... | collective-permute-start | bytes 7471112 | tf_op jit(solution)/shard_map/ppermute | solution.py:573
  164.6 2.1 %own_half.1 = (f32[1024,1024]{1,0:T(8,128)}, f32[1024,1024]{1,0:T(8,128)}) custom-call(s32[1]{0:T(128)} %bitcast.core_ref, bf16[64,152,128]{2,1,0:T(8,128)(2,1)S(1)} %all_to_all.16.kept_ref), custom_call_target="tpu_custom_call" | custom-call | flops 1000000 | bytes 7000000 | tf_op jit(solution)/shard_map/own_half/pallas_call | solution.py:574
  166.8 2.2 %collective-permute-done.4.other_ref = bf16[64,152,128]{2,1,0:T(8,128)(2,1)S(1)} collective-permute-done((bf16[64,152,128]{2,1,0:T(8,128)(2,1)S(1)}, bf16[64,152,128]{2,1,0:T(8,128)(2,1)S(1)}, u32[]{:S(2)}, u32[]{:S(2)}) %collective-permute-start.4) | collective-permute-done | bytes 2490400 | tf_op jit(solution)/shard_map/ppermute | solution.py:573
  169.0 2.8 %other_half.1 = (f32[1024,1024]{1,0:T(8,128)}, f32[1024,1024]{1,0:T(8,128)}, f32[32,1024]{1,0:T(8,128)}, f32[32,1024]{1,0:T(8,128)}, f32[1,1024]{1,0:T(1,128)}, /*index=5*/f32[1,1024]{1,0:T(1,128)}) custom-call(s32[1]{0:T(128)} %bitcast.core_ref, s32[1]{0:T(128)} %bitcast.1.z_ref, ...), custom_call_target="tpu_custom_call", output_to_operand_aliasing={{0}: (4, {}), {1}: (5, {})} | custom-call | flops 1000000 | bytes 9000000 | tf_op jit(solution)/shard_map/other_half/pallas_call | solution.py:584
  (2 shorter events, 0.0 us)
Async XLA Ops:
  0.6 43.4 %copy-start.8 = (s32[512]{0:T(512)S(1)}, s32[512]{0:T(512)}, u32[]{:S(2)}) copy-start(s32[512]{0:T(512)} %param.25) | copy-start | bytes 6148
  0.6 43.5 %copy-start.7 = (s32[512,10]{0,1:T(8,128)S(1)}, s32[512,10]{0,1:T(8,128)}, u32[]{:S(2)}) copy-start(s32[512,10]{0,1:T(8,128)} %param.23) | copy-start | bytes 61444
  0.7 43.7 %copy-start.9 = (s32[512]{0:T(512)S(1)}, s32[512]{0:T(512)}, u32[]{:S(2)}) copy-start(s32[512]{0:T(512)} %param.24) | copy-start | bytes 6148
  2.4 53.3 %copy-start.5 = (f32[1024]{0:T(1024)S(1)}, f32[1024]{0:T(1024)}, u32[]{:S(2)}) copy-start(f32[1024]{0:T(1024)} %param.22) | copy-start | bytes 12292
  2.4 53.3 %copy-start.6 = (f32[1024]{0:T(1024)S(1)}, f32[1024]{0:T(1024)}, u32[]{:S(2)}) copy-start(f32[1024]{0:T(1024)} %param.28) | copy-start | bytes 12292
  2.4 27.9 %collective-permute-start = (bf16[64,1024]{1,0:T(8,128)(2,1)S(1)}, bf16[64,1024]{1,0:T(8,128)(2,1)S(1)}, u32[]{:S(2)}, u32[]{:S(2)}) collective-permute-start(bf16[64,1024]{1,0:T(8,128)(2,1)S(1)} %constant_dynamic-update-slice_fusion), channel_id=1, source_target_pairs={{0,32},{32,0},{64,96},{96,64},{1,33},{33,1},{65,97},{97,65},{2,34}... | collective-permute-start | bytes 393224 | tf_op jit(solution)/shard_map/ppermute | solution.py:598
  30.4 25.3 %all-to-all-start = ((bf16[128,16,128]{2,1,0:T(8,128)(2,1)}), bf16[128,16,128]{2,1,0:T(8,128)(2,1)S(1)}, u32[]{:S(2)}, u32[]{:S(2)}) async-start(bf16[128,16,128]{2,1,0:T(8,128)(2,1)} %aggregate.1), calls=%async_computation | async-start | bytes 1048576 | tf_op jit(solution)/shard_map/all_to_all | solution.py:608
  40.7 14.9 %collective-permute-start.1 = (bf16[128,1024]{1,0:T(8,128)(2,1)S(1)}, bf16[128,1024]{1,0:T(8,128)(2,1)S(1)}, u32[]{:S(2)}, u32[]{:S(2)}) collective-permute-start(bf16[128,1024]{1,0:T(8,128)(2,1)S(1)} %pad_maximum_fusion.pair_ref), channel_id=1, source_target_pairs={{0,96},{96,0},{32,64},{64,32},{1,97},{97,1},{33,65},{65,33},{2,98}... | collective-permute-start | bytes 786440 | tf_op jit(solution)/shard_map/ppermute | solution.py:604
  52.5 1.3 copy-start.2
  53.9 1.3 copy-start.4
  55.7 14.7 %copy-start = (bf16[1024,1024]{1,0:T(8,128)(2,1)S(1)}, bf16[1024,1024]{1,0:T(8,128)(2,1)}, u32[]{:S(2)}) copy-start(bf16[1024,1024]{1,0:T(8,128)(2,1)} %root_ref.1) | copy-start | bytes 6291460
  55.7 14.6 %copy-start.1 = (bf16[1024,1024]{1,0:T(8,128)(2,1)S(1)}, bf16[1024,1024]{1,0:T(8,128)(2,1)}, u32[]{:S(2)}) copy-start(bf16[1024,1024]{1,0:T(8,128)(2,1)} %near_ref.1) | copy-start | bytes 6291460
  55.7 14.6 %copy-start.3 = (bf16[1024,1024]{1,0:T(8,128)(2,1)S(1)}, bf16[1024,1024]{1,0:T(8,128)(2,1)}, u32[]{:S(2)}) copy-start(bf16[1024,1024]{1,0:T(8,128)(2,1)} %copy-done.2) | copy-start | bytes 6291460
  69.0 11.5 %collective-permute-start.2 = (bf16[64,128,128]{2,1,0:T(8,128)(2,1)S(1)}, bf16[64,128,128]{2,1,0:T(8,128)(2,1)S(1)}, u32[]{:S(2)}, u32[]{:S(2)}) collective-permute-start(bf16[64,128,128]{2,1,0:T(8,128)(2,1)S(1)} %get-tuple-element.34), channel_id=1, source_target_pairs={{0,1},{1,0},{2,3},{3,2},{4,5},{5,4},{6,7},{7,6},{8,9},{9,8},{10,11... | collective-permute-start | bytes 6291464 | tf_op jit(solution)/shard_map/ppermute | solution.py:672
  78.7 1.8 %collective-permute-start.3 = (bf16[64,24,128]{2,1,0:T(8,128)(2,1)S(1)}, bf16[64,24,128]{2,1,0:T(8,128)(2,1)S(1)}, u32[]{:S(2)}, u32[]{:S(2)}) collective-permute-start(bf16[64,24,128]{2,1,0:T(8,128)(2,1)S(1)} %get-tuple-element.40), channel_id=1, source_target_pairs={{0,1},{1,0},{2,3},{3,2},{4,5},{5,4},{6,7},{7,6},{8,9},{9,8},{10,11... | collective-permute-start | bytes 1179656 | tf_op jit(solution)/shard_map/ppermute | solution.py:681
  161.8 7.2 %collective-permute-start.4 = (bf16[64,152,128]{2,1,0:T(8,128)(2,1)S(1)}, bf16[64,152,128]{2,1,0:T(8,128)(2,1)S(1)}, u32[]{:S(2)}, u32[]{:S(2)}) collective-permute-start(bf16[64,152,128]{2,1,0:T(8,128)(2,1)S(1)} %all_to_all.16.kept_ref), channel_id=1, source_target_pairs={{0,1},{1,0},{2,3},{3,2},{4,5},{5,4},{6,7},{7,6},{8,9},{9,8},{10,11... | collective-permute-start | bytes 7471112 | tf_op jit(solution)/shard_map/ppermute | solution.py:573

commit v10 on v9

--- a/solution.py
+++ b/solution.py
@@ -139,7 +139,7 @@
     def one_group(g, carry):
         count = counts[g]
 
-        def four(s, total, first):
+        def four(s, total):
             total = list(total)
             for j in range(4):
                 at = index[g * steps + s, j : j + 1, :]
@@ -149,18 +149,18 @@
                     lambda c, v: feat_ref[v * 16 : (v + 1) * 16, c * LANES : (c + 1) * LANES],
                     high, low, chunks, parts,
                 )
-                if first and j == 0:
+                valid = jnp.broadcast_to(s * 4 + j <= count, (16, LANES))
+                if j == 0:
+                    valid = valid & (s > 0)
                     for v in range(parts):
-                        rows[v * 16 : (v + 1) * 16, lanes_at(g)] = found[v]
-                    continue
-                valid = jnp.broadcast_to(s * 4 + j <= count, (16, LANES))
+                        held = rows[v * 16 : (v + 1) * 16, lanes_at(g)]
+                        rows[v * 16 : (v + 1) * 16, lanes_at(g)] = jnp.where(s == 0, found[v], held)
                 for v in range(parts):
                     total[v] = total[v] + jnp.where(valid, found[v].astype(f32), 0.0)
             return tuple(total)
 
-        total = four(0, (jnp.zeros((16, LANES), f32),) * parts, True)
         needed = lax.shift_right_logical(jnp.max(count) + 4, 2)
-        total = lax.fori_loop(1, needed, lambda s, t: four(s, t, False), total)
+        total = lax.fori_loop(0, needed, four, (jnp.zeros((16, LANES), f32),) * parts)
         divisor = jnp.broadcast_to(count.astype(f32), (16, LANES))
         for v in range(parts):
             near = (total[v] / divisor).astype(bf16)
@@ -479,8 +479,7 @@
                     ]
         return carry
 
-    for t in range(hidden_width // tile):
-        first_grads(t, 0)
+    lax.fori_loop(0, hidden_width // tile, first_grads, 0)
     for place, to_ref in enumerate((kept_ref, sent_ref)):
         which = core ^ place
         to_ref[:, 16:, :] = jnp.zeros((to_ref.shape[0], 8, LANES), jnp.bfloat16)

time: 172 us -> 173 us (level)
  no operation moved by 1% of the time
where the time goes in v10:
time: 173 us
  blocking collectives  78.7 us (45%)
  Pallas kernels  61.7 us (36%)
  starting transfers between devices  20.3 us (12%)
  local copies, waits for them, and re-layouts  5.12 us (3%)
  waiting for transfers between devices  4.4 us (3%)
    all_to_all x2, blocking collectives, exchange(): return lax.all_to_all(value, axes, split_axis=0, concat_axis=0, tiled=True)  78.7 us
    pallas_call x1, Pallas kernels, aggregate(): pl.pallas_call(aggregate_kernel, out_shape=jax.ShapeDtypeStruct((owners,...  26 us
    pallas_call x1, Pallas kernels, step(): call(forward_kernel, (shaped(nodes, hidden_width), shaped(64, LANES, LANE...  13.3 us
    all_to_all x1, starting transfers between devices, exchange(): return lax.all_to_all(value, axes, split_axis=0, concat_axis=0, tiled=True)  10.3 us
    pallas_call x1, Pallas kernels, picks(): pl.pallas_call(picks_kernel, out_shape=(jax.ShapeDtypeStruct((2 * nodes,...  8.03 us
    pallas_call x1, Pallas kernels, step(): call(backward_kernel, (shaped(64, 24, LANES), shaped(64, 24, LANES)), 9,...  7.45 us
    unnamed x22, local copies, waits for them, and re-layouts  3.67 us
  transfers between devices with their start and end apart: 6, of which 3 were waited for; matrix products, arithmetic and copies ran while one was open for 1% of the time, Pallas kernels for 25%

profile of v10, /device:TPU:1, one launch (start us, length us, event | category | flops | bytes accessed | tf_op | source)
XLA Modules:
  0.0 172.5 jit_solution(11566230211573488580)
XLA Ops:
  0.6 0.0 copy-start.8
  0.6 0.0 copy-start.7
  0.7 0.0 copy-start.9
  0.7 0.9 constant_dynamic-update-slice_fusion.1
  1.5 0.8 constant_dynamic-update-slice_fusion
  2.4 0.0 copy-start.5
  2.4 0.0 copy-start.6
  2.4 2.5 %collective-permute-start = (bf16[64,1024]{1,0:T(8,128)(2,1)S(1)}, bf16[64,1024]{1,0:T(8,128)(2,1)S(1)}, u32[]{:S(2)}, u32[]{:S(2)}) collective-permute-start(bf16[64,1024]{1,0:T(8,128)(2,1)S(1)} %constant_dynamic-update-slice_fusion), channel_id=1, source_target_pairs={{0,32},{32,0},{64,96},{96,64},{1,33},{33,1},{65,97},{97,65},{2,34}... | collective-permute-start | bytes 393224 | tf_op jit(solution)/shard_map/ppermute | solution.py:597
  4.9 0.9 add_bitcast_fusion.adj_ref
  5.8 26.0 %aggregate.1 = bf16[128,16,128]{2,1,0:T(8,128)(2,1)} custom-call(s32[16,2048]{1,0:T(8,128)S(1)} %add_bitcast_fusion.adj_ref, bf16[32,4096]{1,0:T(8,128)(2,1)} %feat_hbm.1, s32[1,2048]{1,0:T(1,128)} %bitcast.15, s32[1,2048]{1,0:T(1,128)} %bitcast.16), custom_call_target="tpu_custom_call" | custom-call | flops 40000000 | bytes 3000000 | tf_op jit(solution)/shard_map/aggregate/pallas_call | solution.py:229
  31.8 0.0 collective-permute-done
  31.9 10.3 %all-to-all-start = ((bf16[128,16,128]{2,1,0:T(8,128)(2,1)}), bf16[128,16,128]{2,1,0:T(8,128)(2,1)S(1)}, u32[]{:S(2)}, u32[]{:S(2)}) async-start(bf16[128,16,128]{2,1,0:T(8,128)(2,1)} %aggregate.1), calls=%async_computation | async-start | bytes 1048576 | tf_op jit(solution)/shard_map/all_to_all | solution.py:607
  42.2 3.3 %collective-permute-start.1 = (bf16[128,1024]{1,0:T(8,128)(2,1)S(1)}, bf16[128,1024]{1,0:T(8,128)(2,1)S(1)}, u32[]{:S(2)}, u32[]{:S(2)}) collective-permute-start(bf16[128,1024]{1,0:T(8,128)(2,1)S(1)} %pad_maximum_fusion.pair_ref), channel_id=1, source_target_pairs={{0,96},{96,0},{32,64},{64,32},{1,97},{97,1},{33,65},{65,33},{2,98}... | collective-permute-start | bytes 786440 | tf_op jit(solution)/shard_map/ppermute | solution.py:603
  45.5 0.0 copy-done.8
  45.5 0.1 copy.28.count_ref
  45.7 0.0 copy-done.7
  45.7 0.1 copy.25.adj_ref
  45.8 0.0 copy-done.9
  45.8 0.1 copy.26.center_ref
  46.0 8.0 %picks.1 = (bf16[1024,1024]{1,0:T(8,128)(2,1)S(1)}, bf16[1024,1024]{1,0:T(8,128)(2,1)S(1)}) custom-call(s32[512,10]{1,0:T(8,128)S(1)} %copy.25.adj_ref, s32[512,1]{1,0:T(8,128)S(1)} %copy.26.center_ref, s32[512,1]{1,0:T(8,128)S(1)} %copy.28.count_ref), custom_call_target="tpu_custom_call" | custom-call | flops 20000000 | bytes 5000000 | tf_op jit(solution)/shard_map/picks/pallas_call | solution.py:290
  54.0 0.0 copy-start.2
  54.0 1.3 copy-done.2
  55.3 0.0 copy-start.4
  55.4 1.3 copy-done.4
  56.7 0.5 collective-permute-done.1.other_pair_ref
  57.1 0.0 all-to-all-done.arrived_ref
  57.1 0.0 copy-done.5
  57.1 0.0 copy-done.6
  57.1 0.0 copy-start
  57.2 0.0 copy-start.1
  57.2 0.0 copy-start.3
  57.2 13.3 %shard_map.198 = (bf16[512,1024]{1,0:T(8,128)(2,1)}, bf16[64,128,128]{2,1,0:T(8,128)(2,1)S(1)}, bf16[1024,1024]{1,0:T(8,128)(2,1)S(1)}, bf16[1024,1024]{1,0:T(8,...) custom-call(s32[1]{0:T(128)} %bitcast.core_ref, ...), custom_call_target="tpu_custom_call" | custom-call | flops 6000000000 | bytes 18000000 | tf_op jit(solution)/shard_map/pallas_call | solution.py:641
  70.5 1.3 collective-permute-start.2
  71.8 0.0 copy-done
  71.8 0.0 copy-done.1
  71.8 0.0 copy-done.3
  71.8 7.5 %shard_map.199 = (bf16[64,24,128]{2,1,0:T(8,128)(2,1)S(1)}, bf16[64,24,128]{2,1,0:T(8,128)(2,1)S(1)}) custom-call(s32[1]{0:T(128)} %bitcast.core_ref, bf16[512,1024]{1,0:T(8,128)(2,1)S(1)} %get-tuple-element.33.slope_ref, bf16[1024,1024]{1,0:T(8,128)(2,1)S(1)} %copy-done, bf16[1024,1024]{1,0:T(8,128)(2,1)S(1)} %copy-done.1, s32[512,1]{1,0:T(8,128)S(1)} %copy.28.count_ref, ...), custom_call_target="tpu_custom_call" | custom-call | flops 4700000256 | bytes 12000000 | tf_op jit(solution)/shard_map/pallas_call | solution.py:672
  79.3 0.1 collective-permute-start.3
  79.4 1.7 collective-permute-done.3.received_one_ref
  81.1 0.0 collective-permute-done.2.received_ref
  81.1 2.0 %shard_map.200 = bf16[64,152,128]{2,1,0:T(8,128)(2,1)S(1)} custom-call(s32[1]{0:T(128)} %bitcast.core_ref, bf16[1024,1024]{1,0:T(8,128)(2,1)S(1)} %get-tuple-element.32.rows_ref, bf16[512,1024]{1,0:T(8,128)(2,1)S(1)} %get-tuple-element.33.slope_ref, bf16[64,128,128]{2,1,0:T(8,128)(2,1)S(1)} %collective-permute-done.2.received_ref, ...), custom_call_target="tpu_custom_call" | custom-call | flops 1000000000 | bytes 7000000 | tf_op jit(solution)/shard_map/pallas_call | solution.py:681
  83.1 40.7 %all_to_all.15 = bf16[64,152,128]{2,1,0:T(8,128)(2,1)S(1)} all-to-all(bf16[64,152,128]{2,1,0:T(8,128)(2,1)S(1)} %shard_map.200), channel_id=1, replica_groups=mesh['z'=4,'x'=4,'y'=4,'core'=2] {'z','x','y'}, dimensions={0} | all-to-all | bytes 4980736 | tf_op jit(solution)/shard_map/all_to_all | solution.py:607
  123.7 0.4 reduce_sum.12
  124.1 0.3 broadcast_in_dim.43
  124.4 38.0 %all_to_all.16.kept_ref = bf16[64,152,128]{2,1,0:T(8,128)(2,1)S(1)} all-to-all(bf16[64,152,128]{2,1,0:T(8,128)(2,1)S(1)} %broadcast_in_dim.43), channel_id=1, replica_groups=mesh['z'=4,'x'=4,'y'=4,'core'=2] {'z','x','y'}, dimensions={0} | all-to-all | bytes 4980736 | tf_op jit(solution)/shard_map/all_to_all | solution.py:607
  162.4 2.8 %collective-permute-start.4 = (bf16[64,152,128]{2,1,0:T(8,128)(2,1)S(1)}, bf16[64,152,128]{2,1,0:T(8,128)(2,1)S(1)}, u32[]{:S(2)}, u32[]{:S(2)}) collective-permute-start(bf16[64,152,128]{2,1,0:T(8,128)(2,1)S(1)} %all_to_all.16.kept_ref), channel_id=1, source_target_pairs={{0,1},{1,0},{2,3},{3,2},{4,5},{5,4},{6,7},{7,6},{8,9},{9,8},{10,11... | collective-permute-start | bytes 7471112 | tf_op jit(solution)/shard_map/ppermute | solution.py:572
  165.2 2.1 %own_half.1 = (f32[1024,1024]{1,0:T(8,128)}, f32[1024,1024]{1,0:T(8,128)}) custom-call(s32[1]{0:T(128)} %bitcast.core_ref, bf16[64,152,128]{2,1,0:T(8,128)(2,1)S(1)} %all_to_all.16.kept_ref), custom_call_target="tpu_custom_call" | custom-call | flops 1000000 | bytes 7000000 | tf_op jit(solution)/shard_map/own_half/pallas_call | solution.py:573
  167.3 2.2 %collective-permute-done.4.other_ref = bf16[64,152,128]{2,1,0:T(8,128)(2,1)S(1)} collective-permute-done((bf16[64,152,128]{2,1,0:T(8,128)(2,1)S(1)}, bf16[64,152,128]{2,1,0:T(8,128)(2,1)S(1)}, u32[]{:S(2)}, u32[]{:S(2)}) %collective-permute-start.4) | collective-permute-done | bytes 2490400 | tf_op jit(solution)/shard_map/ppermute | solution.py:572
  169.6 2.8 %other_half.1 = (f32[1024,1024]{1,0:T(8,128)}, f32[1024,1024]{1,0:T(8,128)}, f32[32,1024]{1,0:T(8,128)}, f32[32,1024]{1,0:T(8,128)}, f32[1,1024]{1,0:T(1,128)}, /*index=5*/f32[1,1024]{1,0:T(1,128)}) custom-call(s32[1]{0:T(128)} %bitcast.core_ref, s32[1]{0:T(128)} %bitcast.1.z_ref, ...), custom_call_target="tpu_custom_call", output_to_operand_aliasing={{0}: (4, {}), {1}: (5, {})} | custom-call | flops 1000000 | bytes 9000000 | tf_op jit(solution)/shard_map/other_half/pallas_call | solution.py:583
  (2 shorter events, 0.0 us)
Async XLA Ops:
  0.6 44.9 %copy-start.8 = (s32[512]{0:T(512)S(1)}, s32[512]{0:T(512)}, u32[]{:S(2)}) copy-start(s32[512]{0:T(512)} %param.25) | copy-start | bytes 6148
  0.6 45.0 %copy-start.7 = (s32[512,10]{0,1:T(8,128)S(1)}, s32[512,10]{0,1:T(8,128)}, u32[]{:S(2)}) copy-start(s32[512,10]{0,1:T(8,128)} %param.23) | copy-start | bytes 61444
  0.7 45.2 %copy-start.9 = (s32[512]{0:T(512)S(1)}, s32[512]{0:T(512)}, u32[]{:S(2)}) copy-start(s32[512]{0:T(512)} %param.24) | copy-start | bytes 6148
  2.4 54.8 %copy-start.5 = (f32[1024]{0:T(1024)S(1)}, f32[1024]{0:T(1024)}, u32[]{:S(2)}) copy-start(f32[1024]{0:T(1024)} %param.22) | copy-start | bytes 12292
  2.4 54.8 %copy-start.6 = (f32[1024]{0:T(1024)S(1)}, f32[1024]{0:T(1024)}, u32[]{:S(2)}) copy-start(f32[1024]{0:T(1024)} %param.28) | copy-start | bytes 12292
  2.4 29.4 %collective-permute-start = (bf16[64,1024]{1,0:T(8,128)(2,1)S(1)}, bf16[64,1024]{1,0:T(8,128)(2,1)S(1)}, u32[]{:S(2)}, u32[]{:S(2)}) collective-permute-start(bf16[64,1024]{1,0:T(8,128)(2,1)S(1)} %constant_dynamic-update-slice_fusion), channel_id=1, source_target_pairs={{0,32},{32,0},{64,96},{96,64},{1,33},{33,1},{65,97},{97,65},{2,34}... | collective-permute-start | bytes 393224 | tf_op jit(solution)/shard_map/ppermute | solution.py:597
  31.9 25.3 %all-to-all-start = ((bf16[128,16,128]{2,1,0:T(8,128)(2,1)}), bf16[128,16,128]{2,1,0:T(8,128)(2,1)S(1)}, u32[]{:S(2)}, u32[]{:S(2)}) async-start(bf16[128,16,128]{2,1,0:T(8,128)(2,1)} %aggregate.1), calls=%async_computation | async-start | bytes 1048576 | tf_op jit(solution)/shard_map/all_to_all | solution.py:607
  42.2 14.9 %collective-permute-start.1 = (bf16[128,1024]{1,0:T(8,128)(2,1)S(1)}, bf16[128,1024]{1,0:T(8,128)(2,1)S(1)}, u32[]{:S(2)}, u32[]{:S(2)}) collective-permute-start(bf16[128,1024]{1,0:T(8,128)(2,1)S(1)} %pad_maximum_fusion.pair_ref), channel_id=1, source_target_pairs={{0,96},{96,0},{32,64},{64,32},{1,97},{97,1},{33,65},{65,33},{2,98}... | collective-permute-start | bytes 786440 | tf_op jit(solution)/shard_map/ppermute | solution.py:603
  54.0 1.3 copy-start.2
  55.3 1.3 copy-start.4
  57.1 14.7 %copy-start = (bf16[1024,1024]{1,0:T(8,128)(2,1)S(1)}, bf16[1024,1024]{1,0:T(8,128)(2,1)}, u32[]{:S(2)}) copy-start(bf16[1024,1024]{1,0:T(8,128)(2,1)} %root_ref.1) | copy-start | bytes 6291460
  57.2 14.6 %copy-start.1 = (bf16[1024,1024]{1,0:T(8,128)(2,1)S(1)}, bf16[1024,1024]{1,0:T(8,128)(2,1)}, u32[]{:S(2)}) copy-start(bf16[1024,1024]{1,0:T(8,128)(2,1)} %near_ref.1) | copy-start | bytes 6291460
  57.2 14.6 %copy-start.3 = (bf16[1024,1024]{1,0:T(8,128)(2,1)S(1)}, bf16[1024,1024]{1,0:T(8,128)(2,1)}, u32[]{:S(2)}) copy-start(bf16[1024,1024]{1,0:T(8,128)(2,1)} %copy-done.2) | copy-start | bytes 6291460
  70.5 10.5 %collective-permute-start.2 = (bf16[64,128,128]{2,1,0:T(8,128)(2,1)S(1)}, bf16[64,128,128]{2,1,0:T(8,128)(2,1)S(1)}, u32[]{:S(2)}, u32[]{:S(2)}) collective-permute-start(bf16[64,128,128]{2,1,0:T(8,128)(2,1)S(1)} %get-tuple-element.34), channel_id=1, source_target_pairs={{0,1},{1,0},{2,3},{3,2},{4,5},{5,4},{6,7},{7,6},{8,9},{9,8},{10,11... | collective-permute-start | bytes 6291464 | tf_op jit(solution)/shard_map/ppermute | solution.py:671
  79.3 1.8 %collective-permute-start.3 = (bf16[64,24,128]{2,1,0:T(8,128)(2,1)S(1)}, bf16[64,24,128]{2,1,0:T(8,128)(2,1)S(1)}, u32[]{:S(2)}, u32[]{:S(2)}) collective-permute-start(bf16[64,24,128]{2,1,0:T(8,128)(2,1)S(1)} %get-tuple-element.40), channel_id=1, source_target_pairs={{0,1},{1,0},{2,3},{3,2},{4,5},{5,4},{6,7},{7,6},{8,9},{9,8},{10,11... | collective-permute-start | bytes 1179656 | tf_op jit(solution)/shard_map/ppermute | solution.py:680
  162.4 7.2 %collective-permute-start.4 = (bf16[64,152,128]{2,1,0:T(8,128)(2,1)S(1)}, bf16[64,152,128]{2,1,0:T(8,128)(2,1)S(1)}, u32[]{:S(2)}, u32[]{:S(2)}) collective-permute-start(bf16[64,152,128]{2,1,0:T(8,128)(2,1)S(1)} %all_to_all.16.kept_ref), channel_id=1, source_target_pairs={{0,1},{1,0},{2,3},{3,2},{4,5},{5,4},{6,7},{7,6},{8,9},{9,8},{10,11... | collective-permute-start | bytes 7471112 | tf_op jit(solution)/shard_map/ppermute | solution.py:572

commit v11 on v9

--- a/solution.py
+++ b/solution.py
@@ -384,12 +384,9 @@
         rows[nodes:, cols] = (total * inverse).astype(jnp.bfloat16)
         return carry
 
-    first_layer(0, 0)
+    lax.fori_loop(0, hidden_width // tile, first_layer, 0)
     copies[0].wait()
-    for t in range(1, hidden_width // tile):
-        first_layer(t, 0)
-        select(t - 1, 0)
-    select(hidden_width // tile - 1, 0)
+    lax.fori_loop(0, hidden_width // tile, select, 0)
     for copy in copies[1:]:
         copy.wait()
 
@@ -479,8 +476,7 @@
                     ]
         return carry
 
-    for t in range(hidden_width // tile):
-        first_grads(t, 0)
+    lax.fori_loop(0, hidden_width // tile, first_grads, 0)
     for place, to_ref in enumerate((kept_ref, sent_ref)):
         which = core ^ place
         to_ref[:, 16:, :] = jnp.zeros((to_ref.shape[0], 8, LANES), jnp.bfloat16)

time: 172 us -> 172 us (level)
  no operation moved by 1% of the time
where the time goes in v11:
time: 172 us; the launch traced here: 171 us
  blocking collectives  78.7 us (46%)
  Pallas kernels  60.9 us (35%)
  starting transfers between devices  20.2 us (12%)
  local copies, waits for them, and re-layouts  5.12 us (3%)
  waiting for transfers between devices  4.4 us (3%)
    all_to_all x2, blocking collectives, exchange(): return lax.all_to_all(value, axes, split_axis=0, concat_axis=0, tiled=True)  78.7 us
    pallas_call x1, Pallas kernels, aggregate(): pl.pallas_call(aggregate_kernel, out_shape=jax.ShapeDtypeStruct((owners,...  24.5 us
    pallas_call x1, Pallas kernels, step(): call(forward_kernel, (shaped(nodes, hidden_width), shaped(64, LANES, LANE...  14.1 us
    all_to_all x1, starting transfers between devices, exchange(): return lax.all_to_all(value, axes, split_axis=0, concat_axis=0, tiled=True)  10.3 us
    pallas_call x1, Pallas kernels, picks(): pl.pallas_call(picks_kernel, out_shape=(jax.ShapeDtypeStruct((2 * nodes,...  8.03 us
    pallas_call x1, Pallas kernels, step(): call(backward_kernel, (shaped(64, 24, LANES), shaped(64, 24, LANES)), 9,...  7.45 us
    unnamed x22, local copies, waits for them, and re-layouts  3.67 us
  transfers between devices with their start and end apart: 6, of which 3 were waited for; matrix products, arithmetic and copies ran while one was open for 1% of the time, Pallas kernels for 25%

profile of v11, /device:TPU:1, one launch (start us, length us, event | category | flops | bytes accessed | tf_op | source)
XLA Modules:
  0.0 171.4 jit_solution(4406125440226483264)
XLA Ops:
  0.6 0.0 copy-start.8
  0.6 0.0 copy-start.7
  0.7 0.0 copy-start.9
  0.7 0.9 constant_dynamic-update-slice_fusion.1
  1.5 0.8 constant_dynamic-update-slice_fusion
  2.4 0.0 copy-start.5
  2.4 0.0 copy-start.6
  2.4 2.5 %collective-permute-start = (bf16[64,1024]{1,0:T(8,128)(2,1)S(1)}, bf16[64,1024]{1,0:T(8,128)(2,1)S(1)}, u32[]{:S(2)}, u32[]{:S(2)}) collective-permute-start(bf16[64,1024]{1,0:T(8,128)(2,1)S(1)} %constant_dynamic-update-slice_fusion), channel_id=1, source_target_pairs={{0,32},{32,0},{64,96},{96,64},{1,33},{33,1},{65,97},{97,65},{2,34}... | collective-permute-start | bytes 393224 | tf_op jit(solution)/shard_map/ppermute | solution.py:594
  4.9 0.9 add_bitcast_fusion.adj_ref
  5.8 24.5 %aggregate.1 = bf16[128,16,128]{2,1,0:T(8,128)(2,1)} custom-call(s32[16,2048]{1,0:T(8,128)S(1)} %add_bitcast_fusion.adj_ref, bf16[32,4096]{1,0:T(8,128)(2,1)} %feat_hbm.1, s32[1,2048]{1,0:T(1,128)} %bitcast.15, s32[1,2048]{1,0:T(1,128)} %bitcast.16), custom_call_target="tpu_custom_call" | custom-call | flops 40000000 | bytes 3000000 | tf_op jit(solution)/shard_map/aggregate/pallas_call | solution.py:229
  30.3 0.0 collective-permute-done
  30.4 10.3 %all-to-all-start = ((bf16[128,16,128]{2,1,0:T(8,128)(2,1)}), bf16[128,16,128]{2,1,0:T(8,128)(2,1)S(1)}, u32[]{:S(2)}, u32[]{:S(2)}) async-start(bf16[128,16,128]{2,1,0:T(8,128)(2,1)} %aggregate.1), calls=%async_computation | async-start | bytes 1048576 | tf_op jit(solution)/shard_map/all_to_all | solution.py:604
  40.7 3.3 %collective-permute-start.1 = (bf16[128,1024]{1,0:T(8,128)(2,1)S(1)}, bf16[128,1024]{1,0:T(8,128)(2,1)S(1)}, u32[]{:S(2)}, u32[]{:S(2)}) collective-permute-start(bf16[128,1024]{1,0:T(8,128)(2,1)S(1)} %pad_maximum_fusion.pair_ref), channel_id=1, source_target_pairs={{0,96},{96,0},{32,64},{64,32},{1,97},{97,1},{33,65},{65,33},{2,98}... | collective-permute-start | bytes 786440 | tf_op jit(solution)/shard_map/ppermute | solution.py:600
  44.0 0.0 copy-done.8
  44.0 0.1 copy.28.count_ref
  44.2 0.0 copy-done.7
  44.2 0.1 copy.25.adj_ref
  44.3 0.0 copy-done.9
  44.3 0.1 copy.26.center_ref
  44.5 8.0 %picks.1 = (bf16[1024,1024]{1,0:T(8,128)(2,1)S(1)}, bf16[1024,1024]{1,0:T(8,128)(2,1)S(1)}) custom-call(s32[512,10]{1,0:T(8,128)S(1)} %copy.25.adj_ref, s32[512,1]{1,0:T(8,128)S(1)} %copy.26.center_ref, s32[512,1]{1,0:T(8,128)S(1)} %copy.28.count_ref), custom_call_target="tpu_custom_call" | custom-call | flops 20000000 | bytes 5000000 | tf_op jit(solution)/shard_map/picks/pallas_call | solution.py:290
  52.5 0.0 copy-start.2
  52.5 1.3 copy-done.2
  53.9 0.0 copy-start.4
  53.9 1.3 copy-done.4
  55.2 0.5 collective-permute-done.1.other_pair_ref
  55.6 0.0 all-to-all-done.arrived_ref
  55.6 0.0 copy-done.5
  55.7 0.0 copy-done.6
  55.7 0.0 copy-start
  55.7 0.0 copy-start.1
  55.7 0.0 copy-start.3
  55.7 14.1 %shard_map.198 = (bf16[512,1024]{1,0:T(8,128)(2,1)}, bf16[64,128,128]{2,1,0:T(8,128)(2,1)S(1)}, bf16[1024,1024]{1,0:T(8,128)(2,1)S(1)}, bf16[1024,1024]{1,0:T(8,...) custom-call(s32[1]{0:T(128)} %bitcast.core_ref, ...), custom_call_target="tpu_custom_call" | custom-call | flops 6000000000 | bytes 18000000 | tf_op jit(solution)/shard_map/pallas_call | solution.py:638
  69.8 1.1 collective-permute-start.2
  70.8 0.0 copy-done
  70.8 0.0 copy-done.1
  70.8 0.0 copy-done.3
  70.8 7.4 %shard_map.199 = (bf16[64,24,128]{2,1,0:T(8,128)(2,1)S(1)}, bf16[64,24,128]{2,1,0:T(8,128)(2,1)S(1)}) custom-call(s32[1]{0:T(128)} %bitcast.core_ref, bf16[512,1024]{1,0:T(8,128)(2,1)S(1)} %get-tuple-element.33.slope_ref, bf16[1024,1024]{1,0:T(8,128)(2,1)S(1)} %copy-done, bf16[1024,1024]{1,0:T(8,128)(2,1)S(1)} %copy-done.1, s32[512,1]{1,0:T(8,128)S(1)} %copy.28.count_ref, ...), custom_call_target="tpu_custom_call" | custom-call | flops 4700000256 | bytes 12000000 | tf_op jit(solution)/shard_map/pallas_call | solution.py:669
  78.3 0.1 collective-permute-start.3
  78.4 1.7 collective-permute-done.3.received_one_ref
  80.1 0.0 collective-permute-done.2.received_ref
  80.1 2.0 %shard_map.200 = bf16[64,152,128]{2,1,0:T(8,128)(2,1)S(1)} custom-call(s32[1]{0:T(128)} %bitcast.core_ref, bf16[1024,1024]{1,0:T(8,128)(2,1)S(1)} %get-tuple-element.32.rows_ref, bf16[512,1024]{1,0:T(8,128)(2,1)S(1)} %get-tuple-element.33.slope_ref, bf16[64,128,128]{2,1,0:T(8,128)(2,1)S(1)} %collective-permute-done.2.received_ref, ...), custom_call_target="tpu_custom_call" | custom-call | flops 1000000000 | bytes 7000000 | tf_op jit(solution)/shard_map/pallas_call | solution.py:678
  82.1 40.7 %all_to_all.15 = bf16[64,152,128]{2,1,0:T(8,128)(2,1)S(1)} all-to-all(bf16[64,152,128]{2,1,0:T(8,128)(2,1)S(1)} %shard_map.200), channel_id=1, replica_groups=mesh['z'=4,'x'=4,'y'=4,'core'=2] {'z','x','y'}, dimensions={0} | all-to-all | bytes 4980736 | tf_op jit(solution)/shard_map/all_to_all | solution.py:604
  122.7 0.4 reduce_sum.12
  123.1 0.3 broadcast_in_dim.43
  123.4 38.0 %all_to_all.16.kept_ref = bf16[64,152,128]{2,1,0:T(8,128)(2,1)S(1)} all-to-all(bf16[64,152,128]{2,1,0:T(8,128)(2,1)S(1)} %broadcast_in_dim.43), channel_id=1, replica_groups=mesh['z'=4,'x'=4,'y'=4,'core'=2] {'z','x','y'}, dimensions={0} | all-to-all | bytes 4980736 | tf_op jit(solution)/shard_map/all_to_all | solution.py:604
  161.4 2.8 %collective-permute-start.4 = (bf16[64,152,128]{2,1,0:T(8,128)(2,1)S(1)}, bf16[64,152,128]{2,1,0:T(8,128)(2,1)S(1)}, u32[]{:S(2)}, u32[]{:S(2)}) collective-permute-start(bf16[64,152,128]{2,1,0:T(8,128)(2,1)S(1)} %all_to_all.16.kept_ref), channel_id=1, source_target_pairs={{0,1},{1,0},{2,3},{3,2},{4,5},{5,4},{6,7},{7,6},{8,9},{9,8},{10,11... | collective-permute-start | bytes 7471112 | tf_op jit(solution)/shard_map/ppermute | solution.py:569
  164.2 2.1 %own_half.1 = (f32[1024,1024]{1,0:T(8,128)}, f32[1024,1024]{1,0:T(8,128)}) custom-call(s32[1]{0:T(128)} %bitcast.core_ref, bf16[64,152,128]{2,1,0:T(8,128)(2,1)S(1)} %all_to_all.16.kept_ref), custom_call_target="tpu_custom_call" | custom-call | flops 1000000 | bytes 7000000 | tf_op jit(solution)/shard_map/own_half/pallas_call | solution.py:570
  166.3 2.2 %collective-permute-done.4.other_ref = bf16[64,152,128]{2,1,0:T(8,128)(2,1)S(1)} collective-permute-done((bf16[64,152,128]{2,1,0:T(8,128)(2,1)S(1)}, bf16[64,152,128]{2,1,0:T(8,128)(2,1)S(1)}, u32[]{:S(2)}, u32[]{:S(2)}) %collective-permute-start.4) | collective-permute-done | bytes 2490400 | tf_op jit(solution)/shard_map/ppermute | solution.py:569
  168.6 2.8 %other_half.1 = (f32[1024,1024]{1,0:T(8,128)}, f32[1024,1024]{1,0:T(8,128)}, f32[32,1024]{1,0:T(8,128)}, f32[32,1024]{1,0:T(8,128)}, f32[1,1024]{1,0:T(1,128)}, /*index=5*/f32[1,1024]{1,0:T(1,128)}) custom-call(s32[1]{0:T(128)} %bitcast.core_ref, s32[1]{0:T(128)} %bitcast.1.z_ref, ...), custom_call_target="tpu_custom_call", output_to_operand_aliasing={{0}: (4, {}), {1}: (5, {})} | custom-call | flops 1000000 | bytes 9000000 | tf_op jit(solution)/shard_map/other_half/pallas_call | solution.py:580
  (2 shorter events, 0.0 us)
Async XLA Ops:
  0.6 43.4 %copy-start.8 = (s32[512]{0:T(512)S(1)}, s32[512]{0:T(512)}, u32[]{:S(2)}) copy-start(s32[512]{0:T(512)} %param.25) | copy-start | bytes 6148
  0.6 43.5 %copy-start.7 = (s32[512,10]{0,1:T(8,128)S(1)}, s32[512,10]{0,1:T(8,128)}, u32[]{:S(2)}) copy-start(s32[512,10]{0,1:T(8,128)} %param.23) | copy-start | bytes 61444
  0.7 43.7 %copy-start.9 = (s32[512]{0:T(512)S(1)}, s32[512]{0:T(512)}, u32[]{:S(2)}) copy-start(s32[512]{0:T(512)} %param.24) | copy-start | bytes 6148
  2.4 53.3 %copy-start.5 = (f32[1024]{0:T(1024)S(1)}, f32[1024]{0:T(1024)}, u32[]{:S(2)}) copy-start(f32[1024]{0:T(1024)} %param.22) | copy-start | bytes 12292
  2.4 53.3 %copy-start.6 = (f32[1024]{0:T(1024)S(1)}, f32[1024]{0:T(1024)}, u32[]{:S(2)}) copy-start(f32[1024]{0:T(1024)} %param.28) | copy-start | bytes 12292
  2.4 27.9 %collective-permute-start = (bf16[64,1024]{1,0:T(8,128)(2,1)S(1)}, bf16[64,1024]{1,0:T(8,128)(2,1)S(1)}, u32[]{:S(2)}, u32[]{:S(2)}) collective-permute-start(bf16[64,1024]{1,0:T(8,128)(2,1)S(1)} %constant_dynamic-update-slice_fusion), channel_id=1, source_target_pairs={{0,32},{32,0},{64,96},{96,64},{1,33},{33,1},{65,97},{97,65},{2,34}... | collective-permute-start | bytes 393224 | tf_op jit(solution)/shard_map/ppermute | solution.py:594
  30.4 25.3 %all-to-all-start = ((bf16[128,16,128]{2,1,0:T(8,128)(2,1)}), bf16[128,16,128]{2,1,0:T(8,128)(2,1)S(1)}, u32[]{:S(2)}, u32[]{:S(2)}) async-start(bf16[128,16,128]{2,1,0:T(8,128)(2,1)} %aggregate.1), calls=%async_computation | async-start | bytes 1048576 | tf_op jit(solution)/shard_map/all_to_all | solution.py:604
  40.7 14.9 %collective-permute-start.1 = (bf16[128,1024]{1,0:T(8,128)(2,1)S(1)}, bf16[128,1024]{1,0:T(8,128)(2,1)S(1)}, u32[]{:S(2)}, u32[]{:S(2)}) collective-permute-start(bf16[128,1024]{1,0:T(8,128)(2,1)S(1)} %pad_maximum_fusion.pair_ref), channel_id=1, source_target_pairs={{0,96},{96,0},{32,64},{64,32},{1,97},{97,1},{33,65},{65,33},{2,98}... | collective-permute-start | bytes 786440 | tf_op jit(solution)/shard_map/ppermute | solution.py:600
  52.5 1.3 copy-start.2
  53.9 1.3 copy-start.4
  55.7 15.2 %copy-start = (bf16[1024,1024]{1,0:T(8,128)(2,1)S(1)}, bf16[1024,1024]{1,0:T(8,128)(2,1)}, u32[]{:S(2)}) copy-start(bf16[1024,1024]{1,0:T(8,128)(2,1)} %root_ref.1) | copy-start | bytes 6291460
  55.7 15.2 %copy-start.1 = (bf16[1024,1024]{1,0:T(8,128)(2,1)S(1)}, bf16[1024,1024]{1,0:T(8,128)(2,1)}, u32[]{:S(2)}) copy-start(bf16[1024,1024]{1,0:T(8,128)(2,1)} %near_ref.1) | copy-start | bytes 6291460
  55.7 15.2 %copy-start.3 = (bf16[1024,1024]{1,0:T(8,128)(2,1)S(1)}, bf16[1024,1024]{1,0:T(8,128)(2,1)}, u32[]{:S(2)}) copy-start(bf16[1024,1024]{1,0:T(8,128)(2,1)} %copy-done.2) | copy-start | bytes 6291460
  69.8 10.3 %collective-permute-start.2 = (bf16[64,128,128]{2,1,0:T(8,128)(2,1)S(1)}, bf16[64,128,128]{2,1,0:T(8,128)(2,1)S(1)}, u32[]{:S(2)}, u32[]{:S(2)}) collective-permute-start(bf16[64,128,128]{2,1,0:T(8,128)(2,1)S(1)} %get-tuple-element.34), channel_id=1, source_target_pairs={{0,1},{1,0},{2,3},{3,2},{4,5},{5,4},{6,7},{7,6},{8,9},{9,8},{10,11... | collective-permute-start | bytes 6291464 | tf_op jit(solution)/shard_map/ppermute | solution.py:668
  78.3 1.8 %collective-permute-start.3 = (bf16[64,24,128]{2,1,0:T(8,128)(2,1)S(1)}, bf16[64,24,128]{2,1,0:T(8,128)(2,1)S(1)}, u32[]{:S(2)}, u32[]{:S(2)}) collective-permute-start(bf16[64,24,128]{2,1,0:T(8,128)(2,1)S(1)} %get-tuple-element.40), channel_id=1, source_target_pairs={{0,1},{1,0},{2,3},{3,2},{4,5},{5,4},{6,7},{7,6},{8,9},{9,8},{10,11... | collective-permute-start | bytes 1179656 | tf_op jit(solution)/shard_map/ppermute | solution.py:677
  161.4 7.2 %collective-permute-start.4 = (bf16[64,152,128]{2,1,0:T(8,128)(2,1)S(1)}, bf16[64,152,128]{2,1,0:T(8,128)(2,1)S(1)}, u32[]{:S(2)}, u32[]{:S(2)}) collective-permute-start(bf16[64,152,128]{2,1,0:T(8,128)(2,1)S(1)} %all_to_all.16.kept_ref), channel_id=1, source_target_pairs={{0,1},{1,0},{2,3},{3,2},{4,5},{5,4},{6,7},{7,6},{8,9},{9,8},{10,11... | collective-permute-start | bytes 7471112 | tf_op jit(solution)/shard_map/ppermute | solution.py:569

commit v12 on v9

--- a/solution.py
+++ b/solution.py
@@ -479,8 +479,7 @@
                     ]
         return carry
 
-    for t in range(hidden_width // tile):
-        first_grads(t, 0)
+    lax.fori_loop(0, hidden_width // tile, first_grads, 0)
     for place, to_ref in enumerate((kept_ref, sent_ref)):
         which = core ^ place
         to_ref[:, 16:, :] = jnp.zeros((to_ref.shape[0], 8, LANES), jnp.bfloat16)

time: 172 us -> 171 us (level)
  no operation moved by 1% of the time
where the time goes in v12:
time: 171 us
  blocking collectives  78.7 us (46%)
  Pallas kernels  60.2 us (35%)
  starting transfers between devices  20.3 us (12%)
  local copies, waits for them, and re-layouts  5.12 us (3%)
  waiting for transfers between devices  4.4 us (3%)
    all_to_all x2, blocking collectives, exchange(): return lax.all_to_all(value, axes, split_axis=0, concat_axis=0, tiled=True)  78.7 us
    pallas_call x1, Pallas kernels, aggregate(): pl.pallas_call(aggregate_kernel, out_shape=jax.ShapeDtypeStruct((owners,...  24.5 us
    pallas_call x1, Pallas kernels, step(): call(forward_kernel, (shaped(nodes, hidden_width), shaped(64, LANES, LANE...  13.3 us
    all_to_all x1, starting transfers between devices, exchange(): return lax.all_to_all(value, axes, split_axis=0, concat_axis=0, tiled=True)  10.3 us
    pallas_call x1, Pallas kernels, picks(): pl.pallas_call(picks_kernel, out_shape=(jax.ShapeDtypeStruct((2 * nodes,...  8.03 us
    pallas_call x1, Pallas kernels, step(): call(backward_kernel, (shaped(64, 24, LANES), shaped(64, 24, LANES)), 9,...  7.45 us
    unnamed x22, local copies, waits for them, and re-layouts  3.67 us
  transfers between devices with their start and end apart: 6, of which 3 were waited for; matrix products, arithmetic and copies ran while one was open for 1% of the time, Pallas kernels for 25%

profile of v12, /device:TPU:1, one launch (start us, length us, event | category | flops | bytes accessed | tf_op | source)
XLA Modules:
  0.0 171.0 jit_solution(15835529691420060437)
XLA Ops:
  0.6 0.0 copy-start.8
  0.6 0.0 copy-start.7
  0.7 0.0 copy-start.9
  0.7 0.9 constant_dynamic-update-slice_fusion.1
  1.5 0.8 constant_dynamic-update-slice_fusion
  2.4 0.0 copy-start.5
  2.4 0.0 copy-start.6
  2.4 2.5 %collective-permute-start = (bf16[64,1024]{1,0:T(8,128)(2,1)S(1)}, bf16[64,1024]{1,0:T(8,128)(2,1)S(1)}, u32[]{:S(2)}, u32[]{:S(2)}) collective-permute-start(bf16[64,1024]{1,0:T(8,128)(2,1)S(1)} %constant_dynamic-update-slice_fusion), channel_id=1, source_target_pairs={{0,32},{32,0},{64,96},{96,64},{1,33},{33,1},{65,97},{97,65},{2,34}... | collective-permute-start | bytes 393224 | tf_op jit(solution)/shard_map/ppermute | solution.py:597
  4.9 0.9 add_bitcast_fusion.adj_ref
  5.8 24.5 %aggregate.1 = bf16[128,16,128]{2,1,0:T(8,128)(2,1)} custom-call(s32[16,2048]{1,0:T(8,128)S(1)} %add_bitcast_fusion.adj_ref, bf16[32,4096]{1,0:T(8,128)(2,1)} %feat_hbm.1, s32[1,2048]{1,0:T(1,128)} %bitcast.15, s32[1,2048]{1,0:T(1,128)} %bitcast.16), custom_call_target="tpu_custom_call" | custom-call | flops 40000000 | bytes 3000000 | tf_op jit(solution)/shard_map/aggregate/pallas_call | solution.py:229
  30.3 0.0 collective-permute-done
  30.4 10.3 %all-to-all-start = ((bf16[128,16,128]{2,1,0:T(8,128)(2,1)}), bf16[128,16,128]{2,1,0:T(8,128)(2,1)S(1)}, u32[]{:S(2)}, u32[]{:S(2)}) async-start(bf16[128,16,128]{2,1,0:T(8,128)(2,1)} %aggregate.1), calls=%async_computation | async-start | bytes 1048576 | tf_op jit(solution)/shard_map/all_to_all | solution.py:607
  40.7 3.3 %collective-permute-start.1 = (bf16[128,1024]{1,0:T(8,128)(2,1)S(1)}, bf16[128,1024]{1,0:T(8,128)(2,1)S(1)}, u32[]{:S(2)}, u32[]{:S(2)}) collective-permute-start(bf16[128,1024]{1,0:T(8,128)(2,1)S(1)} %pad_maximum_fusion.pair_ref), channel_id=1, source_target_pairs={{0,96},{96,0},{32,64},{64,32},{1,97},{97,1},{33,65},{65,33},{2,98}... | collective-permute-start | bytes 786440 | tf_op jit(solution)/shard_map/ppermute | solution.py:603
  44.0 0.0 copy-done.8
  44.0 0.1 copy.28.count_ref
  44.2 0.0 copy-done.7
  44.2 0.1 copy.25.adj_ref
  44.3 0.0 copy-done.9
  44.3 0.1 copy.26.center_ref
  44.5 8.0 %picks.1 = (bf16[1024,1024]{1,0:T(8,128)(2,1)S(1)}, bf16[1024,1024]{1,0:T(8,128)(2,1)S(1)}) custom-call(s32[512,10]{1,0:T(8,128)S(1)} %copy.25.adj_ref, s32[512,1]{1,0:T(8,128)S(1)} %copy.26.center_ref, s32[512,1]{1,0:T(8,128)S(1)} %copy.28.count_ref), custom_call_target="tpu_custom_call" | custom-call | flops 20000000 | bytes 5000000 | tf_op jit(solution)/shard_map/picks/pallas_call | solution.py:290
  52.5 0.0 copy-start.2
  52.5 1.3 copy-done.2
  53.9 0.0 copy-start.4
  53.9 1.3 copy-done.4
  55.2 0.5 collective-permute-done.1.other_pair_ref
  55.6 0.0 all-to-all-done.arrived_ref
  55.7 0.0 copy-done.5
  55.7 0.0 copy-done.6
  55.7 0.0 copy-start
  55.7 0.0 copy-start.1
  55.7 0.0 copy-start.3
  55.7 13.3 %shard_map.198 = (bf16[512,1024]{1,0:T(8,128)(2,1)}, bf16[64,128,128]{2,1,0:T(8,128)(2,1)S(1)}, bf16[1024,1024]{1,0:T(8,128)(2,1)S(1)}, bf16[1024,1024]{1,0:T(8,...) custom-call(s32[1]{0:T(128)} %bitcast.core_ref, ...), custom_call_target="tpu_custom_call" | custom-call | flops 6000000000 | bytes 18000000 | tf_op jit(solution)/shard_map/pallas_call | solution.py:641
  69.0 1.3 collective-permute-start.2
  70.3 0.0 copy-done
  70.3 0.0 copy-done.1
  70.3 0.0 copy-done.3
  70.3 7.5 %shard_map.199 = (bf16[64,24,128]{2,1,0:T(8,128)(2,1)S(1)}, bf16[64,24,128]{2,1,0:T(8,128)(2,1)S(1)}) custom-call(s32[1]{0:T(128)} %bitcast.core_ref, bf16[512,1024]{1,0:T(8,128)(2,1)S(1)} %get-tuple-element.33.slope_ref, bf16[1024,1024]{1,0:T(8,128)(2,1)S(1)} %copy-done, bf16[1024,1024]{1,0:T(8,128)(2,1)S(1)} %copy-done.1, s32[512,1]{1,0:T(8,128)S(1)} %copy.28.count_ref, ...), custom_call_target="tpu_custom_call" | custom-call | flops 4700000256 | bytes 12000000 | tf_op jit(solution)/shard_map/pallas_call | solution.py:672
  77.8 0.1 collective-permute-start.3
  77.9 1.7 collective-permute-done.3.received_one_ref
  79.6 0.0 collective-permute-done.2.received_ref
  79.6 2.0 %shard_map.200 = bf16[64,152,128]{2,1,0:T(8,128)(2,1)S(1)} custom-call(s32[1]{0:T(128)} %bitcast.core_ref, bf16[1024,1024]{1,0:T(8,128)(2,1)S(1)} %get-tuple-element.32.rows_ref, bf16[512,1024]{1,0:T(8,128)(2,1)S(1)} %get-tuple-element.33.slope_ref, bf16[64,128,128]{2,1,0:T(8,128)(2,1)S(1)} %collective-permute-done.2.received_ref, ...), custom_call_target="tpu_custom_call" | custom-call | flops 1000000000 | bytes 7000000 | tf_op jit(solution)/shard_map/pallas_call | solution.py:681
  81.6 40.7 %all_to_all.15 = bf16[64,152,128]{2,1,0:T(8,128)(2,1)S(1)} all-to-all(bf16[64,152,128]{2,1,0:T(8,128)(2,1)S(1)} %shard_map.200), channel_id=1, replica_groups=mesh['z'=4,'x'=4,'y'=4,'core'=2] {'z','x','y'}, dimensions={0} | all-to-all | bytes 4980736 | tf_op jit(solution)/shard_map/all_to_all | solution.py:607
  122.2 0.4 reduce_sum.12
  122.6 0.3 broadcast_in_dim.43
  122.9 38.0 %all_to_all.16.kept_ref = bf16[64,152,128]{2,1,0:T(8,128)(2,1)S(1)} all-to-all(bf16[64,152,128]{2,1,0:T(8,128)(2,1)S(1)} %broadcast_in_dim.43), channel_id=1, replica_groups=mesh['z'=4,'x'=4,'y'=4,'core'=2] {'z','x','y'}, dimensions={0} | all-to-all | bytes 4980736 | tf_op jit(solution)/shard_map/all_to_all | solution.py:607
  160.9 2.8 %collective-permute-start.4 = (bf16[64,152,128]{2,1,0:T(8,128)(2,1)S(1)}, bf16[64,152,128]{2,1,0:T(8,128)(2,1)S(1)}, u32[]{:S(2)}, u32[]{:S(2)}) collective-permute-start(bf16[64,152,128]{2,1,0:T(8,128)(2,1)S(1)} %all_to_all.16.kept_ref), channel_id=1, source_target_pairs={{0,1},{1,0},{2,3},{3,2},{4,5},{5,4},{6,7},{7,6},{8,9},{9,8},{10,11... | collective-permute-start | bytes 7471112 | tf_op jit(solution)/shard_map/ppermute | solution.py:572
  163.7 2.1 %own_half.1 = (f32[1024,1024]{1,0:T(8,128)}, f32[1024,1024]{1,0:T(8,128)}) custom-call(s32[1]{0:T(128)} %bitcast.core_ref, bf16[64,152,128]{2,1,0:T(8,128)(2,1)S(1)} %all_to_all.16.kept_ref), custom_call_target="tpu_custom_call" | custom-call | flops 1000000 | bytes 7000000 | tf_op jit(solution)/shard_map/own_half/pallas_call | solution.py:573
  165.8 2.2 %collective-permute-done.4.other_ref = bf16[64,152,128]{2,1,0:T(8,128)(2,1)S(1)} collective-permute-done((bf16[64,152,128]{2,1,0:T(8,128)(2,1)S(1)}, bf16[64,152,128]{2,1,0:T(8,128)(2,1)S(1)}, u32[]{:S(2)}, u32[]{:S(2)}) %collective-permute-start.4) | collective-permute-done | bytes 2490400 | tf_op jit(solution)/shard_map/ppermute | solution.py:572
  168.1 2.8 %other_half.1 = (f32[1024,1024]{1,0:T(8,128)}, f32[1024,1024]{1,0:T(8,128)}, f32[32,1024]{1,0:T(8,128)}, f32[32,1024]{1,0:T(8,128)}, f32[1,1024]{1,0:T(1,128)}, /*index=5*/f32[1,1024]{1,0:T(1,128)}) custom-call(s32[1]{0:T(128)} %bitcast.core_ref, s32[1]{0:T(128)} %bitcast.1.z_ref, ...), custom_call_target="tpu_custom_call", output_to_operand_aliasing={{0}: (4, {}), {1}: (5, {})} | custom-call | flops 1000000 | bytes 9000000 | tf_op jit(solution)/shard_map/other_half/pallas_call | solution.py:583
  (2 shorter events, 0.0 us)
Async XLA Ops:
  0.6 43.4 %copy-start.8 = (s32[512]{0:T(512)S(1)}, s32[512]{0:T(512)}, u32[]{:S(2)}) copy-start(s32[512]{0:T(512)} %param.25) | copy-start | bytes 6148
  0.6 43.5 %copy-start.7 = (s32[512,10]{0,1:T(8,128)S(1)}, s32[512,10]{0,1:T(8,128)}, u32[]{:S(2)}) copy-start(s32[512,10]{0,1:T(8,128)} %param.23) | copy-start | bytes 61444
  0.7 43.7 %copy-start.9 = (s32[512]{0:T(512)S(1)}, s32[512]{0:T(512)}, u32[]{:S(2)}) copy-start(s32[512]{0:T(512)} %param.24) | copy-start | bytes 6148
  2.4 53.3 %copy-start.5 = (f32[1024]{0:T(1024)S(1)}, f32[1024]{0:T(1024)}, u32[]{:S(2)}) copy-start(f32[1024]{0:T(1024)} %param.22) | copy-start | bytes 12292
  2.4 53.3 %copy-start.6 = (f32[1024]{0:T(1024)S(1)}, f32[1024]{0:T(1024)}, u32[]{:S(2)}) copy-start(f32[1024]{0:T(1024)} %param.28) | copy-start | bytes 12292
  2.4 27.9 %collective-permute-start = (bf16[64,1024]{1,0:T(8,128)(2,1)S(1)}, bf16[64,1024]{1,0:T(8,128)(2,1)S(1)}, u32[]{:S(2)}, u32[]{:S(2)}) collective-permute-start(bf16[64,1024]{1,0:T(8,128)(2,1)S(1)} %constant_dynamic-update-slice_fusion), channel_id=1, source_target_pairs={{0,32},{32,0},{64,96},{96,64},{1,33},{33,1},{65,97},{97,65},{2,34}... | collective-permute-start | bytes 393224 | tf_op jit(solution)/shard_map/ppermute | solution.py:597
  30.4 25.3 %all-to-all-start = ((bf16[128,16,128]{2,1,0:T(8,128)(2,1)}), bf16[128,16,128]{2,1,0:T(8,128)(2,1)S(1)}, u32[]{:S(2)}, u32[]{:S(2)}) async-start(bf16[128,16,128]{2,1,0:T(8,128)(2,1)} %aggregate.1), calls=%async_computation | async-start | bytes 1048576 | tf_op jit(solution)/shard_map/all_to_all | solution.py:607
  40.7 14.9 %collective-permute-start.1 = (bf16[128,1024]{1,0:T(8,128)(2,1)S(1)}, bf16[128,1024]{1,0:T(8,128)(2,1)S(1)}, u32[]{:S(2)}, u32[]{:S(2)}) collective-permute-start(bf16[128,1024]{1,0:T(8,128)(2,1)S(1)} %pad_maximum_fusion.pair_ref), channel_id=1, source_target_pairs={{0,96},{96,0},{32,64},{64,32},{1,97},{97,1},{33,65},{65,33},{2,98}... | collective-permute-start | bytes 786440 | tf_op jit(solution)/shard_map/ppermute | solution.py:603
  52.5 1.3 copy-start.2
  53.9 1.3 copy-start.4
  55.7 14.7 %copy-start = (bf16[1024,1024]{1,0:T(8,128)(2,1)S(1)}, bf16[1024,1024]{1,0:T(8,128)(2,1)}, u32[]{:S(2)}) copy-start(bf16[1024,1024]{1,0:T(8,128)(2,1)} %root_ref.1) | copy-start | bytes 6291460
  55.7 14.6 %copy-start.1 = (bf16[1024,1024]{1,0:T(8,128)(2,1)S(1)}, bf16[1024,1024]{1,0:T(8,128)(2,1)}, u32[]{:S(2)}) copy-start(bf16[1024,1024]{1,0:T(8,128)(2,1)} %near_ref.1) | copy-start | bytes 6291460
  55.7 14.6 %copy-start.3 = (bf16[1024,1024]{1,0:T(8,128)(2,1)S(1)}, bf16[1024,1024]{1,0:T(8,128)(2,1)}, u32[]{:S(2)}) copy-start(bf16[1024,1024]{1,0:T(8,128)(2,1)} %copy-done.2) | copy-start | bytes 6291460
  69.0 10.5 %collective-permute-start.2 = (bf16[64,128,128]{2,1,0:T(8,128)(2,1)S(1)}, bf16[64,128,128]{2,1,0:T(8,128)(2,1)S(1)}, u32[]{:S(2)}, u32[]{:S(2)}) collective-permute-start(bf16[64,128,128]{2,1,0:T(8,128)(2,1)S(1)} %get-tuple-element.34), channel_id=1, source_target_pairs={{0,1},{1,0},{2,3},{3,2},{4,5},{5,4},{6,7},{7,6},{8,9},{9,8},{10,11... | collective-permute-start | bytes 6291464 | tf_op jit(solution)/shard_map/ppermute | solution.py:671
  77.8 1.8 %collective-permute-start.3 = (bf16[64,24,128]{2,1,0:T(8,128)(2,1)S(1)}, bf16[64,24,128]{2,1,0:T(8,128)(2,1)S(1)}, u32[]{:S(2)}, u32[]{:S(2)}) collective-permute-start(bf16[64,24,128]{2,1,0:T(8,128)(2,1)S(1)} %get-tuple-element.40), channel_id=1, source_target_pairs={{0,1},{1,0},{2,3},{3,2},{4,5},{5,4},{6,7},{7,6},{8,9},{9,8},{10,11... | collective-permute-start | bytes 1179656 | tf_op jit(solution)/shard_map/ppermute | solution.py:680
  160.9 7.2 %collective-permute-start.4 = (bf16[64,152,128]{2,1,0:T(8,128)(2,1)S(1)}, bf16[64,152,128]{2,1,0:T(8,128)(2,1)S(1)}, u32[]{:S(2)}, u32[]{:S(2)}) collective-permute-start(bf16[64,152,128]{2,1,0:T(8,128)(2,1)S(1)} %all_to_all.16.kept_ref), channel_id=1, source_target_pairs={{0,1},{1,0},{2,3},{3,2},{4,5},{5,4},{6,7},{7,6},{8,9},{9,8},{10,11... | collective-permute-start | bytes 7471112 | tf_op jit(solution)/shard_map/ppermute | solution.py:572
